TPU v7x, 512 devices: a whole 4x8x8 slice. The times are simulated.
512 devices in a mesh: shot: 128 (over y, z, x_hi), freq: 4 (over x_lo, core).
Axes of the slice: x: 4 (x_hi: 2, x_lo: 2; x = x_hi * 2 + x_lo), y: 8, z: 8, core: 2. Of those that a mesh axis runs over, the one named last changes fastest.
Arguments:
- blended: bfloat16 [2, 512, 512, 256], P(None, 'shot', 'freq'), may hold values from -6 to 6
- estimate: bfloat16 [2, 512, 512, 256], P(None, 'shot', 'freq'), may hold values from -5 to 5
- partner: int32 [512], P('shot'), may hold values from 0 to 511, as said below
- delays: int32 [512], replicated, may hold values from 0 to 256
- levels: int32 [128], replicated, may hold values from 1 to 4
Outputs:
- deblended: bfloat16 [2, 512, 512, 256], P(None, 'shot', 'freq')
Inputs may be any that keep to these rules, and one draw needn't show every extreme that they name: Shot s of block b = s // 4 is paired with a shot of block (b + 64) modulo 512 / 4; the pairing is mutual, partner[partner[s]] = s.
All inputs are finite; a program needn't handle non-finite values.
Results may differ from a plain program's by a relative error of at most 0.005.
Values may be sent and summed in bfloat16 or wider, within the bound.
No kernel may reach another device: no remote copies, remote signals or barrier semaphores. Data moves between devices by JAX's collectives and lax.ppermute only.
A program may use at most 64 MiB of HBM per device.

v0:
```python
import functools
import math

import jax
import jax.numpy as jnp
import numpy as np
from jax import lax
from jax.experimental import pallas as pl
from jax.experimental.pallas import tpu as pltpu
from jax.sharding import Mesh
from jax.sharding import PartitionSpec as P

NT = 1024
PASSES = 2
SHOTS_DEV = 4
ROLES = 4
RELAX = 0.5
LEVEL_SCALE = 0.25
TINY = 1e-37
ROOT8 = 1.0 / math.sqrt(8.0)
HALF_ROOT = math.sqrt(0.5)
TAPER = [math.sin(math.pi * (t + 0.5) / 8) ** 2 * ROOT8 for t in range(8)]
GROUP = ("yh", "h")
SUM_GROUP = ("yh", "h", "f")

f32 = jnp.float32
bf16 = jnp.bfloat16
VMEM = pl.BlockSpec(memory_space=pltpu.VMEM)
SMEM = pl.BlockSpec(memory_space=pltpu.SMEM)


def receiver_tables(length, sign):
    k = np.arange(length)
    angle = 2.0 * np.pi / length * ((k[:, None] * k[None, :]) % length)
    c, s = np.cos(angle) / math.sqrt(length), sign * np.sin(angle) / math.sqrt(length)
    full = np.block([[c, -s], [s, c]]).astype(np.float32)
    high = full.astype(jnp.bfloat16)
    low = (full - high.astype(np.float32)).astype(jnp.bfloat16)
    return np.stack([high, low])


def add(a, b):
    return (a[0] + b[0], a[1] + b[1])


def sub(a, b):
    return (a[0] - b[0], a[1] - b[1])


def turn(a, sign):
    return (a[1], -a[0]) if sign > 0 else (-a[1], a[0])


def twist(a, power, sign):
    if power == 0:
        return a
    if power == 2:
        return turn(a, sign)
    re, im = a
    if sign > 0:
        one = ((re + im) * HALF_ROOT, (im - re) * HALF_ROOT)
    else:
        one = ((re - im) * HALF_ROOT, (im + re) * HALF_ROOT)
    return one if power == 1 else turn(one, sign)


def dft4(a, b, c, d, sign):
    s0, s1, s2, s3 = add(a, c), sub(a, c), add(b, d), turn(sub(b, d), sign)
    return [add(s0, s2), add(s1, s3), sub(s0, s2), sub(s1, s3)]


def dft8(x, sign, part="both"):
    even = dft4(x[0], x[2], x[4], x[6], sign)
    odd = dft4(x[1], x[3], x[5], x[7], sign)
    odd = [twist(odd[k], k, sign) for k in range(4)]
    first = [add(even[k], odd[k]) for k in range(4)] if part != "second" else []
    second = [sub(even[k], odd[k]) for k in range(4)] if part != "first" else []
    return first + second


def windowed(first, second):
    both = first + second
    return [(both[t][0] * TAPER[t], both[t][1] * TAPER[t]) for t in range(8)]


def load(ref, ab, block, rows, half, q):
    lo, hi = half * 128, q + half * 128
    out = []
    for t in range(SHOTS_DEV):
        at = (ab, block, t) if block is not None else (ab, t)
        out.append((ref[(*at, rows, slice(lo, lo + 128))], ref[(*at, rows, slice(hi, hi + 128))]))
    return out


def place(n):
    g = lax.axis_index("g")
    first, last = g == 0, g == n - 1
    return g, first, last


def fetch_halo(n, up_ref, down_ref, halo_ref):
    _, first, last = place(n)
    for ab in range(2):
        source = jnp.where(first, 0, ab)
        halo_ref[0, ab] = up_ref[source].astype(f32)
        source = jnp.where(last, 1, ab)
        scale = jnp.where(last, 0.0, 1.0) if ab == 1 else 1.0
        halo_ref[1, ab] = down_ref[source].astype(f32) * scale


def spectra(z_ref, halo_ref, ab, rows, half, q):
    prev = load(halo_ref, 0, ab, rows, half, q)
    even = load(z_ref, ab, 0, rows, half, q)
    odd = load(z_ref, ab, 1, rows, half, q)
    after = load(halo_ref, 1, ab, rows, half, q)
    for pair in ((prev, even), (even, odd), (odd, after)):
        yield dft8(windowed(*pair), 1)


def pack_kernel(nf, e_ref, b_ref, partner_ref, delays_ref, out_ref):
    q = e_ref.shape[3]
    fl = e_ref.shape[2] // ROLES
    block = (lax.axis_index("yh") * lax.axis_size("g") + lax.axis_index("g")) * 2 + lax.axis_index("h")
    row = lax.broadcasted_iota(jnp.int32, (16, 2 * q), 0)
    meta = jnp.zeros((16, 2 * q), f32)
    for t in range(SHOTS_DEV):
        other = partner_ref[t]
        offset = (delays_ref[other] - delays_ref[block * SHOTS_DEV + t]) & (NT - 1)
        for i, value in enumerate((other & (SHOTS_DEV - 1), offset >> 5, offset & 31)):
            meta = jnp.where(row == 3 * t + i, value.astype(f32), meta)
    for role in range(ROLES):
        rows = slice(role * fl, (role + 1) * fl)
        for k, ref in enumerate((e_ref, b_ref)):
            for t in range(SHOTS_DEV):
                out_ref[role, k * SHOTS_DEV + t, :, :q] = ref[0, t, rows, :]
                out_ref[role, k * SHOTS_DEV + t, :, q:] = ref[1, t, rows, :]
        out_ref[role, 2 * SHOTS_DEV, :16, :] = meta.astype(bf16)
        out_ref[role, 2 * SHOTS_DEV, 16:, :] = jnp.zeros((fl - 16, 2 * q), bf16)


def phases(index):
    quadrant = (index + 128) >> 8
    x = (index - (quadrant << 8)).astype(f32) * (2.0 * math.pi / NT)
    x2 = x * x
    s = x * (1 + x2 * (-1 / 6 + x2 * (1 / 120 + x2 * (-1 / 5040 + x2 * (1 / 362880)))))
    c = 1 + x2 * (-1 / 2 + x2 * (1 / 24 + x2 * (-1 / 720 + x2 * (1 / 40320))))
    swap = (quadrant & 1) == 1
    cos, sin = jnp.where(swap, s, c), jnp.where(swap, c, s)
    cos = jnp.where(((quadrant + 1) & 2) == 2, -cos, cos)
    sin = jnp.where((quadrant & 2) == 2, -sin, sin)
    return cos, sin


def relax(e_ref, bh_ref, meta_ref, phase_ref, z_ref, down_ref, up_ref):
    fl, q = e_ref.shape[3], e_ref.shape[4] // 2

    def body(i, carry):
        rows = pl.ds(pl.multiple_of(i * 16, 16), 16)
        for ab in range(2):
            for p in range(2):
                for t in range(SHOTS_DEV):
                    slot = jnp.broadcast_to(meta_ref[2 * ab + p, 3 * t : 3 * t + 1, :128], (16, 128))
                    cos = phase_ref[ab, p, t, 0, rows, :] * RELAX
                    sin = phase_ref[ab, p, t, 1, rows, :] * RELAX
                    for half in range(q // 128):
                        spans = (slice(half * 128, half * 128 + 128), slice(q + half * 128, q + half * 128 + 128))
                        other = [e_ref[1 - ab, p, 0, rows, span] for span in spans]
                        for k in range(1, SHOTS_DEV):
                            other = [
                                jnp.where(slot == k, e_ref[1 - ab, p, k, rows, span], o)
                                for o, span in zip(other, spans)
                            ]
                        shifted = (other[0] * cos + other[1] * sin, other[1] * cos - other[0] * sin)
                        for span, shift in zip(spans, shifted):
                            mine = e_ref[ab, p, t, rows, span]
                            z = mine + RELAX * (bh_ref[ab, p, t, rows, span] - mine) - shift
                            z_ref[ab, p, t, rows, span] = z
                            side = down_ref if p == 0 else up_ref
                            side[ab, t, rows, span] = z.astype(bf16)
        return carry

    lax.fori_loop(0, fl // 16, body, 0)


def first_kernel(in_ref, table_ref, z_ref, bh_ref, meta_ref, phase_ref, down_ref, up_ref, e_ref):
    fl, q2 = in_ref.shape[2], in_ref.shape[3]
    high, low = table_ref[0], table_ref[1]
    for src in range(ROLES):
        ab, p = src // 2, src % 2
        data = in_ref[src, : 2 * SHOTS_DEV].reshape(2 * SHOTS_DEV * fl, q2)
        out = jnp.dot(data, high, preferred_element_type=f32) + jnp.dot(data, low, preferred_element_type=f32)
        out = out.reshape(2, SHOTS_DEV, fl, q2)
        e_ref[ab, p] = out[0]
        bh_ref[ab, p] = out[1]
        meta = in_ref[src, 2 * SHOTS_DEV, :16, :128].astype(f32)
        meta_ref[src] = meta
        whole = meta.astype(jnp.int32)
        freq = lax.axis_index("f") * (ROLES * fl) + (lax.axis_index("yh") * 2 + lax.axis_index("h")) * fl
        freq = freq + lax.broadcasted_iota(jnp.int32, (fl, 128), 0)
        for t in range(SHOTS_DEV):
            offset = whole[3 * t + 1 : 3 * t + 2, :] * 32 + whole[3 * t + 2 : 3 * t + 3, :]
            cos, sin = phases((freq * offset) & (NT - 1))
            phase_ref[ab, p, t, 0] = cos
            phase_ref[ab, p, t, 1] = sin
    relax(e_ref, bh_ref, meta_ref, phase_ref, z_ref, down_ref, up_ref)


def sums_kernel(n, z_ref, up_ref, down_ref, out_ref, halo_ref):
    fl, q = z_ref.shape[3], z_ref.shape[4] // 2
    fetch_halo(n, up_ref, down_ref, halo_ref)

    def body(i, totals):
        rows = pl.ds(pl.multiple_of(i * 8, 8), 8)
        totals = list(totals)
        for ab in range(2):
            for half in range(q // 128):
                for w, x in enumerate(spectra(z_ref, halo_ref, ab, rows, half, q)):
                    for re, im in x:
                        square = re * re + im * im
                        totals[ab * 3 + w] += square * lax.rsqrt(jnp.maximum(square, TINY))
        return tuple(totals)

    totals = lax.fori_loop(0, fl // 8, body, (jnp.zeros((8, 128), f32),) * 6)
    row = lax.broadcasted_iota(jnp.int32, (8, 128), 0)
    tile = jnp.zeros((8, 128), f32)
    for k, total in enumerate(totals):
        tile = jnp.where(row == k, jnp.sum(total, axis=0, keepdims=True), tile)
    for k in range(out_ref.shape[0]):
        out_ref[k] = tile


def shrink_windows(n, count, z_ref, up_ref, down_ref, parts_ref, levels_ref, e_ref, halo_ref):
    fl, q = z_ref.shape[3], z_ref.shape[4] // 2
    fetch_halo(n, up_ref, down_ref, halo_ref)
    g, first, _ = place(n)
    tile = parts_ref[0]
    for k in range(1, parts_ref.shape[0]):
        tile = tile + parts_ref[k]
    total = jnp.sum(tile, axis=1, keepdims=True)
    lams = []
    for ab in range(2):
        for w in range(3):
            window = jnp.maximum((ab * n + g) * 2 + w - 1, 0)
            scale = LEVEL_SCALE / count * levels_ref[window].astype(f32)
            lams.append(jnp.broadcast_to(total[3 * ab + w : 3 * ab + w + 1, :] * scale, (8, 128)))
    here = jnp.where(first, 0.0, ROOT8)

    def body(i, carry):
        rows = pl.ds(pl.multiple_of(i * 8, 8), 8)
        for ab in range(2):
            for half in range(q // 128):
                parts = []
                for w, x in enumerate(spectra(z_ref, halo_ref, ab, rows, half, q)):
                    lam = lams[3 * ab + w]
                    root = here if (ab == 0 and w == 0) else ROOT8
                    kept = []
                    for re, im in x:
                        inverse = lax.rsqrt(jnp.maximum(re * re + im * im, TINY))
                        factor = jnp.maximum(root - lam * inverse * root, 0.0)
                        kept.append((re * factor, im * factor))
                    parts.append(dft8(kept, -1, ("second", "both", "first")[w]))
                for p, (a, b) in enumerate(((parts[0], parts[1][:4]), (parts[1][4:], parts[2]))):
                    for t in range(SHOTS_DEV):
                        re, im = add(a[t], b[t])
                        e_ref[ab, p, t, rows, slice(half * 128, half * 128 + 128)] = re
                        e_ref[ab, p, t, rows, slice(q + half * 128, q + half * 128 + 128)] = im
        return carry

    lax.fori_loop(0, fl // 8, body, 0)


def middle_kernel(n, count, z_ref, up_ref, down_ref, parts_ref, levels_ref, bh_ref, meta_ref, phase_ref,
                  z_out, down_out, up_out, e_ref, halo_ref):
    shrink_windows(n, count, z_ref, up_ref, down_ref, parts_ref, levels_ref, e_ref, halo_ref)
    relax(e_ref, bh_ref, meta_ref, phase_ref, z_out, down_out, up_out)


def last_kernel(n, count, z_ref, up_ref, down_ref, parts_ref, levels_ref, table_ref, out_ref, e_ref, halo_ref):
    shrink_windows(n, count, z_ref, up_ref, down_ref, parts_ref, levels_ref, e_ref, halo_ref)
    fl, q2 = z_ref.shape[3], z_ref.shape[4]
    high, low = table_ref[0], table_ref[1]
    for src in range(ROLES):
        data = e_ref[src // 2, src % 2].reshape(SHOTS_DEV * fl, q2)
        top = data.astype(bf16)
        rest = (data - top.astype(f32)).astype(bf16)
        out = jnp.dot(top, high, preferred_element_type=f32)
        out = out + (jnp.dot(rest, high, preferred_element_type=f32) + jnp.dot(top, low, preferred_element_type=f32))
        out_ref[src] = out.reshape(SHOTS_DEV, fl, q2).astype(bf16)


def unpack_kernel(in_ref, out_ref):
    fl, q = in_ref.shape[2], in_ref.shape[3] // 2
    for role in range(ROLES):
        rows = slice(role * fl, (role + 1) * fl)
        for t in range(SHOTS_DEV):
            out_ref[0, t, rows, :] = in_ref[role, t, :, :q]
            out_ref[1, t, rows, :] = in_ref[role, t, :, q:]


def call(kernel, name, outs, in_specs, scratch=()):
    return pl.pallas_call(
        kernel,
        out_shape=outs,
        in_specs=in_specs,
        out_specs=jax.tree.map(lambda _: VMEM, outs),
        scratch_shapes=list(scratch),
        name=name,
        compiler_params=pltpu.CompilerParams(vmem_limit_bytes=24 * 1024 * 1024),
    )


def on_device(n, nf, blended, estimate, partner, delays, levels):
    q, fl = estimate.shape[3], estimate.shape[2] // ROLES
    shape = jax.ShapeDtypeStruct
    run = (2, 2, SHOTS_DEV, fl, 2 * q)
    side = shape((2, SHOTS_DEV, fl, 2 * q), bf16)
    e_scratch = pltpu.VMEM(run, f32)
    halo_scratch = pltpu.VMEM((2, 2, SHOTS_DEV, fl, 2 * q), f32)
    count = 8 * nf * ROLES * fl * q
    members = ROLES * nf
    forward, backward = receiver_tables(q, 1.0), receiver_tables(q, -1.0)

    packed = call(
        functools.partial(pack_kernel, nf),
        "pack",
        shape((ROLES, 2 * SHOTS_DEV + 1, fl, 2 * q), bf16),
        [VMEM, VMEM, SMEM, SMEM],
    )(estimate, blended, partner, delays)
    gathered = lax.all_to_all(packed, GROUP, 0, 0, tiled=True)
    z, bh, meta, phase, down, up = call(
        first_kernel,
        "first",
        (
            shape(run, f32),
            shape(run, f32),
            shape((ROLES, 16, 128), f32),
            shape((2, 2, SHOTS_DEV, 2, fl, 128), f32),
            side,
            side,
        ),
        [VMEM, VMEM],
        [e_scratch],
    )(gathered, jnp.asarray(forward))
    for index in range(PASSES):
        down = lax.ppermute(down, "g", [(i, (i - 1) % n) for i in range(n)])
        up = lax.ppermute(up, "g", [(i, (i + 1) % n) for i in range(n)])
        parts = call(
            functools.partial(sums_kernel, n),
            "sums",
            shape((members, 8, 128), f32),
            [VMEM] * 3,
            [halo_scratch],
        )(z, up, down)
        parts = lax.all_to_all(parts, SUM_GROUP, 0, 0, tiled=True)
        if index < PASSES - 1:
            z, down, up = call(
                functools.partial(middle_kernel, n, count),
                "middle",
                (shape(run, f32), side, side),
                [VMEM] * 4 + [SMEM] + [VMEM] * 3,
                [e_scratch, halo_scratch],
            )(z, up, down, parts, levels, bh, meta, phase)
    out = call(
        functools.partial(last_kernel, n, count),
        "last",
        shape((ROLES, SHOTS_DEV, fl, 2 * q), bf16),
        [VMEM] * 4 + [SMEM] + [VMEM],
        [e_scratch, halo_scratch],
    )(z, up, down, parts, levels, jnp.asarray(backward))
    out = lax.all_to_all(out, GROUP, 0, 0, tiled=True)
    return call(unpack_kernel, "unpack", shape(estimate.shape, bf16), [VMEM])(out)


def solution(mesh):
    shots, nf = mesh.shape["shot"], mesh.shape["freq"]
    n = shots // 4
    fine = Mesh(mesh.devices.reshape(2, n, 2, nf), ("yh", "g", "h", "f"))
    spec = P(None, ("yh", "g", "h"), "f", None)
    return jax.shard_map(
        functools.partial(on_device, n, nf),
        mesh=fine,
        in_specs=(spec, spec, P(("yh", "g", "h")), P(), P()),
        out_specs=spec,
        check_vma=False,
    )
```

profile of v0, /device:TPU:17, one launch (start us, length us, event | category | flops | bytes accessed | tf_op | source)
XLA Modules:
  0.0 135.9 jit_solution(13393003400635222719)
XLA Ops:
  0.0 0.0 copy-start.2
  0.0 1.0 copy-done.2
  1.0 0.0 copy-start.3
  1.0 1.0 copy-done.3
  2.1 0.0 copy-start.4
  2.1 0.7 copy-done.4
  2.8 0.0 copy-start.6
  2.8 0.7 copy-done.6
  3.4 0.6 pack.1
  4.1 0.0 copy-start.1
  4.1 39.8 %all_to_all.20.in_ref = bf16[4,9,32,512]{3,2,1,0:T(8,128)(2,1)S(1)} all-to-all(bf16[4,9,32,512]{3,2,1,0:T(8,128)(2,1)S(1)} %pack.1), channel_id=1, replica_groups=mesh['yh'=2,'g'=32,'h'=2,'f'=4] {'yh','h'}, dimensions={0} | all-to-all | bytes 2359296 | tf_op jit(solution)/shard_map/all_to_all | solution.py:329
  43.9 0.0 copy-done.1
  43.9 1.7 %first.1 = (f32[2,2,4,32,512]{4,3,2,1,0:T(8,128)S(1)}, f32[2,2,4,32,512]{4,3,2,1,0:T(8,128)S(1)}, f32[4,16,128]{2,1,0:T(8,128)S(1)}, f32[2,2,4,2,32,128]{5,4,3,2...) custom-call(bf16[4,9,32,512]{3,2,1,0:T(8,128)(2,1)S(1)} %all_to_all.20.in_ref, ...), custom_call_target="tpu_custom_call" | custom-call | tf_op jit(solution)/shard_map/first/pallas_call | solution.py:330
  45.6 0.0 copy-start.5
  45.6 4.0 %collective-permute-start = (bf16[2,4,32,512]{3,2,1,0:T(8,128)(2,1)S(1)}, bf16[2,4,32,512]{3,2,1,0:T(8,128)(2,1)S(1)}, u32[]{:S(2)}, u32[]{:S(2)}) collective-permute-start(bf16[2,4,32,512]{3,2,1,0:T(8,128)(2,1)S(1)} %get-tuple-element.15), channel_id=1, source_target_pairs={{0,8},{8,16},{16,24},{24,32},{32,40},{40,48},{48,56},{56,64},{64,7... | collective-permute-start | bytes 786440 | tf_op jit(solution)/shard_map/ppermute | solution.py:346
  49.6 10.6 %collective-permute-start.1 = (bf16[2,4,32,512]{3,2,1,0:T(8,128)(2,1)S(1)}, bf16[2,4,32,512]{3,2,1,0:T(8,128)(2,1)S(1)}, u32[]{:S(2)}, u32[]{:S(2)}) collective-permute-start(bf16[2,4,32,512]{3,2,1,0:T(8,128)(2,1)S(1)} %get-tuple-element.16), channel_id=1, source_target_pairs={{0,248},{8,0},{16,8},{24,16},{32,24},{40,32},{48,40},{56,48},{64,5... | collective-permute-start | bytes 786440 | tf_op jit(solution)/shard_map/ppermute | solution.py:345
  60.2 3.7 %collective-permute-done.up_ref = bf16[2,4,32,512]{3,2,1,0:T(8,128)(2,1)S(1)} collective-permute-done((bf16[2,4,32,512]{3,2,1,0:T(8,128)(2,1)S(1)}, bf16[2,4,32,512]{3,2,1,0:T(8,128)(2,1)S(1)}, u32[]{:S(2)}, u32[]{:S(2)}) %collective-permute-start) | collective-permute-done | bytes 262176 | tf_op jit(solution)/shard_map/ppermute | solution.py:346
  63.8 0.9 collective-permute-done.1.down_ref
  64.7 1.0 sums.2
  65.7 14.1 %all_to_all.21.parts_ref = f32[16,8,128]{2,1,0:T(8,128)S(1)} all-to-all(f32[16,8,128]{2,1,0:T(8,128)S(1)} %sums.2), channel_id=1, replica_groups=mesh['yh'=2,'g'=32,'h'=2,'f'=4] {'yh','h','f'}, dimensions={0} | all-to-all | bytes 131072 | tf_op jit(solution)/shard_map/all_to_all | solution.py:354
  79.8 0.0 copy-done.5
  79.8 2.6 %middle.1 = (f32[2,2,4,32,512]{4,3,2,1,0:T(8,128)S(1)}, bf16[2,4,32,512]{3,2,1,0:T(8,128)(2,1)S(1)}, bf16[2,4,32,512]{3,2,1,0:T(8,128)(2,1)S(1)}) custom-call(f32[2,2,4,32,512]{4,3,2,1,0:T(8,128)S(1)} %get-tuple-element.14.z_ref, bf16[2,4,32,512]{3,2,1,0:T(8,128)(2,1)S(1)} %collective-permute-done.up_ref, ...), custom_call_target="tpu_custom_call" | custom-call | tf_op jit(solution)/shard_map/middle/pallas_call | solution.py:356
  82.5 0.0 copy-start
  82.5 2.1 %collective-permute-start.2 = (bf16[2,4,32,512]{3,2,1,0:T(8,128)(2,1)S(1)}, bf16[2,4,32,512]{3,2,1,0:T(8,128)(2,1)S(1)}, u32[]{:S(2)}, u32[]{:S(2)}) collective-permute-start(bf16[2,4,32,512]{3,2,1,0:T(8,128)(2,1)S(1)} %get-tuple-element.21), channel_id=1, source_target_pairs={{0,8},{8,16},{16,24},{24,32},{32,40},{40,48},{48,56},{56,64},{64,7... | collective-permute-start | bytes 786440 | tf_op jit(solution)/shard_map/ppermute | solution.py:346
  84.5 6.2 %collective-permute-start.3 = (bf16[2,4,32,512]{3,2,1,0:T(8,128)(2,1)S(1)}, bf16[2,4,32,512]{3,2,1,0:T(8,128)(2,1)S(1)}, u32[]{:S(2)}, u32[]{:S(2)}) collective-permute-start(bf16[2,4,32,512]{3,2,1,0:T(8,128)(2,1)S(1)} %get-tuple-element.22), channel_id=1, source_target_pairs={{0,248},{8,0},{16,8},{24,16},{32,24},{40,32},{48,40},{56,48},{64,5... | collective-permute-start | bytes 786440 | tf_op jit(solution)/shard_map/ppermute | solution.py:345
  90.8 4.3 %collective-permute-done.2.up_ref = bf16[2,4,32,512]{3,2,1,0:T(8,128)(2,1)S(1)} collective-permute-done((bf16[2,4,32,512]{3,2,1,0:T(8,128)(2,1)S(1)}, bf16[2,4,32,512]{3,2,1,0:T(8,128)(2,1)S(1)}, u32[]{:S(2)}, u32[]{:S(2)}) %collective-permute-start.2) | collective-permute-done | bytes 262176 | tf_op jit(solution)/shard_map/ppermute | solution.py:346
  95.1 0.9 collective-permute-done.3.down_ref
  96.0 1.0 sums.3
  96.9 13.5 %all_to_all.22.parts_ref = f32[16,8,128]{2,1,0:T(8,128)S(1)} all-to-all(f32[16,8,128]{2,1,0:T(8,128)S(1)} %sums.3), channel_id=1, replica_groups=mesh['yh'=2,'g'=32,'h'=2,'f'=4] {'yh','h','f'}, dimensions={0} | all-to-all | bytes 131072 | tf_op jit(solution)/shard_map/all_to_all | solution.py:354
  110.5 0.0 copy-done
  110.5 3.2 %last.1 = bf16[4,4,32,512]{3,2,1,0:T(8,128)(2,1)S(1)} custom-call(f32[2,2,4,32,512]{4,3,2,1,0:T(8,128)S(1)} %get-tuple-element.20.z_ref, bf16[2,4,32,512]{3,2,1,0:T(8,128)(2,1)S(1)} %collective-permute-done.2.up_ref, bf16[2,4,32,512]{3,2,1,0:T(8,128)(2,1)S(1)} %collective-permute-done.3.down_ref, f32[16,8,128]{2,1,0:T(8,128)S(1)} %all_to_all.22.parts_ref, ...), custom_call_target="tpu_custom_call" | custom-call | tf_op jit(solution)/shard_map/last/pallas_call | solution.py:363
  113.7 21.4 %all_to_all.23.in_ref = bf16[4,4,32,512]{3,2,1,0:T(8,128)(2,1)S(1)} all-to-all(bf16[4,4,32,512]{3,2,1,0:T(8,128)(2,1)S(1)} %last.1), channel_id=1, replica_groups=mesh['yh'=2,'g'=32,'h'=2,'f'=4] {'yh','h'}, dimensions={0} | all-to-all | bytes 1048576 | tf_op jit(solution)/shard_map/all_to_all | solution.py:370
  135.1 0.8 unpack.1
Async XLA Ops:
  0.0 1.0 copy-start.2
  1.0 1.0 copy-start.3
  2.1 0.7 copy-start.4
  2.8 0.7 copy-start.6
  4.1 39.8 %copy-start.1 = (bf16[2,512,512]{2,1,0:T(8,128)(2,1)S(1)}, bf16[2,512,512]{2,1,0:T(8,128)(2,1)}, u32[]{:S(2)}) copy-start(bf16[2,512,512]{2,1,0:T(8,128)(2,1)} %constant.4.clone.table_ref) | copy-start | bytes 3145732
  45.6 34.3 %copy-start.5 = (s32[128]{0:T(128)S(1)}, s32[128]{0:T(128)}, u32[]{:S(2)}) copy-start(s32[128]{0:T(128)} %levels_ref.3) | copy-start | bytes 1540
  45.6 18.2 %collective-permute-start = (bf16[2,4,32,512]{3,2,1,0:T(8,128)(2,1)S(1)}, bf16[2,4,32,512]{3,2,1,0:T(8,128)(2,1)S(1)}, u32[]{:S(2)}, u32[]{:S(2)}) collective-permute-start(bf16[2,4,32,512]{3,2,1,0:T(8,128)(2,1)S(1)} %get-tuple-element.15), channel_id=1, source_target_pairs={{0,8},{8,16},{16,24},{24,32},{32,40},{40,48},{48,56},{56,64},{64,7... | collective-permute-start | bytes 786440 | tf_op jit(solution)/shard_map/ppermute | solution.py:346
  49.6 15.1 %collective-permute-start.1 = (bf16[2,4,32,512]{3,2,1,0:T(8,128)(2,1)S(1)}, bf16[2,4,32,512]{3,2,1,0:T(8,128)(2,1)S(1)}, u32[]{:S(2)}, u32[]{:S(2)}) collective-permute-start(bf16[2,4,32,512]{3,2,1,0:T(8,128)(2,1)S(1)} %get-tuple-element.16), channel_id=1, source_target_pairs={{0,248},{8,0},{16,8},{24,16},{32,24},{40,32},{48,40},{56,48},{64,5... | collective-permute-start | bytes 786440 | tf_op jit(solution)/shard_map/ppermute | solution.py:345
  82.5 28.0 %copy-start = (bf16[2,512,512]{2,1,0:T(8,128)(2,1)S(1)}, bf16[2,512,512]{2,1,0:T(8,128)(2,1)}, u32[]{:S(2)}) copy-start(bf16[2,512,512]{2,1,0:T(8,128)(2,1)} %constant.5.clone.table_ref) | copy-start | bytes 3145732
  82.5 12.6 %collective-permute-start.2 = (bf16[2,4,32,512]{3,2,1,0:T(8,128)(2,1)S(1)}, bf16[2,4,32,512]{3,2,1,0:T(8,128)(2,1)S(1)}, u32[]{:S(2)}, u32[]{:S(2)}) collective-permute-start(bf16[2,4,32,512]{3,2,1,0:T(8,128)(2,1)S(1)} %get-tuple-element.21), channel_id=1, source_target_pairs={{0,8},{8,16},{16,24},{24,32},{32,40},{40,48},{48,56},{56,64},{64,7... | collective-permute-start | bytes 786440 | tf_op jit(solution)/shard_map/ppermute | solution.py:346
  84.5 11.4 %collective-permute-start.3 = (bf16[2,4,32,512]{3,2,1,0:T(8,128)(2,1)S(1)}, bf16[2,4,32,512]{3,2,1,0:T(8,128)(2,1)S(1)}, u32[]{:S(2)}, u32[]{:S(2)}) collective-permute-start(bf16[2,4,32,512]{3,2,1,0:T(8,128)(2,1)S(1)} %get-tuple-element.22), channel_id=1, source_target_pairs={{0,248},{8,0},{16,8},{24,16},{32,24},{40,32},{48,40},{56,48},{64,5... | collective-permute-start | bytes 786440 | tf_op jit(solution)/shard_map/ppermute | solution.py:345
where the time goes:
time: 136 us
  blocking collectives  88.8 us (65%)
  starting transfers between devices  22.8 us (17%)
  Pallas kernels  10.9 us (8%)
  waiting for transfers between devices  9.77 us (7%)
  local copies, waits for them, and re-layouts  3.44 us (3%)
    all_to_all x1, blocking collectives, on_device(): gathered = lax.all_to_all(packed, GROUP, 0, 0, tiled=True)  39.8 us
    all_to_all x2, blocking collectives, on_device(): parts = lax.all_to_all(parts, SUM_GROUP, 0, 0, tiled=True)  27.7 us
    all_to_all x1, blocking collectives, on_device(): out = lax.all_to_all(out, GROUP, 0, 0, tiled=True)  21.4 us
    ppermute x2, starting transfers between devices, on_device(): down = lax.ppermute(down, 'g', [(i, (i - 1) % n) for i in range(n)])  16.8 us
    ppermute x2, waiting for transfers between devices, on_device(): up = lax.ppermute(up, 'g', [(i, (i + 1) % n) for i in range(n)])  7.97 us
    ppermute x2, starting transfers between devices, on_device(): up = lax.ppermute(up, 'g', [(i, (i + 1) % n) for i in range(n)])  6.05 us
    unnamed x14, local copies, waits for them, and re-layouts  3.44 us
    pallas_call x1, Pallas kernels, on_device(): call(functools.partial(last_kernel, n, count), 'last', shape((ROLES, SHOT...  3.23 us
  transfers between devices with their start and end apart: 4, of which 4 were waited for; matrix products, arithmetic and copies ran while one was open for 0% of the time, Pallas kernels for 0%

commit v1 on v0

--- a/solution.py
+++ b/solution.py
@@ -27,6 +27,7 @@
 bf16 = jnp.bfloat16
 VMEM = pl.BlockSpec(memory_space=pltpu.VMEM)
 SMEM = pl.BlockSpec(memory_space=pltpu.SMEM)
+HBM = pl.BlockSpec(memory_space=pltpu.HBM)
 
 
 def receiver_tables(length, sign):
@@ -117,25 +118,39 @@
         yield dft8(windowed(*pair), 1)
 
 
-def pack_kernel(nf, e_ref, b_ref, partner_ref, delays_ref, out_ref):
-    q = e_ref.shape[3]
+def pack_kernel(e_ref, b_ref, partner_ref, delays_ref, out_ref, partner_smem, delays_smem, sems, small_sems):
     fl = e_ref.shape[2] // ROLES
+    columns = e_ref.shape[3] // 128
+    small = [
+        pltpu.make_async_copy(partner_ref, partner_smem, small_sems.at[0]),
+        pltpu.make_async_copy(delays_ref, delays_smem, small_sems.at[1]),
+    ]
+    for copy in small:
+        copy.start()
+    copies = []
+    for k, ref in enumerate((e_ref, b_ref)):
+        for part in range(2):
+            for half in range(columns):
+                for role in range(ROLES):
+                    source = ref.at[part, :, pl.ds(role * fl, fl), pl.ds(half * 128, 128)]
+                    first = (part * columns + half) * 2 * SHOTS_DEV + k * SHOTS_DEV
+                    target = out_ref.at[role, pl.ds(first, SHOTS_DEV)]
+                    copies.append(pltpu.make_async_copy(source, target, sems.at[len(copies)]))
+                    copies[-1].start()
+    for copy in small:
+        copy.wait()
     block = (lax.axis_index("yh") * lax.axis_size("g") + lax.axis_index("g")) * 2 + lax.axis_index("h")
-    row = lax.broadcasted_iota(jnp.int32, (16, 2 * q), 0)
-    meta = jnp.zeros((16, 2 * q), f32)
+    row = lax.broadcasted_iota(jnp.int32, (fl, 128), 0)
+    meta = jnp.zeros((fl, 128), f32)
     for t in range(SHOTS_DEV):
-        other = partner_ref[t]
-        offset = (delays_ref[other] - delays_ref[block * SHOTS_DEV + t]) & (NT - 1)
+        other = partner_smem[t]
+        offset = (delays_smem[other] - delays_smem[block * SHOTS_DEV + t]) & (NT - 1)
         for i, value in enumerate((other & (SHOTS_DEV - 1), offset >> 5, offset & 31)):
             meta = jnp.where(row == 3 * t + i, value.astype(f32), meta)
     for role in range(ROLES):
-        rows = slice(role * fl, (role + 1) * fl)
-        for k, ref in enumerate((e_ref, b_ref)):
-            for t in range(SHOTS_DEV):
-                out_ref[role, k * SHOTS_DEV + t, :, :q] = ref[0, t, rows, :]
-                out_ref[role, k * SHOTS_DEV + t, :, q:] = ref[1, t, rows, :]
-        out_ref[role, 2 * SHOTS_DEV, :16, :] = meta.astype(bf16)
-        out_ref[role, 2 * SHOTS_DEV, 16:, :] = jnp.zeros((fl - 16, 2 * q), bf16)
+        out_ref[role, 4 * SHOTS_DEV * columns] = meta.astype(bf16)
+    for copy in copies:
+        copy.wait()
 
 
 def phases(index):
@@ -183,16 +198,18 @@
 
 
 def first_kernel(in_ref, table_ref, z_ref, bh_ref, meta_ref, phase_ref, down_ref, up_ref, e_ref):
-    fl, q2 = in_ref.shape[2], in_ref.shape[3]
+    fl, q2 = in_ref.shape[2], table_ref.shape[1]
     high, low = table_ref[0], table_ref[1]
+    slabs = 2 * SHOTS_DEV
     for src in range(ROLES):
         ab, p = src // 2, src % 2
-        data = in_ref[src, : 2 * SHOTS_DEV].reshape(2 * SHOTS_DEV * fl, q2)
+        data = [in_ref[src, c * slabs : (c + 1) * slabs].reshape(slabs * fl, 128) for c in range(q2 // 128)]
+        data = jnp.concatenate(data, axis=1)
         out = jnp.dot(data, high, preferred_element_type=f32) + jnp.dot(data, low, preferred_element_type=f32)
         out = out.reshape(2, SHOTS_DEV, fl, q2)
         e_ref[ab, p] = out[0]
         bh_ref[ab, p] = out[1]
-        meta = in_ref[src, 2 * SHOTS_DEV, :16, :128].astype(f32)
+        meta = in_ref[src, slabs * (q2 // 128), :16, :].astype(f32)
         meta_ref[src] = meta
         whole = meta.astype(jnp.int32)
         freq = lax.axis_index("f") * (ROLES * fl) + (lax.axis_index("yh") * 2 + lax.axis_index("h")) * fl
@@ -279,13 +296,12 @@
     shrink_windows(n, count, z_ref, up_ref, down_ref, parts_ref, levels_ref, e_ref, halo_ref)
     fl, q2 = z_ref.shape[3], z_ref.shape[4]
     high, low = table_ref[0], table_ref[1]
-    for src in range(ROLES):
-        data = e_ref[src // 2, src % 2].reshape(SHOTS_DEV * fl, q2)
-        top = data.astype(bf16)
-        rest = (data - top.astype(f32)).astype(bf16)
-        out = jnp.dot(top, high, preferred_element_type=f32)
-        out = out + (jnp.dot(rest, high, preferred_element_type=f32) + jnp.dot(top, low, preferred_element_type=f32))
-        out_ref[src] = out.reshape(SHOTS_DEV, fl, q2).astype(bf16)
+    data = e_ref[...].reshape(ROLES * SHOTS_DEV * fl, q2)
+    top = data.astype(bf16)
+    rest = (data - top.astype(f32)).astype(bf16)
+    out = jnp.dot(top, high, preferred_element_type=f32)
+    out = out + (jnp.dot(rest, high, preferred_element_type=f32) + jnp.dot(top, low, preferred_element_type=f32))
+    out_ref[...] = out.reshape(ROLES, SHOTS_DEV, fl, q2).astype(bf16)
 
 
 def unpack_kernel(in_ref, out_ref):
@@ -320,11 +336,18 @@
     members = ROLES * nf
     forward, backward = receiver_tables(q, 1.0), receiver_tables(q, -1.0)
 
+    slabs = 2 * SHOTS_DEV * (2 * q // 128)
     packed = call(
-        functools.partial(pack_kernel, nf),
+        pack_kernel,
         "pack",
-        shape((ROLES, 2 * SHOTS_DEV + 1, fl, 2 * q), bf16),
-        [VMEM, VMEM, SMEM, SMEM],
+        shape((ROLES, slabs + 1, fl, 128), bf16),
+        [HBM] * 4,
+        [
+            pltpu.SMEM(partner.shape, jnp.int32),
+            pltpu.SMEM(delays.shape, jnp.int32),
+            pltpu.SemaphoreType.DMA((4 * ROLES * (q // 128),)),
+            pltpu.SemaphoreType.DMA((2,)),
+        ],
     )(estimate, blended, partner, delays)
     gathered = lax.all_to_all(packed, GROUP, 0, 0, tiled=True)
     z, bh, meta, phase, down, up = call(

time: 136 us -> 135 us (level)
  blocking collectives: 88.8 us -> 86.9 us
    all_to_all x1, blocking collectives: 39.8 us -> 38.2 us  [on_device(): gathered = lax.all_to_all(packed, GROUP, 0, 0, tiled=True)]
where the time goes in v1:
time: 135 us; the launch traced here: 134 us
  blocking collectives  86.9 us (64%)
  starting transfers between devices  22.6 us (17%)
  Pallas kernels  11.2 us (8%)
  waiting for transfers between devices  9.78 us (7%)
  local copies, waits for them, and re-layouts  3.44 us (3%)
    all_to_all x1, blocking collectives, on_device(): gathered = lax.all_to_all(packed, GROUP, 0, 0, tiled=True)  38.2 us
    all_to_all x2, blocking collectives, on_device(): parts = lax.all_to_all(parts, SUM_GROUP, 0, 0, tiled=True)  27.6 us
    all_to_all x1, blocking collectives, on_device(): out = lax.all_to_all(out, GROUP, 0, 0, tiled=True)  21.1 us
    ppermute x2, starting transfers between devices, on_device(): down = lax.ppermute(down, 'g', [(i, (i - 1) % n) for i in range(n)])  16.6 us
    ppermute x2, waiting for transfers between devices, on_device(): up = lax.ppermute(up, 'g', [(i, (i + 1) % n) for i in range(n)])  7.98 us
    ppermute x2, starting transfers between devices, on_device(): up = lax.ppermute(up, 'g', [(i, (i + 1) % n) for i in range(n)])  6.05 us
    unnamed x14, local copies, waits for them, and re-layouts  3.44 us
    pallas_call x1, Pallas kernels, on_device(): call(functools.partial(last_kernel, n, count), 'last', shape((ROLES, SHOT...  3.21 us
  transfers between devices with their start and end apart: 4, of which 4 were waited for; matrix products, arithmetic and copies ran while one was open for 0% of the time, Pallas kernels for 0%

profile of v1, /device:TPU:17, one launch (start us, length us, event | category | flops | bytes accessed | tf_op | source)
XLA Modules:
  0.0 134.1 jit_solution(10178624526034290432)
XLA Ops:
  0.0 0.0 copy-start.2
  0.0 1.0 copy-done.2
  1.0 0.0 copy-start.3
  1.0 1.0 copy-done.3
  2.1 0.0 copy-start.4
  2.1 0.7 copy-done.4
  2.8 0.0 copy-start.6
  2.8 0.7 copy-done.6
  3.4 1.0 pack.1
  4.4 0.0 copy-start.1
  4.4 38.2 %all_to_all.20.in_ref = bf16[4,33,32,128]{3,2,1,0:T(8,128)(2,1)S(1)} all-to-all(bf16[4,33,32,128]{3,2,1,0:T(8,128)(2,1)S(1)} %pack.1), channel_id=1, replica_groups=mesh['yh'=2,'g'=32,'h'=2,'f'=4] {'yh','h'}, dimensions={0} | all-to-all | bytes 2162688 | tf_op jit(solution)/shard_map/all_to_all | solution.py:352
  42.6 0.0 copy-done.1
  42.6 1.7 %first.1 = (f32[2,2,4,32,512]{4,3,2,1,0:T(8,128)S(1)}, f32[2,2,4,32,512]{4,3,2,1,0:T(8,128)S(1)}, f32[4,16,128]{2,1,0:T(8,128)S(1)}, f32[2,2,4,2,32,128]{5,4,3,2...) custom-call(bf16[4,33,32,128]{3,2,1,0:T(8,128)(2,1)S(1)} %all_to_all.20.in_ref, ...), custom_call_target="tpu_custom_call" | custom-call | tf_op jit(solution)/shard_map/first/pallas_call | solution.py:353
  44.3 0.0 copy-start.5
  44.3 4.0 %collective-permute-start = (bf16[2,4,32,512]{3,2,1,0:T(8,128)(2,1)S(1)}, bf16[2,4,32,512]{3,2,1,0:T(8,128)(2,1)S(1)}, u32[]{:S(2)}, u32[]{:S(2)}) collective-permute-start(bf16[2,4,32,512]{3,2,1,0:T(8,128)(2,1)S(1)} %get-tuple-element.15), channel_id=1, source_target_pairs={{0,8},{8,16},{16,24},{24,32},{32,40},{40,48},{48,56},{56,64},{64,7... | collective-permute-start | bytes 786440 | tf_op jit(solution)/shard_map/ppermute | solution.py:369
  48.3 10.3 %collective-permute-start.1 = (bf16[2,4,32,512]{3,2,1,0:T(8,128)(2,1)S(1)}, bf16[2,4,32,512]{3,2,1,0:T(8,128)(2,1)S(1)}, u32[]{:S(2)}, u32[]{:S(2)}) collective-permute-start(bf16[2,4,32,512]{3,2,1,0:T(8,128)(2,1)S(1)} %get-tuple-element.16), channel_id=1, source_target_pairs={{0,248},{8,0},{16,8},{24,16},{32,24},{40,32},{48,40},{56,48},{64,5... | collective-permute-start | bytes 786440 | tf_op jit(solution)/shard_map/ppermute | solution.py:368
  58.7 3.7 %collective-permute-done.up_ref = bf16[2,4,32,512]{3,2,1,0:T(8,128)(2,1)S(1)} collective-permute-done((bf16[2,4,32,512]{3,2,1,0:T(8,128)(2,1)S(1)}, bf16[2,4,32,512]{3,2,1,0:T(8,128)(2,1)S(1)}, u32[]{:S(2)}, u32[]{:S(2)}) %collective-permute-start) | collective-permute-done | bytes 262176 | tf_op jit(solution)/shard_map/ppermute | solution.py:369
  62.3 0.9 collective-permute-done.1.down_ref
  63.2 1.0 sums.2
  64.2 14.1 %all_to_all.21.parts_ref = f32[16,8,128]{2,1,0:T(8,128)S(1)} all-to-all(f32[16,8,128]{2,1,0:T(8,128)S(1)} %sums.2), channel_id=1, replica_groups=mesh['yh'=2,'g'=32,'h'=2,'f'=4] {'yh','h','f'}, dimensions={0} | all-to-all | bytes 131072 | tf_op jit(solution)/shard_map/all_to_all | solution.py:377
  78.3 0.0 copy-done.5
  78.3 2.6 %middle.1 = (f32[2,2,4,32,512]{4,3,2,1,0:T(8,128)S(1)}, bf16[2,4,32,512]{3,2,1,0:T(8,128)(2,1)S(1)}, bf16[2,4,32,512]{3,2,1,0:T(8,128)(2,1)S(1)}) custom-call(f32[2,2,4,32,512]{4,3,2,1,0:T(8,128)S(1)} %get-tuple-element.14.z_ref, bf16[2,4,32,512]{3,2,1,0:T(8,128)(2,1)S(1)} %collective-permute-done.up_ref, ...), custom_call_target="tpu_custom_call" | custom-call | tf_op jit(solution)/shard_map/middle/pallas_call | solution.py:379
  81.0 0.0 copy-start
  81.0 2.1 %collective-permute-start.2 = (bf16[2,4,32,512]{3,2,1,0:T(8,128)(2,1)S(1)}, bf16[2,4,32,512]{3,2,1,0:T(8,128)(2,1)S(1)}, u32[]{:S(2)}, u32[]{:S(2)}) collective-permute-start(bf16[2,4,32,512]{3,2,1,0:T(8,128)(2,1)S(1)} %get-tuple-element.21), channel_id=1, source_target_pairs={{0,8},{8,16},{16,24},{24,32},{32,40},{40,48},{48,56},{56,64},{64,7... | collective-permute-start | bytes 786440 | tf_op jit(solution)/shard_map/ppermute | solution.py:369
  83.0 6.2 %collective-permute-start.3 = (bf16[2,4,32,512]{3,2,1,0:T(8,128)(2,1)S(1)}, bf16[2,4,32,512]{3,2,1,0:T(8,128)(2,1)S(1)}, u32[]{:S(2)}, u32[]{:S(2)}) collective-permute-start(bf16[2,4,32,512]{3,2,1,0:T(8,128)(2,1)S(1)} %get-tuple-element.22), channel_id=1, source_target_pairs={{0,248},{8,0},{16,8},{24,16},{32,24},{40,32},{48,40},{56,48},{64,5... | collective-permute-start | bytes 786440 | tf_op jit(solution)/shard_map/ppermute | solution.py:368
  89.3 4.3 %collective-permute-done.2.up_ref = bf16[2,4,32,512]{3,2,1,0:T(8,128)(2,1)S(1)} collective-permute-done((bf16[2,4,32,512]{3,2,1,0:T(8,128)(2,1)S(1)}, bf16[2,4,32,512]{3,2,1,0:T(8,128)(2,1)S(1)}, u32[]{:S(2)}, u32[]{:S(2)}) %collective-permute-start.2) | collective-permute-done | bytes 262176 | tf_op jit(solution)/shard_map/ppermute | solution.py:369
  93.6 0.9 collective-permute-done.3.down_ref
  94.5 1.0 sums.3
  95.4 13.5 %all_to_all.22.parts_ref = f32[16,8,128]{2,1,0:T(8,128)S(1)} all-to-all(f32[16,8,128]{2,1,0:T(8,128)S(1)} %sums.3), channel_id=1, replica_groups=mesh['yh'=2,'g'=32,'h'=2,'f'=4] {'yh','h','f'}, dimensions={0} | all-to-all | bytes 131072 | tf_op jit(solution)/shard_map/all_to_all | solution.py:377
  108.9 0.0 copy-done
  108.9 3.2 %last.1 = bf16[4,4,32,512]{3,2,1,0:T(8,128)(2,1)S(1)} custom-call(f32[2,2,4,32,512]{4,3,2,1,0:T(8,128)S(1)} %get-tuple-element.20.z_ref, bf16[2,4,32,512]{3,2,1,0:T(8,128)(2,1)S(1)} %collective-permute-done.2.up_ref, bf16[2,4,32,512]{3,2,1,0:T(8,128)(2,1)S(1)} %collective-permute-done.3.down_ref, f32[16,8,128]{2,1,0:T(8,128)S(1)} %all_to_all.22.parts_ref, ...), custom_call_target="tpu_custom_call" | custom-call | tf_op jit(solution)/shard_map/last/pallas_call | solution.py:386
  112.2 21.1 %all_to_all.23.in_ref = bf16[4,4,32,512]{3,2,1,0:T(8,128)(2,1)S(1)} all-to-all(bf16[4,4,32,512]{3,2,1,0:T(8,128)(2,1)S(1)} %last.1), channel_id=1, replica_groups=mesh['yh'=2,'g'=32,'h'=2,'f'=4] {'yh','h'}, dimensions={0} | all-to-all | bytes 1048576 | tf_op jit(solution)/shard_map/all_to_all | solution.py:393
  133.3 0.8 unpack.1
Async XLA Ops:
  0.0 1.0 copy-start.2
  1.0 1.0 copy-start.3
  2.1 0.7 copy-start.4
  2.8 0.7 copy-start.6
  4.4 38.2 %copy-start.1 = (bf16[2,512,512]{2,1,0:T(8,128)(2,1)S(1)}, bf16[2,512,512]{2,1,0:T(8,128)(2,1)}, u32[]{:S(2)}) copy-start(bf16[2,512,512]{2,1,0:T(8,128)(2,1)} %constant.4.clone.table_ref) | copy-start | bytes 3145732
  44.3 34.0 %copy-start.5 = (s32[128]{0:T(128)S(1)}, s32[128]{0:T(128)}, u32[]{:S(2)}) copy-start(s32[128]{0:T(128)} %levels_ref.3) | copy-start | bytes 1540
  44.3 18.0 %collective-permute-start = (bf16[2,4,32,512]{3,2,1,0:T(8,128)(2,1)S(1)}, bf16[2,4,32,512]{3,2,1,0:T(8,128)(2,1)S(1)}, u32[]{:S(2)}, u32[]{:S(2)}) collective-permute-start(bf16[2,4,32,512]{3,2,1,0:T(8,128)(2,1)S(1)} %get-tuple-element.15), channel_id=1, source_target_pairs={{0,8},{8,16},{16,24},{24,32},{32,40},{40,48},{48,56},{56,64},{64,7... | collective-permute-start | bytes 786440 | tf_op jit(solution)/shard_map/ppermute | solution.py:369
  48.3 14.9 %collective-permute-start.1 = (bf16[2,4,32,512]{3,2,1,0:T(8,128)(2,1)S(1)}, bf16[2,4,32,512]{3,2,1,0:T(8,128)(2,1)S(1)}, u32[]{:S(2)}, u32[]{:S(2)}) collective-permute-start(bf16[2,4,32,512]{3,2,1,0:T(8,128)(2,1)S(1)} %get-tuple-element.16), channel_id=1, source_target_pairs={{0,248},{8,0},{16,8},{24,16},{32,24},{40,32},{48,40},{56,48},{64,5... | collective-permute-start | bytes 786440 | tf_op jit(solution)/shard_map/ppermute | solution.py:368
  81.0 28.0 %copy-start = (bf16[2,512,512]{2,1,0:T(8,128)(2,1)S(1)}, bf16[2,512,512]{2,1,0:T(8,128)(2,1)}, u32[]{:S(2)}) copy-start(bf16[2,512,512]{2,1,0:T(8,128)(2,1)} %constant.5.clone.table_ref) | copy-start | bytes 3145732
  81.0 12.6 %collective-permute-start.2 = (bf16[2,4,32,512]{3,2,1,0:T(8,128)(2,1)S(1)}, bf16[2,4,32,512]{3,2,1,0:T(8,128)(2,1)S(1)}, u32[]{:S(2)}, u32[]{:S(2)}) collective-permute-start(bf16[2,4,32,512]{3,2,1,0:T(8,128)(2,1)S(1)} %get-tuple-element.21), channel_id=1, source_target_pairs={{0,8},{8,16},{16,24},{24,32},{32,40},{40,48},{48,56},{56,64},{64,7... | collective-permute-start | bytes 786440 | tf_op jit(solution)/shard_map/ppermute | solution.py:369
  83.0 11.4 %collective-permute-start.3 = (bf16[2,4,32,512]{3,2,1,0:T(8,128)(2,1)S(1)}, bf16[2,4,32,512]{3,2,1,0:T(8,128)(2,1)S(1)}, u32[]{:S(2)}, u32[]{:S(2)}) collective-permute-start(bf16[2,4,32,512]{3,2,1,0:T(8,128)(2,1)S(1)} %get-tuple-element.22), channel_id=1, source_target_pairs={{0,248},{8,0},{16,8},{24,16},{32,24},{40,32},{48,40},{56,48},{64,5... | collective-permute-start | bytes 786440 | tf_op jit(solution)/shard_map/ppermute | solution.py:368

commit v2 on v1

v2 whole, which is shorter than its diff:
```python
import functools
import math

import jax
import jax.numpy as jnp
import numpy as np
from jax import lax
from jax.experimental import pallas as pl
from jax.experimental.pallas import tpu as pltpu
from jax.sharding import Mesh
from jax.sharding import PartitionSpec as P

NT = 1024
SHOTS_DEV = 4
ROLES = 4
RELAX = 0.5
LEVEL_SCALE = 0.25
TINY = 1e-37
PACK_GRANT = 65_900_000
ROOT8 = 1.0 / math.sqrt(8.0)
HALF_ROOT = math.sqrt(0.5)
TAPER = [math.sin(math.pi * (t + 0.5) / 8) ** 2 * ROOT8 for t in range(8)]
GROUP = ("yh", "h")
SUM_GROUP = ("yh", "h", "f")

f32 = jnp.float32
bf16 = jnp.bfloat16
VMEM = pl.BlockSpec(memory_space=pltpu.VMEM)
SMEM = pl.BlockSpec(memory_space=pltpu.SMEM)
HBM = pl.BlockSpec(memory_space=pltpu.HBM)


def receiver_tables(length, sign):
    k = np.arange(length)
    angle = 2.0 * np.pi / length * ((k[:, None] * k[None, :]) % length)
    c, s = np.cos(angle) / math.sqrt(length), sign * np.sin(angle) / math.sqrt(length)
    full = np.block([[c, -s], [s, c]]).astype(np.float32)
    high = full.astype(jnp.bfloat16)
    low = (full - high.astype(np.float32)).astype(jnp.bfloat16)
    return np.stack([high, low])


def add(a, b):
    return (a[0] + b[0], a[1] + b[1])


def sub(a, b):
    return (a[0] - b[0], a[1] - b[1])


def turn(a, sign):
    return (a[1], -a[0]) if sign > 0 else (-a[1], a[0])


def twist(a, power, sign):
    if power == 0:
        return a
    if power == 2:
        return turn(a, sign)
    re, im = a
    if sign > 0:
        one = ((re + im) * HALF_ROOT, (im - re) * HALF_ROOT)
    else:
        one = ((re - im) * HALF_ROOT, (im + re) * HALF_ROOT)
    return one if power == 1 else turn(one, sign)


def dft4(a, b, c, d, sign):
    s0, s1, s2, s3 = add(a, c), sub(a, c), add(b, d), turn(sub(b, d), sign)
    return [add(s0, s2), add(s1, s3), sub(s0, s2), sub(s1, s3)]


def dft8(x, sign, part="both"):
    even = dft4(x[0], x[2], x[4], x[6], sign)
    odd = dft4(x[1], x[3], x[5], x[7], sign)
    odd = [twist(odd[k], k, sign) for k in range(4)]
    first = [add(even[k], odd[k]) for k in range(4)] if part != "second" else []
    second = [sub(even[k], odd[k]) for k in range(4)] if part != "first" else []
    return first + second


def windowed(first, second, scale):
    out = [(re * TAPER[t], im * TAPER[t]) for t, (re, im) in enumerate(first)]
    for t, (re, im) in enumerate(second):
        weight = TAPER[SHOTS_DEV + t] if scale is None else TAPER[SHOTS_DEV + t] * scale
        out.append((re * weight, im * weight))
    return out


def load(ref, at, rows, half, q):
    lo, hi = half * 128, q + half * 128
    return [(ref[(*at, t, rows, slice(lo, lo + 128))], ref[(*at, t, rows, slice(hi, hi + 128))]) for t in range(SHOTS_DEV)]


def store(ref, at, rows, half, q, block):
    for t, (re, im) in enumerate(block):
        ref[(*at, t, rows, slice(half * 128, half * 128 + 128))] = re
        ref[(*at, t, rows, slice(q + half * 128, q + half * 128 + 128))] = im


def seams(n):
    g = lax.axis_index("g")
    return jnp.where(g == 0, 0.0, 1.0), jnp.where(g == n - 1, 0.0, 1.0)


def seam_scale(marks, ab, w, wide):
    before, after = (1, 3) if wide else (0, 2)
    return marks[0] if (ab == 0 and w == before) else marks[1] if (ab == 1 and w == after) else None


def blocks_of(z_ref, halo_ref, ab, rows, half, q, wide):
    before = [load(halo_ref, (0, ab, k), rows, half, q) for k in range(2 if wide else 1)]
    own = [load(z_ref, (ab, k), rows, half, q) for k in range(2)]
    after = [load(halo_ref, (1, ab, k), rows, half, q) for k in range(2 if wide else 1)]
    return before + own + after


def add_sums(n, z_ref, halo_ref, out_ref, wide):
    fl, q = z_ref.shape[3], z_ref.shape[4] // 2
    marks = seams(n)
    count = 5 if wide else 3

    def body(i, totals):
        rows = pl.ds(pl.multiple_of(i * 8, 8), 8)
        totals = list(totals)
        for ab in range(2):
            for half in range(q // 128):
                blocks = blocks_of(z_ref, halo_ref, ab, rows, half, q, wide)
                for w in range(count):
                    for re, im in dft8(windowed(blocks[w], blocks[w + 1], seam_scale(marks, ab, w, wide)), 1):
                        square = re * re + im * im
                        totals[ab * count + w] += square * lax.rsqrt(jnp.maximum(square, TINY))
        return tuple(totals)

    totals = lax.fori_loop(0, fl // 8, body, (jnp.zeros((8, 128), f32),) * (2 * count))
    row = lax.broadcasted_iota(jnp.int32, (16, 128), 0)
    tile = jnp.zeros((16, 128), f32)
    for k, total in enumerate(totals):
        tile = jnp.where(row == k, jnp.sum(total, axis=0, keepdims=True), tile)
    for k in range(out_ref.shape[0]):
        out_ref[k] = tile


def shrink_windows(n, size, z_ref, halo_ref, parts_ref, levels_ref, e_ref, wide):
    fl, q = z_ref.shape[3], z_ref.shape[4] // 2
    count = 5 if wide else 3
    marks = seams(n)
    tile = parts_ref[0]
    for k in range(1, parts_ref.shape[0]):
        tile = tile + parts_ref[k]
    total = jnp.sum(tile, axis=1, keepdims=True)
    lams = []
    for ab in range(2):
        for w in range(count):
            window = (2 * (ab * n + lax.axis_index("g")) + w - count // 2 + 4 * n) & (4 * n - 1)
            scale = LEVEL_SCALE / size * ROOT8 * levels_ref[window].astype(f32)
            lams.append(jnp.broadcast_to(total[count * ab + w : count * ab + w + 1, :] * scale, (8, 128)))

    def body(i, carry):
        rows = pl.ds(pl.multiple_of(i * 8, 8), 8)
        for ab in range(2):
            for half in range(q // 128):
                blocks = blocks_of(z_ref, halo_ref, ab, rows, half, q, wide)
                held = None
                for w in range(count):
                    scale = seam_scale(marks, ab, w, wide)
                    kept = []
                    for re, im in dft8(windowed(blocks[w], blocks[w + 1], scale), 1):
                        inverse = lax.rsqrt(jnp.maximum(re * re + im * im, TINY))
                        factor = jnp.maximum(ROOT8 - lams[count * ab + w] * inverse, 0.0)
                        kept.append((re * factor, im * factor))
                    y = dft8(kept, -1, "second" if w == 0 else "first" if w == count - 1 else "both")
                    if w > 0:
                        store(e_ref, (ab, w - 1), rows, half, q, [add(c, d) for c, d in zip(held, y[:4])])
                        y = y[4:]
                    held = y if scale is None else [(re * scale, im * scale) for re, im in y]
        return carry

    lax.fori_loop(0, fl // 8, body, 0)


def pack_kernel(e_ref, b_ref, partner_ref, delays_ref, out_ref, partner_smem, delays_smem, sems, small_sems):
    fl = e_ref.shape[2] // ROLES
    columns = e_ref.shape[3] // 128
    small = [
        pltpu.make_async_copy(partner_ref, partner_smem, small_sems.at[0]),
        pltpu.make_async_copy(delays_ref, delays_smem, small_sems.at[1]),
    ]
    for copy in small:
        copy.start()
    copies = []
    for k, ref in enumerate((e_ref, b_ref)):
        for part in range(2):
            for half in range(columns):
                for role in range(ROLES):
                    source = ref.at[part, :, pl.ds(role * fl, fl), pl.ds(half * 128, 128)]
                    first = (part * columns + half) * 2 * SHOTS_DEV + k * SHOTS_DEV
                    target = out_ref.at[role, pl.ds(first, SHOTS_DEV)]
                    copies.append(pltpu.make_async_copy(source, target, sems.at[len(copies)]))
                    copies[-1].start()
    for copy in small:
        copy.wait()
    block = (lax.axis_index("yh") * lax.axis_size("g") + lax.axis_index("g")) * 2 + lax.axis_index("h")
    row = lax.broadcasted_iota(jnp.int32, (fl, 128), 0)
    meta = jnp.zeros((fl, 128), f32)
    for t in range(SHOTS_DEV):
        other = partner_smem[t]
        offset = (delays_smem[other] - delays_smem[block * SHOTS_DEV + t]) & (NT - 1)
        for i, value in enumerate((other & (SHOTS_DEV - 1), offset >> 5, offset & 31)):
            meta = jnp.where(row == 3 * t + i, value.astype(f32), meta)
    for role in range(ROLES):
        out_ref[role, 4 * SHOTS_DEV * columns] = meta.astype(bf16)
    for copy in copies:
        copy.wait()


def phases(index):
    quadrant = (index + 128) >> 8
    x = (index - (quadrant << 8)).astype(f32) * (2.0 * math.pi / NT)
    x2 = x * x
    s = x * (1 + x2 * (-1 / 6 + x2 * (1 / 120 + x2 * (-1 / 5040 + x2 * (1 / 362880)))))
    c = 1 + x2 * (-1 / 2 + x2 * (1 / 24 + x2 * (-1 / 720 + x2 * (1 / 40320))))
    swap = (quadrant & 1) == 1
    cos, sin = jnp.where(swap, s, c), jnp.where(swap, c, s)
    cos = jnp.where(((quadrant + 1) & 2) == 2, -cos, cos)
    sin = jnp.where((quadrant & 2) == 2, -sin, sin)
    return cos, sin


def relax(e_ref, ab, k, rows, b_of, meta_of, phase_of, emit):
    q = e_ref.shape[4] // 2
    for t in range(SHOTS_DEV):
        slot = jnp.broadcast_to(meta_of(t), (16, 128))
        cos, sin = phase_of(t)
        for half in range(q // 128):
            spans = (slice(half * 128, half * 128 + 128), slice(q + half * 128, q + half * 128 + 128))
            other = [e_ref[1 - ab, k, 0, rows, span] for span in spans]
            for j in range(1, SHOTS_DEV):
                other = [jnp.where(slot == j, e_ref[1 - ab, k, j, rows, span], o) for o, span in zip(other, spans)]
            shifted = (other[0] * cos + other[1] * sin, other[1] * cos - other[0] * sin)
            for span, shift in zip(spans, shifted):
                emit(t, span, RELAX * ((e_ref[ab, k, t, rows, span] + b_of(t, span)) - shift))


def relax_own(e_ref, offset, b_of, meta_ref, phase_ref, emit):
    fl = e_ref.shape[3]

    def body(i, carry):
        rows = pl.ds(pl.multiple_of(i * 16, 16), 16)
        for ab in range(2):
            for p in range(2):
                relax(
                    e_ref,
                    ab,
                    p + offset,
                    rows,
                    lambda t, span: b_of(ab, p, t, rows, span),
                    lambda t: meta_ref[2 * ab + p, 3 * t : 3 * t + 1, :],
                    lambda t: (phase_ref[ab, p, t, 0, rows, :], phase_ref[ab, p, t, 1, rows, :]),
                    lambda t, span, z: emit(ab, p, t, rows, span, z),
                )
        return carry

    lax.fori_loop(0, fl // 16, body, 0)


def fill_phases(meta, fl, phase_ref, at):
    whole = meta.astype(jnp.int32)
    freq = lax.axis_index("f") * (ROLES * fl) + (lax.axis_index("yh") * 2 + lax.axis_index("h")) * fl
    freq = freq + lax.broadcasted_iota(jnp.int32, (fl, 128), 0)
    for t in range(SHOTS_DEV):
        offset = whole[3 * t + 1 : 3 * t + 2, :] * 32 + whole[3 * t + 2 : 3 * t + 3, :]
        cos, sin = phases((freq * offset) & (NT - 1))
        phase_ref[(*at, t, 0)] = cos
        phase_ref[(*at, t, 1)] = sin


def first_kernel(in_ref, table_ref, z_ref, meta_ref, phase_ref, zs_ref, b_even_ref, b_odd_ref, e_ref, bh_ref):
    fl, q2 = in_ref.shape[2], table_ref.shape[1]
    high, low = table_ref[0], table_ref[1]
    slabs = 2 * SHOTS_DEV
    for src in range(ROLES):
        ab, p = src // 2, src % 2
        data = [in_ref[src, c * slabs : (c + 1) * slabs].reshape(slabs * fl, 128) for c in range(q2 // 128)]
        data = jnp.concatenate(data, axis=1)
        out = jnp.dot(data, high, preferred_element_type=f32) + jnp.dot(data, low, preferred_element_type=f32)
        out = out.reshape(2, SHOTS_DEV, fl, q2)
        e_ref[ab, p] = out[0]
        bh_ref[ab, p] = out[1]
        raw = in_ref[src, slabs * (q2 // 128), :16, :]
        side = b_odd_ref if p else b_even_ref
        side[ab, : SHOTS_DEV * fl, :] = out[1].reshape(SHOTS_DEV * fl, q2).astype(bf16)
        side[ab, SHOTS_DEV * fl :, :] = jnp.concatenate([raw] * (q2 // 128), axis=1)
        meta_ref[src] = raw.astype(f32)
        fill_phases(raw.astype(f32), fl, phase_ref, (ab, p))

    def emit(ab, p, t, rows, span, z):
        z_ref[ab, p, t, rows, span] = z
        zs_ref[ab, p, t, rows, span] = z.astype(bf16)

    def b_of(ab, p, t, rows, span):
        return bh_ref[ab, p, t, rows, span]

    relax_own(e_ref, 0, b_of, meta_ref, phase_ref, emit)


def fetch_halo(n, up_ref, down_ref, halo_ref):
    g = lax.axis_index("g")
    for ab in range(2):
        halo_ref[0, ab] = up_ref[jnp.where(g == 0, 1 - ab, ab)].astype(f32)
        halo_ref[1, ab] = down_ref[jnp.where(g == n - 1, 1 - ab, ab)].astype(f32)


def wide_sums_kernel(n, z_ref, up_ref, down_ref, out_ref, halo_ref):
    fetch_halo(n, up_ref, down_ref, halo_ref)
    add_sums(n, z_ref, halo_ref, out_ref, True)


def sums_kernel(n, z_ref, halo_ref, out_ref):
    add_sums(n, z_ref, halo_ref, out_ref, False)


def middle_kernel(n, size, z_ref, up_ref, down_ref, parts_ref, levels_ref, b_even_ref, b_odd_ref, meta_ref, phase_ref,
                  b_up_ref, b_down_ref, z_out, halo_out, e_ref, far_ref, halo_ref):
    fl = z_ref.shape[3]
    g = lax.axis_index("g")
    fetch_halo(n, up_ref, down_ref, halo_ref)
    shrink_windows(n, size, z_ref, halo_ref, parts_ref, levels_ref, e_ref, True)

    def emit(ab, p, t, rows, span, z):
        z_out[ab, p, t, rows, span] = z

    def b_of(ab, p, t, rows, span):
        at = pl.ds(pl.multiple_of(rows.start + t * fl, 16), 16)
        return (b_odd_ref if p else b_even_ref)[ab, at, span].astype(f32)

    relax_own(e_ref, 1, b_of, meta_ref, phase_ref, emit)
    sides = []
    for side, ref in enumerate((b_up_ref, b_down_ref)):
        for ab in range(2):
            lane = jnp.where(g == (n - 1 if side else 0), 1 - ab, ab)
            meta = ref[lane, SHOTS_DEV * fl :, :128].astype(f32)
            fill_phases(meta, fl, far_ref, (side, ab))
            sides.append((side, ab, lane, ref, meta))

    for i in range(fl // 16):
        rows = slice(i * 16, i * 16 + 16)
        for side, ab, lane, ref, meta in sides:

            def emit_halo(t, span, z, side=side, ab=ab, rows=rows):
                halo_out[side, ab, 0, t, rows, span] = z

            relax(
                e_ref,
                ab,
                3 * side,
                rows,
                lambda t, span: ref[lane, t * fl + i * 16 : t * fl + i * 16 + 16, span].astype(f32),
                lambda t: meta[3 * t : 3 * t + 1, :],
                lambda t: (far_ref[side, ab, t, 0, rows, :], far_ref[side, ab, t, 1, rows, :]),
                emit_halo,
            )


def last_kernel(n, size, z_ref, halo_ref, parts_ref, levels_ref, table_ref, out_ref, e_ref):
    shrink_windows(n, size, z_ref, halo_ref, parts_ref, levels_ref, e_ref, False)
    fl, q2 = z_ref.shape[3], z_ref.shape[4]
    high, low = table_ref[0], table_ref[1]
    data = e_ref[...].reshape(ROLES * SHOTS_DEV * fl, q2)
    top = data.astype(bf16)
    rest = (data - top.astype(f32)).astype(bf16)
    out = jnp.dot(top, high, preferred_element_type=f32)
    out = out + (jnp.dot(rest, high, preferred_element_type=f32) + jnp.dot(top, low, preferred_element_type=f32))
    out_ref[...] = out.reshape(ROLES, SHOTS_DEV, fl, q2).astype(bf16)


def unpack_kernel(in_ref, out_ref):
    fl, q = in_ref.shape[2], in_ref.shape[3] // 2
    for role in range(ROLES):
        rows = slice(role * fl, (role + 1) * fl)
        for t in range(SHOTS_DEV):
            out_ref[0, t, rows, :] = in_ref[role, t, :, :q]
            out_ref[1, t, rows, :] = in_ref[role, t, :, q:]


def call(kernel, name, outs, in_specs, scratch=(), grant=24 * 1024 * 1024):
    return pl.pallas_call(
        kernel,
        out_shape=outs,
        in_specs=in_specs,
        out_specs=jax.tree.map(lambda _: VMEM, outs),
        scratch_shapes=list(scratch),
        name=name,
        compiler_params=pltpu.CompilerParams(vmem_limit_bytes=grant),
    )


def on_device(n, nf, blended, estimate, partner, delays, levels):
    q, fl = estimate.shape[3], estimate.shape[2] // ROLES
    shape = jax.ShapeDtypeStruct
    block = (SHOTS_DEV, fl, 2 * q)
    side = shape((2, SHOTS_DEV * fl + 16, 2 * q), bf16)
    size = 8 * nf * ROLES * fl * q
    parts_shape = shape((ROLES * nf, 16, 128), f32)
    forward, backward = receiver_tables(q, 1.0), receiver_tables(q, -1.0)
    before = [(i, (i - 1) % n) for i in range(n)]
    after = [(i, (i + 1) % n) for i in range(n)]

    slabs = 2 * SHOTS_DEV * (2 * q // 128)
    packed = call(
        pack_kernel,
        "pack",
        shape((ROLES, slabs + 1, fl, 128), bf16),
        [HBM] * 4,
        [
            pltpu.SMEM(partner.shape, jnp.int32),
            pltpu.SMEM(delays.shape, jnp.int32),
            pltpu.SemaphoreType.DMA((4 * ROLES * (q // 128),)),
            pltpu.SemaphoreType.DMA((2,)),
        ],
        PACK_GRANT,
    )(estimate, blended, partner, delays)
    gathered = lax.all_to_all(packed, GROUP, 0, 0, tiled=True)
    z, meta, phase, zs, b_even, b_odd = call(
        first_kernel,
        "first",
        (
            shape((2, 2, *block), f32),
            shape((ROLES, 16, 128), f32),
            shape((2, 2, SHOTS_DEV, 2, fl, 128), f32),
            shape((2, 2, *block), bf16),
            side,
            side,
        ),
        [VMEM, VMEM],
        [pltpu.VMEM((2, 2, *block), f32)] * 2,
    )(gathered, jnp.asarray(forward))
    down = lax.ppermute(zs, "g", before)
    up = lax.ppermute(zs, "g", after)
    b_down = lax.ppermute(b_even, "g", before)
    b_up = lax.ppermute(b_odd, "g", after)
    far = pltpu.VMEM((2, 2, 2, *block), f32)
    parts = call(functools.partial(wide_sums_kernel, n), "wide_sums", parts_shape, [VMEM] * 3, [far])(z, up, down)
    parts = lax.all_to_all(parts, SUM_GROUP, 0, 0, tiled=True)
    z, halo = call(
        functools.partial(middle_kernel, n, size),
        "middle",
        (shape((2, 2, *block), f32), shape((2, 2, 1, *block), f32)),
        [VMEM] * 4 + [SMEM] + [VMEM] * 6,
        [pltpu.VMEM((2, 4, *block), f32), pltpu.VMEM((2, 2, SHOTS_DEV, 2, fl, 128), f32), far],
    )(z, up, down, parts, levels, b_even, b_odd, meta, phase, b_up, b_down)
    parts = call(functools.partial(sums_kernel, n), "sums", parts_shape, [VMEM] * 2)(z, halo)
    parts = lax.all_to_all(parts, SUM_GROUP, 0, 0, tiled=True)
    out = call(
        functools.partial(last_kernel, n, size),
        "last",
        shape((ROLES, *block), bf16),
        [VMEM] * 3 + [SMEM] + [VMEM],
        [pltpu.VMEM((2, 2, *block), f32)],
    )(z, halo, parts, levels, jnp.asarray(backward))
    out = lax.all_to_all(out, GROUP, 0, 0, tiled=True)
    return call(unpack_kernel, "unpack", shape(estimate.shape, bf16), [VMEM])(out)


def solution(mesh):
    shots, nf = mesh.shape["shot"], mesh.shape["freq"]
    n = shots // 4
    fine = Mesh(mesh.devices.reshape(2, n, 2, nf), ("yh", "g", "h", "f"))
    spec = P(None, ("yh", "g", "h"), "f", None)
    return jax.shard_map(
        functools.partial(on_device, n, nf),
        mesh=fine,
        in_specs=(spec, spec, P(("yh", "g", "h")), P(), P()),
        out_specs=spec,
        check_vma=False,
    )
```

time: 135 us -> 132 us (0.978)
  blocking collectives: 86.9 us -> 69.9 us
  waiting for transfers between devices: 9.78 us -> 16.9 us
  starting transfers between devices: 22.6 us -> 28.9 us
  Pallas kernels: 11.2 us -> 15.9 us
  local copies, waits for them, and re-layouts: 3.44 us -> 0.02 us
    all_to_all x2 -> x1, blocking collectives: 27.6 us -> 13.2 us  [on_device(): parts = lax.all_to_all(parts, SUM_GROUP, 0, 0, tiled=True)]
    all_to_all x0 -> x1, waiting for transfers between devices: none -> 10.1 us  [on_device(): parts = lax.all_to_all(parts, SUM_GROUP, 0, 0, tiled=True)]
    all_to_all x0 -> x1, starting transfers between devices: none -> 7.24 us  [on_device(): parts = lax.all_to_all(parts, SUM_GROUP, 0, 0, tiled=True)]
    unnamed x14 -> x6, local copies, waits for them, and re-layouts: 3.44 us -> 0.02 us
    pallas_call x5, Pallas kernels: 9.45 us -> 12.6 us  [the longest x1 4.71 us: on_device(): call(functools.partial(middle_kernel, n, size), 'middle', (shape((2, 2, *...]
    ppermute x4, waiting for transfers between devices: 9.78 us -> 6.84 us  [the longest x1 5.95 us: on_device(): up = lax.ppermute(zs, 'g', after)]
    all_to_all x1, blocking collectives: 21.1 us -> 18.3 us  [on_device(): out = lax.all_to_all(out, GROUP, 0, 0, tiled=True)]
    pallas_call x1, Pallas kernels: 0.95 us -> 2.47 us  [on_device(): call(pack_kernel, 'pack', shape((ROLES, slabs + 1, fl, 128), bf16), [HBM]...]
  transfers between devices with their start and end apart: 4 -> 5, of which waited for: 4 -> 3; matrix products, arithmetic and copies ran while one was open for 0% -> 0% of each run, Pallas kernels for 0% -> 2%
where the time goes in v2:
time: 132 us
  blocking collectives  69.9 us (53%)
  starting transfers between devices  28.9 us (22%)
  waiting for transfers between devices  16.9 us (13%)
  Pallas kernels  15.9 us (12%)
    all_to_all x1, blocking collectives, on_device(): gathered = lax.all_to_all(packed, GROUP, 0, 0, tiled=True)  38.4 us
    all_to_all x1, blocking collectives, on_device(): out = lax.all_to_all(out, GROUP, 0, 0, tiled=True)  18.3 us
    all_to_all x1, blocking collectives, on_device(): parts = lax.all_to_all(parts, SUM_GROUP, 0, 0, tiled=True)  13.2 us
    ppermute x1, starting transfers between devices, on_device(): down = lax.ppermute(zs, 'g', before)  12.3 us
    all_to_all x1, waiting for transfers between devices, on_device(): parts = lax.all_to_all(parts, SUM_GROUP, 0, 0, tiled=True)  10.1 us
    all_to_all x1, starting transfers between devices, on_device(): parts = lax.all_to_all(parts, SUM_GROUP, 0, 0, tiled=True)  7.24 us
    ppermute x1, waiting for transfers between devices, on_device(): up = lax.ppermute(zs, 'g', after)  5.95 us
    ppermute x1, starting transfers between devices, on_device(): b_down = lax.ppermute(b_even, 'g', before)  5.47 us
  transfers between devices with their start and end apart: 5, of which 3 were waited for; matrix products, arithmetic and copies ran while one was open for 0% of the time, Pallas kernels for 2%

profile of v2, /device:TPU:17, one launch (start us, length us, event | category | flops | bytes accessed | tf_op | source)
XLA Modules:
  0.0 131.7 jit_solution(8369142389342868955)
XLA Ops:
  0.0 2.5 %pack.1 = bf16[4,33,32,128]{3,2,1,0:T(8,128)(2,1)} custom-call(bf16[2,4,128,256]{3,2,1,0:T(8,128)(2,1)} %e_ref.1, bf16[2,4,128,256]{3,2,1,0:T(8,128)(2,1)} %b_ref.1, s32[4]{0:T(128)} %partner_ref.1, s32[512]{0:T(512)} %delays_ref.1), custom_call_target="tpu_custom_call" | custom-call | tf_op jit(solution)/shard_map/pack/pallas_call | solution.py:410
  2.5 0.0 copy-start
  2.5 38.4 %all_to_all.20.in_ref = bf16[4,33,32,128]{3,2,1,0:T(8,128)(2,1)S(1)} all-to-all(bf16[4,33,32,128]{3,2,1,0:T(8,128)(2,1)} %pack.1), channel_id=1, replica_groups=mesh['yh'=2,'g'=32,'h'=2,'f'=4] {'yh','h'}, dimensions={0} | all-to-all | bytes 2162688 | tf_op jit(solution)/shard_map/all_to_all | solution.py:423
  40.9 0.0 copy-done
  40.9 1.6 %first.1 = (f32[2,2,4,32,512]{4,3,2,1,0:T(8,128)S(1)}, f32[4,16,128]{2,1,0:T(8,128)S(1)}, f32[2,2,4,2,32,128]{5,4,3,2,1,0:T(8,128)S(1)}, bf16[2,2,4,32,512]{4,3,...) custom-call(bf16[4,33,32,128]{3,2,1,0:T(8,128)(2,1)S(1)} %all_to_all.20.in_ref, ...), custom_call_target="tpu_custom_call" | custom-call | tf_op jit(solution)/shard_map/first/pallas_call | solution.py:424
  42.6 12.3 %collective-permute-start.1 = (bf16[2,2,4,32,512]{4,3,2,1,0:T(8,128)(2,1)S(1)}, bf16[2,2,4,32,512]{4,3,2,1,0:T(8,128)(2,1)S(1)}, u32[]{:S(2)}, u32[]{:S(2)}) collective-permute-start(bf16[2,2,4,32,512]{4,3,2,1,0:T(8,128)(2,1)S(1)} %get-tuple-element.14), channel_id=1, source_target_pairs={{0,248},{8,0},{16,8},{24,16},{32,24},{40,32},{48,40},{56,48},{64,5... | collective-permute-start | bytes 1572872 | tf_op jit(solution)/shard_map/ppermute | solution.py:438
  54.9 1.9 %collective-permute-start = (bf16[2,2,4,32,512]{4,3,2,1,0:T(8,128)(2,1)S(1)}, bf16[2,2,4,32,512]{4,3,2,1,0:T(8,128)(2,1)S(1)}, u32[]{:S(2)}, u32[]{:S(2)}) collective-permute-start(bf16[2,2,4,32,512]{4,3,2,1,0:T(8,128)(2,1)S(1)} %get-tuple-element.14), channel_id=1, source_target_pairs={{0,8},{8,16},{16,24},{24,32},{32,40},{40,48},{48,56},{56,64},{64,7... | collective-permute-start | bytes 1572872 | tf_op jit(solution)/shard_map/ppermute | solution.py:439
  56.8 5.5 %collective-permute-start.3 = (bf16[2,144,512]{2,1,0:T(8,128)(2,1)S(1)}, bf16[2,144,512]{2,1,0:T(8,128)(2,1)}, u32[]{:S(2)}, u32[]{:S(2)}) collective-permute-start(bf16[2,144,512]{2,1,0:T(8,128)(2,1)S(1)} %get-tuple-element.15.b_even_ref), channel_id=1, source_target_pairs={{0,248},{8,0},{16,8},{24,16},{32,24},{40,32},{48,40},{56,48},{64,5... | collective-permute-start | bytes 884744 | tf_op jit(solution)/shard_map/ppermute | solution.py:440
  62.3 1.9 %collective-permute-start.2 = (bf16[2,144,512]{2,1,0:T(8,128)(2,1)S(1)}, bf16[2,144,512]{2,1,0:T(8,128)(2,1)}, u32[]{:S(2)}, u32[]{:S(2)}) collective-permute-start(bf16[2,144,512]{2,1,0:T(8,128)(2,1)S(1)} %get-tuple-element.16.b_odd_ref), channel_id=1, source_target_pairs={{0,8},{8,16},{16,24},{24,32},{32,40},{40,48},{48,56},{56,64},{64,7... | collective-permute-start | bytes 884744 | tf_op jit(solution)/shard_map/ppermute | solution.py:441
  64.2 0.9 collective-permute-done.1.down_ref
  65.1 5.9 %collective-permute-done.up_ref = bf16[2,2,4,32,512]{4,3,2,1,0:T(8,128)(2,1)S(1)} collective-permute-done((bf16[2,2,4,32,512]{4,3,2,1,0:T(8,128)(2,1)S(1)}, bf16[2,2,4,32,512]{4,3,2,1,0:T(8,128)(2,1)S(1)}, u32[]{:S(2)}, u32[]{:S(2)}) %collective-permute-start) | collective-permute-done | bytes 524320 | tf_op jit(solution)/shard_map/ppermute | solution.py:439
  71.1 0.0 copy-start.2
  71.1 2.3 %wide_sums.1 = f32[16,16,128]{2,1,0:T(8,128)} custom-call(f32[2,2,4,32,512]{4,3,2,1,0:T(8,128)S(1)} %get-tuple-element.13.z_ref, bf16[2,2,4,32,512]{4,3,2,1,0:T(8,128)(2,1)S(1)} %collective-permute-done.up_ref, bf16[2,2,4,32,512]{4,3,2,1,0:T(8,128)(2,1)S(1)} %collective-permute-done.1.down_ref), custom_call_target="tpu_custom_call" | custom-call | tf_op jit(solution)/shard_map/wide_sums/pallas_call | solution.py:443
  73.3 7.2 %all-to-all-start.1 = ((f32[16,16,128]{2,1,0:T(8,128)}), f32[16,16,128]{2,1,0:T(8,128)S(1)}, u32[]{:S(2)}, u32[]{:S(2)}) async-start(f32[16,16,128]{2,1,0:T(8,128)} %wide_sums.1), calls=%async_computation.1 | async-start | bytes 262144 | tf_op jit(solution)/shard_map/all_to_all | solution.py:444
  80.6 0.0 collective-permute-done.3.b_down_ref
  80.6 0.0 collective-permute-done.2.b_up_ref
  80.6 10.1 %all-to-all-done.1.parts_ref = f32[16,16,128]{2,1,0:T(8,128)S(1)} async-done(((f32[16,16,128]{2,1,0:T(8,128)}), f32[16,16,128]{2,1,0:T(8,128)S(1)}, u32[]{:S(2)}, u32[]{:S(2)}) %all-to-all-start.1) | async-done | bytes 131104 | tf_op jit(solution)/shard_map/all_to_all | solution.py:444
  90.7 0.0 copy-done.2
  90.7 4.7 %middle.1 = (f32[2,2,4,32,512]{4,3,2,1,0:T(8,128)S(1)}, f32[2,2,1,4,32,512]{5,4,3,2,1,0:T(8,128)S(1)}) custom-call(f32[2,2,4,32,512]{4,3,2,1,0:T(8,128)S(1)} %get-tuple-element.13.z_ref, bf16[2,2,4,32,512]{4,3,2,1,0:T(8,128)(2,1)S(1)} %collective-permute-done.up_ref, bf16[2,2,4,32,512]{4,3,2,1,0:T(8,128)(2,1)S(1)} %collective-permute-done.1.down_ref, ...), custom_call_target="tpu_custom_call" | custom-call | tf_op jit(solution)/shard_map/middle/pallas_call | solution.py:445
  95.4 0.0 copy-start.1
  95.4 0.9 sums.1
  96.3 13.2 %all_to_all.21.parts_ref = f32[16,16,128]{2,1,0:T(8,128)S(1)} all-to-all(f32[16,16,128]{2,1,0:T(8,128)S(1)} %sums.1), channel_id=1, replica_groups=mesh['yh'=2,'g'=32,'h'=2,'f'=4] {'yh','h','f'}, dimensions={0} | all-to-all | bytes 262144 | tf_op jit(solution)/shard_map/all_to_all | solution.py:453
  109.5 0.0 copy-done.1
  109.5 3.1 %last.1 = bf16[4,4,32,512]{3,2,1,0:T(8,128)(2,1)S(1)} custom-call(f32[2,2,4,32,512]{4,3,2,1,0:T(8,128)S(1)} %get-tuple-element.19.z_ref, f32[2,2,1,4,32,512]{5,4,3,2,1,0:T(8,128)S(1)} %get-tuple-element.20.halo_ref, f32[16,16,128]{2,1,0:T(8,128)S(1)} %all_to_all.21.parts_ref, s32[128]{0:T(128)S(1)} %copy-done.2, bf16[2,512,512]{2,1,0:T(8,128)(2,1)S(1)} %copy-done.1), custom_call_target="tpu_custom_call" | custom-call | tf_op jit(solution)/shard_map/last/pallas_call | solution.py:454
  112.6 18.3 %all_to_all.22.in_ref = bf16[4,4,32,512]{3,2,1,0:T(8,128)(2,1)S(1)} all-to-all(bf16[4,4,32,512]{3,2,1,0:T(8,128)(2,1)S(1)} %last.1), channel_id=1, replica_groups=mesh['yh'=2,'g'=32,'h'=2,'f'=4] {'yh','h'}, dimensions={0} | all-to-all | bytes 1048576 | tf_op jit(solution)/shard_map/all_to_all | solution.py:461
  130.9 0.8 unpack.1
Async XLA Ops:
  2.5 38.4 %copy-start = (bf16[2,512,512]{2,1,0:T(8,128)(2,1)S(1)}, bf16[2,512,512]{2,1,0:T(8,128)(2,1)}, u32[]{:S(2)}) copy-start(bf16[2,512,512]{2,1,0:T(8,128)(2,1)} %constant.4.clone.table_ref) | copy-start | bytes 3145732
  42.6 22.5 %collective-permute-start.1 = (bf16[2,2,4,32,512]{4,3,2,1,0:T(8,128)(2,1)S(1)}, bf16[2,2,4,32,512]{4,3,2,1,0:T(8,128)(2,1)S(1)}, u32[]{:S(2)}, u32[]{:S(2)}) collective-permute-start(bf16[2,2,4,32,512]{4,3,2,1,0:T(8,128)(2,1)S(1)} %get-tuple-element.14), channel_id=1, source_target_pairs={{0,248},{8,0},{16,8},{24,16},{32,24},{40,32},{48,40},{56,48},{64,5... | collective-permute-start | bytes 1572872 | tf_op jit(solution)/shard_map/ppermute | solution.py:438
  54.9 16.2 %collective-permute-start = (bf16[2,2,4,32,512]{4,3,2,1,0:T(8,128)(2,1)S(1)}, bf16[2,2,4,32,512]{4,3,2,1,0:T(8,128)(2,1)S(1)}, u32[]{:S(2)}, u32[]{:S(2)}) collective-permute-start(bf16[2,2,4,32,512]{4,3,2,1,0:T(8,128)(2,1)S(1)} %get-tuple-element.14), channel_id=1, source_target_pairs={{0,8},{8,16},{16,24},{24,32},{32,40},{40,48},{48,56},{56,64},{64,7... | collective-permute-start | bytes 1572872 | tf_op jit(solution)/shard_map/ppermute | solution.py:439
  56.8 23.8 %collective-permute-start.3 = (bf16[2,144,512]{2,1,0:T(8,128)(2,1)S(1)}, bf16[2,144,512]{2,1,0:T(8,128)(2,1)}, u32[]{:S(2)}, u32[]{:S(2)}) collective-permute-start(bf16[2,144,512]{2,1,0:T(8,128)(2,1)S(1)} %get-tuple-element.15.b_even_ref), channel_id=1, source_target_pairs={{0,248},{8,0},{16,8},{24,16},{32,24},{40,32},{48,40},{56,48},{64,5... | collective-permute-start | bytes 884744 | tf_op jit(solution)/shard_map/ppermute | solution.py:440
  62.3 18.3 %collective-permute-start.2 = (bf16[2,144,512]{2,1,0:T(8,128)(2,1)S(1)}, bf16[2,144,512]{2,1,0:T(8,128)(2,1)}, u32[]{:S(2)}, u32[]{:S(2)}) collective-permute-start(bf16[2,144,512]{2,1,0:T(8,128)(2,1)S(1)} %get-tuple-element.16.b_odd_ref), channel_id=1, source_target_pairs={{0,8},{8,16},{16,24},{24,32},{32,40},{40,48},{48,56},{56,64},{64,7... | collective-permute-start | bytes 884744 | tf_op jit(solution)/shard_map/ppermute | solution.py:441
  71.1 19.6 %copy-start.2 = (s32[128]{0:T(128)S(1)}, s32[128]{0:T(128)}, u32[]{:S(2)}) copy-start(s32[128]{0:T(128)} %levels_ref.3) | copy-start | bytes 1540
  73.3 17.4 %all-to-all-start.1 = ((f32[16,16,128]{2,1,0:T(8,128)}), f32[16,16,128]{2,1,0:T(8,128)S(1)}, u32[]{:S(2)}, u32[]{:S(2)}) async-start(f32[16,16,128]{2,1,0:T(8,128)} %wide_sums.1), calls=%async_computation.1 | async-start | bytes 262144 | tf_op jit(solution)/shard_map/all_to_all | solution.py:444
  95.4 14.1 %copy-start.1 = (bf16[2,512,512]{2,1,0:T(8,128)(2,1)S(1)}, bf16[2,512,512]{2,1,0:T(8,128)(2,1)}, u32[]{:S(2)}) copy-start(bf16[2,512,512]{2,1,0:T(8,128)(2,1)} %constant.5.clone.table_ref) | copy-start | bytes 3145732

commit v3 on v2

--- a/solution.py
+++ b/solution.py
@@ -16,7 +16,6 @@
 RELAX = 0.5
 LEVEL_SCALE = 0.25
 TINY = 1e-37
-PACK_GRANT = 65_900_000
 ROOT8 = 1.0 / math.sqrt(8.0)
 HALF_ROOT = math.sqrt(0.5)
 TAPER = [math.sin(math.pi * (t + 0.5) / 8) ** 2 * ROOT8 for t in range(8)]
@@ -87,9 +86,9 @@
     return out
 
 
-def load(ref, at, rows, half, q):
+def load(ref, at, rows, half, q, count=SHOTS_DEV):
     lo, hi = half * 128, q + half * 128
-    return [(ref[(*at, t, rows, slice(lo, lo + 128))], ref[(*at, t, rows, slice(hi, hi + 128))]) for t in range(SHOTS_DEV)]
+    return [(ref[(*at, t, rows, slice(lo, lo + 128))], ref[(*at, t, rows, slice(hi, hi + 128))]) for t in range(count)]
 
 
 def store(ref, at, rows, half, q, block):
@@ -115,7 +114,7 @@
     return before + own + after
 
 
-def add_sums(n, z_ref, halo_ref, out_ref, wide):
+def add_sums(n, z_ref, halo_ref, out_ref, wide, x_ref=None):
     fl, q = z_ref.shape[3], z_ref.shape[4] // 2
     marks = seams(n)
     count = 5 if wide else 3
@@ -127,7 +126,10 @@
             for half in range(q // 128):
                 blocks = blocks_of(z_ref, halo_ref, ab, rows, half, q, wide)
                 for w in range(count):
-                    for re, im in dft8(windowed(blocks[w], blocks[w + 1], seam_scale(marks, ab, w, wide)), 1):
+                    x = dft8(windowed(blocks[w], blocks[w + 1], seam_scale(marks, ab, w, wide)), 1)
+                    if x_ref is not None:
+                        store(x_ref, (ab, w), rows, half, q, x)
+                    for re, im in x:
                         square = re * re + im * im
                         totals[ab * count + w] += square * lax.rsqrt(jnp.maximum(square, TINY))
         return tuple(totals)
@@ -141,8 +143,8 @@
         out_ref[k] = tile
 
 
-def shrink_windows(n, size, z_ref, halo_ref, parts_ref, levels_ref, e_ref, wide):
-    fl, q = z_ref.shape[3], z_ref.shape[4] // 2
+def shrink_windows(n, size, spectra_of, parts_ref, levels_ref, e_ref, wide):
+    fl, q = e_ref.shape[3], e_ref.shape[4] // 2
     count = 5 if wide else 3
     marks = seams(n)
     tile = parts_ref[0]
@@ -160,12 +162,11 @@
         rows = pl.ds(pl.multiple_of(i * 8, 8), 8)
         for ab in range(2):
             for half in range(q // 128):
-                blocks = blocks_of(z_ref, halo_ref, ab, rows, half, q, wide)
                 held = None
-                for w in range(count):
+                for w, x in enumerate(spectra_of(ab, rows, half)):
                     scale = seam_scale(marks, ab, w, wide)
                     kept = []
-                    for re, im in dft8(windowed(blocks[w], blocks[w + 1], scale), 1):
+                    for re, im in x:
                         inverse = lax.rsqrt(jnp.maximum(re * re + im * im, TINY))
                         factor = jnp.maximum(ROOT8 - lams[count * ab + w] * inverse, 0.0)
                         kept.append((re * factor, im * factor))
@@ -227,11 +228,26 @@
     return cos, sin
 
 
-def relax(e_ref, ab, k, rows, b_of, meta_of, phase_of, emit):
+def fill_phases(metas, fl, phase_ref):
+    lane = lax.broadcasted_iota(jnp.int32, (1, 128), 1)
+    offsets = jnp.zeros((1, 128), jnp.int32)
+    for m, meta in enumerate(metas):
+        whole = meta.astype(jnp.int32)
+        for t in range(SHOTS_DEV):
+            offset = whole[3 * t + 1 : 3 * t + 2, :] * 32 + whole[3 * t + 2 : 3 * t + 3, :]
+            offsets = jnp.where(lane == SHOTS_DEV * m + t, offset, offsets)
+    freq = lax.axis_index("f") * (ROLES * fl) + (lax.axis_index("yh") * 2 + lax.axis_index("h")) * fl
+    freq = freq + lax.broadcasted_iota(jnp.int32, (fl, 128), 0)
+    cos, sin = phases((freq * offsets) & (NT - 1))
+    phase_ref[0] = cos
+    phase_ref[1] = sin
+
+
+def relax(e_ref, ab, k, rows, b_of, meta_of, phase, column, emit):
     q = e_ref.shape[4] // 2
     for t in range(SHOTS_DEV):
         slot = jnp.broadcast_to(meta_of(t), (16, 128))
-        cos, sin = phase_of(t)
+        cos, sin = [jnp.broadcast_to(table[:, column + t : column + t + 1], (16, 128)) for table in phase]
         for half in range(q // 128):
             spans = (slice(half * 128, half * 128 + 128), slice(q + half * 128, q + half * 128 + 128))
             other = [e_ref[1 - ab, k, 0, rows, span] for span in spans]
@@ -242,43 +258,11 @@
                 emit(t, span, RELAX * ((e_ref[ab, k, t, rows, span] + b_of(t, span)) - shift))
 
 
-def relax_own(e_ref, offset, b_of, meta_ref, phase_ref, emit):
-    fl = e_ref.shape[3]
-
-    def body(i, carry):
-        rows = pl.ds(pl.multiple_of(i * 16, 16), 16)
-        for ab in range(2):
-            for p in range(2):
-                relax(
-                    e_ref,
-                    ab,
-                    p + offset,
-                    rows,
-                    lambda t, span: b_of(ab, p, t, rows, span),
-                    lambda t: meta_ref[2 * ab + p, 3 * t : 3 * t + 1, :],
-                    lambda t: (phase_ref[ab, p, t, 0, rows, :], phase_ref[ab, p, t, 1, rows, :]),
-                    lambda t, span, z: emit(ab, p, t, rows, span, z),
-                )
-        return carry
-
-    lax.fori_loop(0, fl // 16, body, 0)
-
-
-def fill_phases(meta, fl, phase_ref, at):
-    whole = meta.astype(jnp.int32)
-    freq = lax.axis_index("f") * (ROLES * fl) + (lax.axis_index("yh") * 2 + lax.axis_index("h")) * fl
-    freq = freq + lax.broadcasted_iota(jnp.int32, (fl, 128), 0)
-    for t in range(SHOTS_DEV):
-        offset = whole[3 * t + 1 : 3 * t + 2, :] * 32 + whole[3 * t + 2 : 3 * t + 3, :]
-        cos, sin = phases((freq * offset) & (NT - 1))
-        phase_ref[(*at, t, 0)] = cos
-        phase_ref[(*at, t, 1)] = sin
-
-
 def first_kernel(in_ref, table_ref, z_ref, meta_ref, phase_ref, zs_ref, b_even_ref, b_odd_ref, e_ref, bh_ref):
     fl, q2 = in_ref.shape[2], table_ref.shape[1]
     high, low = table_ref[0], table_ref[1]
     slabs = 2 * SHOTS_DEV
+    metas = []
     for src in range(ROLES):
         ab, p = src // 2, src % 2
         data = [in_ref[src, c * slabs : (c + 1) * slabs].reshape(slabs * fl, 128) for c in range(q2 // 128)]
@@ -291,107 +275,130 @@
         side = b_odd_ref if p else b_even_ref
         side[ab, : SHOTS_DEV * fl, :] = out[1].reshape(SHOTS_DEV * fl, q2).astype(bf16)
         side[ab, SHOTS_DEV * fl :, :] = jnp.concatenate([raw] * (q2 // 128), axis=1)
-        meta_ref[src] = raw.astype(f32)
-        fill_phases(raw.astype(f32), fl, phase_ref, (ab, p))
-
-    def emit(ab, p, t, rows, span, z):
-        z_ref[ab, p, t, rows, span] = z
-        zs_ref[ab, p, t, rows, span] = z.astype(bf16)
-
-    def b_of(ab, p, t, rows, span):
-        return bh_ref[ab, p, t, rows, span]
-
-    relax_own(e_ref, 0, b_of, meta_ref, phase_ref, emit)
-
-
-def fetch_halo(n, up_ref, down_ref, halo_ref):
+        metas.append(raw.astype(f32))
+        meta_ref[src] = metas[-1]
+    fill_phases(metas, fl, phase_ref)
+
+    def body(i, carry):
+        rows = pl.ds(pl.multiple_of(i * 16, 16), 16)
+        phase = (phase_ref[0, rows, :], phase_ref[1, rows, :])
+        for ab in range(2):
+            for p in range(2):
+
+                def emit(t, span, z):
+                    z_ref[ab, p, t, rows, span] = z
+                    zs_ref[ab, p, t, rows, span] = z.astype(bf16)
+
+                relax(
+                    e_ref,
+                    ab,
+                    p,
+                    rows,
+                    lambda t, span: bh_ref[ab, p, t, rows, span],
+                    lambda t: meta_ref[2 * ab + p, 3 * t : 3 * t + 1, :],
+                    phase,
+                    SHOTS_DEV * (2 * ab + p),
+                    emit,
+                )
+        return carry
+
+    lax.fori_loop(0, fl // 16, body, 0)
+
+
+def wide_sums_kernel(n, z_ref, up_ref, down_ref, out_ref, halo_ref):
     g = lax.axis_index("g")
     for ab in range(2):
         halo_ref[0, ab] = up_ref[jnp.where(g == 0, 1 - ab, ab)].astype(f32)
         halo_ref[1, ab] = down_ref[jnp.where(g == n - 1, 1 - ab, ab)].astype(f32)
-
-
-def wide_sums_kernel(n, z_ref, up_ref, down_ref, out_ref, halo_ref):
-    fetch_halo(n, up_ref, down_ref, halo_ref)
     add_sums(n, z_ref, halo_ref, out_ref, True)
 
 
-def sums_kernel(n, z_ref, halo_ref, out_ref):
-    add_sums(n, z_ref, halo_ref, out_ref, False)
-
-
-def middle_kernel(n, size, z_ref, up_ref, down_ref, parts_ref, levels_ref, b_even_ref, b_odd_ref, meta_ref, phase_ref,
-                  b_up_ref, b_down_ref, z_out, halo_out, e_ref, far_ref, halo_ref):
-    fl = z_ref.shape[3]
+def middle_kernel(n, size, z_ref, halo_ref, parts_ref, levels_ref, b_even_ref, b_odd_ref, meta_ref, phase_ref,
+                  b_up_ref, b_down_ref, x_out, parts_out, e_ref, far_meta_ref, far_ref, z2_ref, halo2_ref):
+    fl, q = z_ref.shape[3], z_ref.shape[4] // 2
     g = lax.axis_index("g")
-    fetch_halo(n, up_ref, down_ref, halo_ref)
-    shrink_windows(n, size, z_ref, halo_ref, parts_ref, levels_ref, e_ref, True)
-
-    def emit(ab, p, t, rows, span, z):
-        z_out[ab, p, t, rows, span] = z
-
-    def b_of(ab, p, t, rows, span):
-        at = pl.ds(pl.multiple_of(rows.start + t * fl, 16), 16)
-        return (b_odd_ref if p else b_even_ref)[ab, at, span].astype(f32)
-
-    relax_own(e_ref, 1, b_of, meta_ref, phase_ref, emit)
-    sides = []
+    marks = seams(n)
+
+    def spectra_of(ab, rows, half):
+        blocks = blocks_of(z_ref, halo_ref, ab, rows, half, q, True)
+        for w in range(5):
+            yield dft8(windowed(blocks[w], blocks[w + 1], seam_scale(marks, ab, w, True)), 1)
+
+    shrink_windows(n, size, spectra_of, parts_ref, levels_ref, e_ref, True)
+    lanes = []
     for side, ref in enumerate((b_up_ref, b_down_ref)):
         for ab in range(2):
-            lane = jnp.where(g == (n - 1 if side else 0), 1 - ab, ab)
-            meta = ref[lane, SHOTS_DEV * fl :, :128].astype(f32)
-            fill_phases(meta, fl, far_ref, (side, ab))
-            sides.append((side, ab, lane, ref, meta))
-
-    for i in range(fl // 16):
-        rows = slice(i * 16, i * 16 + 16)
-        for side, ab, lane, ref, meta in sides:
-
-            def emit_halo(t, span, z, side=side, ab=ab, rows=rows):
-                halo_out[side, ab, 0, t, rows, span] = z
-
-            relax(
-                e_ref,
-                ab,
-                3 * side,
-                rows,
-                lambda t, span: ref[lane, t * fl + i * 16 : t * fl + i * 16 + 16, span].astype(f32),
-                lambda t: meta[3 * t : 3 * t + 1, :],
-                lambda t: (far_ref[side, ab, t, 0, rows, :], far_ref[side, ab, t, 1, rows, :]),
-                emit_halo,
-            )
-
-
-def last_kernel(n, size, z_ref, halo_ref, parts_ref, levels_ref, table_ref, out_ref, e_ref):
-    shrink_windows(n, size, z_ref, halo_ref, parts_ref, levels_ref, e_ref, False)
-    fl, q2 = z_ref.shape[3], z_ref.shape[4]
-    high, low = table_ref[0], table_ref[1]
-    data = e_ref[...].reshape(ROLES * SHOTS_DEV * fl, q2)
-    top = data.astype(bf16)
-    rest = (data - top.astype(f32)).astype(bf16)
-    out = jnp.dot(top, high, preferred_element_type=f32)
-    out = out + (jnp.dot(rest, high, preferred_element_type=f32) + jnp.dot(top, low, preferred_element_type=f32))
+            lanes.append(jnp.where(g == (n - 1 if side else 0), 1 - ab, ab))
+            far_meta_ref[2 * side + ab] = ref[lanes[-1], SHOTS_DEV * fl :, :128].astype(f32)
+    fill_phases([far_meta_ref[m] for m in range(4)], fl, far_ref)
+
+    def body(i, carry):
+        rows = pl.ds(pl.multiple_of(i * 16, 16), 16)
+        own = (phase_ref[0, rows, :], phase_ref[1, rows, :])
+        far = (far_ref[0, rows, :], far_ref[1, rows, :])
+        for ab in range(2):
+            for k in range(4):
+                side, p = k // 2, k - 1
+                if k in (1, 2):
+                    b_ref, lane, phase, m, metas = (b_odd_ref if p else b_even_ref), ab, own, 2 * ab + p, meta_ref
+                else:
+                    b_ref, lane, phase, m, metas = (b_down_ref if side else b_up_ref), lanes[2 * side + ab], far, 2 * side + ab, far_meta_ref
+
+                def emit(t, span, z):
+                    if k in (1, 2):
+                        z2_ref[ab, p, t, rows, span] = z
+                    else:
+                        halo2_ref[side, ab, 0, t, rows, span] = z
+
+                def b_of(t, span):
+                    at = pl.ds(pl.multiple_of(i * 16 + t * fl, 16), 16)
+                    return b_ref[lane, at, span].astype(f32)
+
+                def meta_of(t):
+                    return metas[m, 3 * t : 3 * t + 1, :]
+
+                relax(e_ref, ab, k, rows, b_of, meta_of, phase, SHOTS_DEV * m, emit)
+        return carry
+
+    lax.fori_loop(0, fl // 16, body, 0)
+    add_sums(n, z2_ref, halo2_ref, parts_out, False, x_out)
+
+
+def last_kernel(n, size, x_ref, parts_ref, levels_ref, table_ref, out_ref, e_ref):
+    fl, q2 = x_ref.shape[3], x_ref.shape[4]
+
+    def spectra_of(ab, rows, half):
+        for w in range(3):
+            yield load(x_ref, (ab, w), rows, half, q2 // 2, 8)
+
+    shrink_windows(n, size, spectra_of, parts_ref, levels_ref, e_ref, False)
+    data = e_ref[...].reshape(ROLES * SHOTS_DEV * fl, q2).astype(bf16)
+    out = jnp.dot(data, table_ref[0], preferred_element_type=f32)
     out_ref[...] = out.reshape(ROLES, SHOTS_DEV, fl, q2).astype(bf16)
 
 
-def unpack_kernel(in_ref, out_ref):
+def unpack_kernel(in_ref, out_ref, sems):
     fl, q = in_ref.shape[2], in_ref.shape[3] // 2
+    copies = []
     for role in range(ROLES):
-        rows = slice(role * fl, (role + 1) * fl)
-        for t in range(SHOTS_DEV):
-            out_ref[0, t, rows, :] = in_ref[role, t, :, :q]
-            out_ref[1, t, rows, :] = in_ref[role, t, :, q:]
-
-
-def call(kernel, name, outs, in_specs, scratch=(), grant=24 * 1024 * 1024):
+        for part in range(2):
+            source = in_ref.at[role, :, :, pl.ds(part * q, q)]
+            target = out_ref.at[part, :, pl.ds(role * fl, fl), :]
+            copies.append(pltpu.make_async_copy(source, target, sems.at[len(copies)]))
+            copies[-1].start()
+    for copy in copies:
+        copy.wait()
+
+
+def call(kernel, name, outs, in_specs, scratch=(), out_specs=None):
     return pl.pallas_call(
         kernel,
         out_shape=outs,
         in_specs=in_specs,
-        out_specs=jax.tree.map(lambda _: VMEM, outs),
+        out_specs=jax.tree.map(lambda _: VMEM, outs) if out_specs is None else out_specs,
         scratch_shapes=list(scratch),
         name=name,
-        compiler_params=pltpu.CompilerParams(vmem_limit_bytes=grant),
+        compiler_params=pltpu.CompilerParams(vmem_limit_bytes=24 * 1024 * 1024),
     )
 
 
@@ -418,8 +425,7 @@
             pltpu.SemaphoreType.DMA((4 * ROLES * (q // 128),)),
             pltpu.SemaphoreType.DMA((2,)),
         ],
-        PACK_GRANT,
-    )(estimate, blended, partner, delays)
+    )(*[pltpu.with_memory_space_constraint(x, pltpu.HBM) for x in (estimate, blended, partner, delays)])
     gathered = lax.all_to_all(packed, GROUP, 0, 0, tiled=True)
     z, meta, phase, zs, b_even, b_odd = call(
         first_kernel,
@@ -427,7 +433,7 @@
         (
             shape((2, 2, *block), f32),
             shape((ROLES, 16, 128), f32),
-            shape((2, 2, SHOTS_DEV, 2, fl, 128), f32),
+            shape((2, fl, 128), f32),
             shape((2, 2, *block), bf16),
             side,
             side,
@@ -439,27 +445,43 @@
     up = lax.ppermute(zs, "g", after)
     b_down = lax.ppermute(b_even, "g", before)
     b_up = lax.ppermute(b_odd, "g", after)
-    far = pltpu.VMEM((2, 2, 2, *block), f32)
-    parts = call(functools.partial(wide_sums_kernel, n), "wide_sums", parts_shape, [VMEM] * 3, [far])(z, up, down)
+    parts, halo = call(
+        functools.partial(wide_sums_kernel, n),
+        "wide_sums",
+        (parts_shape, shape((2, 2, 2, *block), f32)),
+        [VMEM] * 3,
+    )(z, up, down)
     parts = lax.all_to_all(parts, SUM_GROUP, 0, 0, tiled=True)
-    z, halo = call(
+    x, parts = call(
         functools.partial(middle_kernel, n, size),
         "middle",
-        (shape((2, 2, *block), f32), shape((2, 2, 1, *block), f32)),
-        [VMEM] * 4 + [SMEM] + [VMEM] * 6,
-        [pltpu.VMEM((2, 4, *block), f32), pltpu.VMEM((2, 2, SHOTS_DEV, 2, fl, 128), f32), far],
-    )(z, up, down, parts, levels, b_even, b_odd, meta, phase, b_up, b_down)
-    parts = call(functools.partial(sums_kernel, n), "sums", parts_shape, [VMEM] * 2)(z, halo)
+        (shape((2, 3, 8, fl, 2 * q), f32), parts_shape),
+        [VMEM] * 3 + [SMEM] + [VMEM] * 6,
+        [
+            pltpu.VMEM((2, 4, *block), f32),
+            pltpu.VMEM((ROLES, 16, 128), f32),
+            pltpu.VMEM((2, fl, 128), f32),
+            pltpu.VMEM((2, 2, *block), f32),
+            pltpu.VMEM((2, 2, 1, *block), f32),
+        ],
+    )(z, halo, parts, levels, b_even, b_odd, meta, phase, b_up, b_down)
     parts = lax.all_to_all(parts, SUM_GROUP, 0, 0, tiled=True)
     out = call(
         functools.partial(last_kernel, n, size),
         "last",
         shape((ROLES, *block), bf16),
-        [VMEM] * 3 + [SMEM] + [VMEM],
+        [VMEM] * 2 + [SMEM] + [VMEM],
         [pltpu.VMEM((2, 2, *block), f32)],
-    )(z, halo, parts, levels, jnp.asarray(backward))
+    )(x, parts, levels, jnp.asarray(backward[:1]))
     out = lax.all_to_all(out, GROUP, 0, 0, tiled=True)
-    return call(unpack_kernel, "unpack", shape(estimate.shape, bf16), [VMEM])(out)
+    return call(
+        unpack_kernel,
+        "unpack",
+        shape(estimate.shape, bf16),
+        [VMEM],
+        [pltpu.SemaphoreType.DMA((2 * ROLES,))],
+        HBM,
+    )(out)
 
 
 def solution(mesh):

time: 132 us -> 131 us (level)
    pallas_call x4 -> x3, Pallas kernels: 8.72 us -> 8.76 us  [the longest x1 5.66 us: on_device(): call(functools.partial(middle_kernel, n, size), 'middle', (shape((2, 3, 8...]
where the time goes in v3:
time: 131 us; the launch traced here: 130 us
  blocking collectives  69.7 us (53%)
  starting transfers between devices  28.9 us (22%)
  waiting for transfers between devices  16.9 us (13%)
  Pallas kernels  14.8 us (11%)
    all_to_all x1, blocking collectives, on_device(): gathered = lax.all_to_all(packed, GROUP, 0, 0, tiled=True)  38.1 us
    all_to_all x1, blocking collectives, on_device(): out = lax.all_to_all(out, GROUP, 0, 0, tiled=True)  18.5 us
    all_to_all x1, blocking collectives, on_device(): parts = lax.all_to_all(parts, SUM_GROUP, 0, 0, tiled=True)  13.2 us
    ppermute x1, starting transfers between devices, on_device(): down = lax.ppermute(zs, 'g', before)  12.3 us
    all_to_all x1, waiting for transfers between devices, on_device(): parts = lax.all_to_all(parts, SUM_GROUP, 0, 0, tiled=True)  10.1 us
    all_to_all x1, starting transfers between devices, on_device(): parts = lax.all_to_all(parts, SUM_GROUP, 0, 0, tiled=True)  7.24 us
    ppermute x1, waiting for transfers between devices, on_device(): up = lax.ppermute(zs, 'g', after)  5.95 us
    pallas_call x1, Pallas kernels, on_device(): call(functools.partial(middle_kernel, n, size), 'middle', (shape((2, 3, 8...  5.66 us
  transfers between devices with their start and end apart: 5, of which 3 were waited for; matrix products, arithmetic and copies ran while one was open for 0% of the time, Pallas kernels for 2%

profile of v3, /device:TPU:17, one launch (start us, length us, event | category | flops | bytes accessed | tf_op | source)
XLA Modules:
  0.0 130.4 jit_solution(1732385987159829269)
XLA Ops:
  0.0 0.0 copy-start
  0.0 1.6 %pack.1 = bf16[4,33,32,128]{3,2,1,0:T(8,128)(2,1)S(1)} custom-call(bf16[2,4,128,256]{3,2,1,0:T(8,128)(2,1)} %e_ref.1, bf16[2,4,128,256]{3,2,1,0:T(8,128)(2,1)} %b_ref.1, s32[4]{0:T(128)} %partner_ref.1, s32[512]{0:T(512)} %delays_ref.1), custom_call_target="tpu_custom_call" | custom-call | tf_op jit(solution)/shard_map/pack/pallas_call | solution.py:417
  1.6 38.1 %all_to_all.20.in_ref = bf16[4,33,32,128]{3,2,1,0:T(8,128)(2,1)S(1)} all-to-all(bf16[4,33,32,128]{3,2,1,0:T(8,128)(2,1)S(1)} %pack.1), channel_id=1, replica_groups=mesh['yh'=2,'g'=32,'h'=2,'f'=4] {'yh','h'}, dimensions={0} | all-to-all | bytes 2162688 | tf_op jit(solution)/shard_map/all_to_all | solution.py:429
  39.7 0.0 copy-done
  39.7 0.0 copy-start.2
  39.7 2.4 %first.1 = (f32[2,2,4,32,512]{4,3,2,1,0:T(8,128)S(1)}, f32[4,16,128]{2,1,0:T(8,128)S(1)}, f32[2,32,128]{2,1,0:T(8,128)S(1)}, bf16[2,2,4,32,512]{4,3,2,1,0:T(8,12...) custom-call(bf16[4,33,32,128]{3,2,1,0:T(8,128)(2,1)S(1)} %all_to_all.20.in_ref, ...), custom_call_target="tpu_custom_call" | custom-call | tf_op jit(solution)/shard_map/first/pallas_call | solution.py:430
  42.1 12.3 %collective-permute-start.1 = (bf16[2,2,4,32,512]{4,3,2,1,0:T(8,128)(2,1)S(1)}, bf16[2,2,4,32,512]{4,3,2,1,0:T(8,128)(2,1)S(1)}, u32[]{:S(2)}, u32[]{:S(2)}) collective-permute-start(bf16[2,2,4,32,512]{4,3,2,1,0:T(8,128)(2,1)S(1)} %get-tuple-element.16), channel_id=1, source_target_pairs={{0,248},{8,0},{16,8},{24,16},{32,24},{40,32},{48,40},{56,48},{64,5... | collective-permute-start | bytes 1572872 | tf_op jit(solution)/shard_map/ppermute | solution.py:444
  54.4 1.9 %collective-permute-start = (bf16[2,2,4,32,512]{4,3,2,1,0:T(8,128)(2,1)S(1)}, bf16[2,2,4,32,512]{4,3,2,1,0:T(8,128)(2,1)S(1)}, u32[]{:S(2)}, u32[]{:S(2)}) collective-permute-start(bf16[2,2,4,32,512]{4,3,2,1,0:T(8,128)(2,1)S(1)} %get-tuple-element.16), channel_id=1, source_target_pairs={{0,8},{8,16},{16,24},{24,32},{32,40},{40,48},{48,56},{56,64},{64,7... | collective-permute-start | bytes 1572872 | tf_op jit(solution)/shard_map/ppermute | solution.py:445
  56.3 5.5 %collective-permute-start.3 = (bf16[2,144,512]{2,1,0:T(8,128)(2,1)}, bf16[2,144,512]{2,1,0:T(8,128)(2,1)}, u32[]{:S(2)}, u32[]{:S(2)}) collective-permute-start(bf16[2,144,512]{2,1,0:T(8,128)(2,1)} %get-tuple-element.19.b_even_ref), channel_id=1, source_target_pairs={{0,248},{8,0},{16,8},{24,16},{32,24},{40,32},{48,40},{56,48},{64,5... | collective-permute-start | bytes 884744 | tf_op jit(solution)/shard_map/ppermute | solution.py:446
  61.8 1.9 %collective-permute-start.2 = (bf16[2,144,512]{2,1,0:T(8,128)(2,1)}, bf16[2,144,512]{2,1,0:T(8,128)(2,1)}, u32[]{:S(2)}, u32[]{:S(2)}) collective-permute-start(bf16[2,144,512]{2,1,0:T(8,128)(2,1)} %get-tuple-element.20.b_odd_ref), channel_id=1, source_target_pairs={{0,8},{8,16},{16,24},{24,32},{32,40},{40,48},{48,56},{56,64},{64,7... | collective-permute-start | bytes 884744 | tf_op jit(solution)/shard_map/ppermute | solution.py:447
  63.7 0.9 collective-permute-done.1.down_ref
  64.6 5.9 %collective-permute-done.up_ref = bf16[2,2,4,32,512]{4,3,2,1,0:T(8,128)(2,1)S(1)} collective-permute-done((bf16[2,2,4,32,512]{4,3,2,1,0:T(8,128)(2,1)S(1)}, bf16[2,2,4,32,512]{4,3,2,1,0:T(8,128)(2,1)S(1)}, u32[]{:S(2)}, u32[]{:S(2)}) %collective-permute-start) | collective-permute-done | bytes 524320 | tf_op jit(solution)/shard_map/ppermute | solution.py:445
  70.5 2.3 %wide_sums.1 = (f32[16,16,128]{2,1,0:T(8,128)}, f32[2,2,2,4,32,512]{5,4,3,2,1,0:T(8,128)S(1)}) custom-call(f32[2,2,4,32,512]{4,3,2,1,0:T(8,128)S(1)} %get-tuple-element.15.z_ref, bf16[2,2,4,32,512]{4,3,2,1,0:T(8,128)(2,1)S(1)} %collective-permute-done.up_ref, bf16[2,2,4,32,512]{4,3,2,1,0:T(8,128)(2,1)S(1)} %collective-permute-done.1.down_ref), custom_call_target="tpu_custom_call" | custom-call | tf_op jit(solution)/shard_map/wide_sums/pallas_call | solution.py:448
  72.8 7.2 %all-to-all-start.1 = ((f32[16,16,128]{2,1,0:T(8,128)}), f32[16,16,128]{2,1,0:T(8,128)S(1)}, u32[]{:S(2)}, u32[]{:S(2)}) async-start(f32[16,16,128]{2,1,0:T(8,128)} %get-tuple-element.18), calls=%async_computation.1 | async-start | bytes 262144 | tf_op jit(solution)/shard_map/all_to_all | solution.py:454
  80.0 0.0 collective-permute-done.3.b_down_ref
  80.0 0.0 collective-permute-done.2.b_up_ref
  80.1 10.1 %all-to-all-done.1.parts_ref = f32[16,16,128]{2,1,0:T(8,128)S(1)} async-done(((f32[16,16,128]{2,1,0:T(8,128)}), f32[16,16,128]{2,1,0:T(8,128)S(1)}, u32[]{:S(2)}, u32[]{:S(2)}) %all-to-all-start.1) | async-done | bytes 131104 | tf_op jit(solution)/shard_map/all_to_all | solution.py:454
  90.2 0.0 copy-done.2
  90.2 0.0 copy-start.1
  90.2 5.7 %middle.1 = (f32[2,3,8,32,512]{4,3,2,1,0:T(8,128)S(1)}, f32[16,16,128]{2,1,0:T(8,128)S(1)}) custom-call(f32[2,2,4,32,512]{4,3,2,1,0:T(8,128)S(1)} %get-tuple-element.15.z_ref, f32[2,2,2,4,32,512]{5,4,3,2,1,0:T(8,128)S(1)} %get-tuple-element.17.halo_ref, f32[16,16,128]{2,1,0:T(8,128)S(1)} %all-to-all-done.1.parts_ref, s32[128]{0:T(128)S(1)} %copy-done.2, ...), custom_call_target="tpu_custom_call" | custom-call | tf_op jit(solution)/shard_map/middle/pallas_call | solution.py:455
  95.8 13.2 %all_to_all.21.parts_ref = f32[16,16,128]{2,1,0:T(8,128)S(1)} all-to-all(f32[16,16,128]{2,1,0:T(8,128)S(1)} %get-tuple-element.24), channel_id=1, replica_groups=mesh['yh'=2,'g'=32,'h'=2,'f'=4] {'yh','h','f'}, dimensions={0} | all-to-all | bytes 262144 | tf_op jit(solution)/shard_map/all_to_all | solution.py:468
  109.0 0.0 copy-done.1
  109.0 2.0 %last.1 = bf16[4,4,32,512]{3,2,1,0:T(8,128)(2,1)S(1)} custom-call(f32[2,3,8,32,512]{4,3,2,1,0:T(8,128)S(1)} %get-tuple-element.23.x_ref, f32[16,16,128]{2,1,0:T(8,128)S(1)} %all_to_all.21.parts_ref, s32[128]{0:T(128)S(1)} %copy-done.2, bf16[1,512,512]{2,1,0:T(8,128)(2,1)S(1)} %copy-done.1), custom_call_target="tpu_custom_call" | custom-call | tf_op jit(solution)/shard_map/last/pallas_call | solution.py:469
  111.0 18.5 %all_to_all.22.in_ref = bf16[4,4,32,512]{3,2,1,0:T(8,128)(2,1)S(1)} all-to-all(bf16[4,4,32,512]{3,2,1,0:T(8,128)(2,1)S(1)} %last.1), channel_id=1, replica_groups=mesh['yh'=2,'g'=32,'h'=2,'f'=4] {'yh','h'}, dimensions={0} | all-to-all | bytes 1048576 | tf_op jit(solution)/shard_map/all_to_all | solution.py:476
  129.5 0.8 unpack.1
Async XLA Ops:
  0.0 39.7 %copy-start = (bf16[2,512,512]{2,1,0:T(8,128)(2,1)S(1)}, bf16[2,512,512]{2,1,0:T(8,128)(2,1)}, u32[]{:S(2)}) copy-start(bf16[2,512,512]{2,1,0:T(8,128)(2,1)} %constant.4.clone.table_ref) | copy-start | bytes 3145732
  39.7 50.5 %copy-start.2 = (s32[128]{0:T(128)S(1)}, s32[128]{0:T(128)}, u32[]{:S(2)}) copy-start(s32[128]{0:T(128)} %levels_ref.3) | copy-start | bytes 1540
  42.1 22.5 %collective-permute-start.1 = (bf16[2,2,4,32,512]{4,3,2,1,0:T(8,128)(2,1)S(1)}, bf16[2,2,4,32,512]{4,3,2,1,0:T(8,128)(2,1)S(1)}, u32[]{:S(2)}, u32[]{:S(2)}) collective-permute-start(bf16[2,2,4,32,512]{4,3,2,1,0:T(8,128)(2,1)S(1)} %get-tuple-element.16), channel_id=1, source_target_pairs={{0,248},{8,0},{16,8},{24,16},{32,24},{40,32},{48,40},{56,48},{64,5... | collective-permute-start | bytes 1572872 | tf_op jit(solution)/shard_map/ppermute | solution.py:444
  54.4 16.2 %collective-permute-start = (bf16[2,2,4,32,512]{4,3,2,1,0:T(8,128)(2,1)S(1)}, bf16[2,2,4,32,512]{4,3,2,1,0:T(8,128)(2,1)S(1)}, u32[]{:S(2)}, u32[]{:S(2)}) collective-permute-start(bf16[2,2,4,32,512]{4,3,2,1,0:T(8,128)(2,1)S(1)} %get-tuple-element.16), channel_id=1, source_target_pairs={{0,8},{8,16},{16,24},{24,32},{32,40},{40,48},{48,56},{56,64},{64,7... | collective-permute-start | bytes 1572872 | tf_op jit(solution)/shard_map/ppermute | solution.py:445
  56.3 23.7 %collective-permute-start.3 = (bf16[2,144,512]{2,1,0:T(8,128)(2,1)}, bf16[2,144,512]{2,1,0:T(8,128)(2,1)}, u32[]{:S(2)}, u32[]{:S(2)}) collective-permute-start(bf16[2,144,512]{2,1,0:T(8,128)(2,1)} %get-tuple-element.19.b_even_ref), channel_id=1, source_target_pairs={{0,248},{8,0},{16,8},{24,16},{32,24},{40,32},{48,40},{56,48},{64,5... | collective-permute-start | bytes 884744 | tf_op jit(solution)/shard_map/ppermute | solution.py:446
  61.8 18.3 %collective-permute-start.2 = (bf16[2,144,512]{2,1,0:T(8,128)(2,1)}, bf16[2,144,512]{2,1,0:T(8,128)(2,1)}, u32[]{:S(2)}, u32[]{:S(2)}) collective-permute-start(bf16[2,144,512]{2,1,0:T(8,128)(2,1)} %get-tuple-element.20.b_odd_ref), channel_id=1, source_target_pairs={{0,8},{8,16},{16,24},{24,32},{32,40},{40,48},{48,56},{56,64},{64,7... | collective-permute-start | bytes 884744 | tf_op jit(solution)/shard_map/ppermute | solution.py:447
  72.8 17.3 %all-to-all-start.1 = ((f32[16,16,128]{2,1,0:T(8,128)}), f32[16,16,128]{2,1,0:T(8,128)S(1)}, u32[]{:S(2)}, u32[]{:S(2)}) async-start(f32[16,16,128]{2,1,0:T(8,128)} %get-tuple-element.18), calls=%async_computation.1 | async-start | bytes 262144 | tf_op jit(solution)/shard_map/all_to_all | solution.py:454
  90.2 18.8 %copy-start.1 = (bf16[1,512,512]{2,1,0:T(8,128)(2,1)S(1)}, bf16[1,512,512]{2,1,0:T(8,128)(2,1)}, u32[]{:S(2)}) copy-start(bf16[1,512,512]{2,1,0:T(8,128)(2,1)} %constant.5.clone.table_ref) | copy-start | bytes 1572868

commit v4 on v3

--- a/solution.py
+++ b/solution.py
@@ -47,35 +47,32 @@
     return (a[0] - b[0], a[1] - b[1])
 
 
-def turn(a, sign):
-    return (a[1], -a[0]) if sign > 0 else (-a[1], a[0])
-
-
-def twist(a, power, sign):
-    if power == 0:
-        return a
-    if power == 2:
-        return turn(a, sign)
+def add_turned(a, b, sign):
+    return (a[0] + b[1], a[1] - b[0]) if sign > 0 else (a[0] - b[1], a[1] + b[0])
+
+
+def eighth(a, sign):
     re, im = a
     if sign > 0:
-        one = ((re + im) * HALF_ROOT, (im - re) * HALF_ROOT)
-    else:
-        one = ((re - im) * HALF_ROOT, (im + re) * HALF_ROOT)
-    return one if power == 1 else turn(one, sign)
+        return ((re + im) * HALF_ROOT, (im - re) * HALF_ROOT)
+    return ((re - im) * HALF_ROOT, (im + re) * HALF_ROOT)
 
 
 def dft4(a, b, c, d, sign):
-    s0, s1, s2, s3 = add(a, c), sub(a, c), add(b, d), turn(sub(b, d), sign)
-    return [add(s0, s2), add(s1, s3), sub(s0, s2), sub(s1, s3)]
+    s0, s1, s2, s3 = add(a, c), sub(a, c), add(b, d), sub(b, d)
+    return [add(s0, s2), add_turned(s1, s3, sign), sub(s0, s2), add_turned(s1, s3, -sign)]
 
 
 def dft8(x, sign, part="both"):
     even = dft4(x[0], x[2], x[4], x[6], sign)
     odd = dft4(x[1], x[3], x[5], x[7], sign)
-    odd = [twist(odd[k], k, sign) for k in range(4)]
-    first = [add(even[k], odd[k]) for k in range(4)] if part != "second" else []
-    second = [sub(even[k], odd[k]) for k in range(4)] if part != "first" else []
-    return first + second
+    one, three = eighth(odd[1], sign), eighth(odd[3], sign)
+    out = []
+    if part != "second":
+        out += [add(even[0], odd[0]), add(even[1], one), add_turned(even[2], odd[2], sign), add_turned(even[3], three, sign)]
+    if part != "first":
+        out += [sub(even[0], odd[0]), sub(even[1], one), add_turned(even[2], odd[2], -sign), add_turned(even[3], three, -sign)]
+    return out
 
 
 def windowed(first, second, scale):
@@ -245,14 +242,16 @@
 
 def relax(e_ref, ab, k, rows, b_of, meta_of, phase, column, emit):
     q = e_ref.shape[4] // 2
-    for t in range(SHOTS_DEV):
-        slot = jnp.broadcast_to(meta_of(t), (16, 128))
-        cos, sin = [jnp.broadcast_to(table[:, column + t : column + t + 1], (16, 128)) for table in phase]
-        for half in range(q // 128):
-            spans = (slice(half * 128, half * 128 + 128), slice(q + half * 128, q + half * 128 + 128))
-            other = [e_ref[1 - ab, k, 0, rows, span] for span in spans]
+    slots = [jnp.broadcast_to(meta_of(t), (16, 128)) for t in range(SHOTS_DEV)]
+    turns = [[jnp.broadcast_to(table[:, column + t : column + t + 1], (16, 128)) for table in phase] for t in range(SHOTS_DEV)]
+    for half in range(q // 128):
+        spans = (slice(half * 128, half * 128 + 128), slice(q + half * 128, q + half * 128 + 128))
+        others = [[e_ref[1 - ab, k, j, rows, span] for span in spans] for j in range(SHOTS_DEV)]
+        for t in range(SHOTS_DEV):
+            cos, sin = turns[t]
+            other = others[0]
             for j in range(1, SHOTS_DEV):
-                other = [jnp.where(slot == j, e_ref[1 - ab, k, j, rows, span], o) for o, span in zip(other, spans)]
+                other = [jnp.where(slots[t] == j, new, old) for old, new in zip(other, others[j])]
             shifted = (other[0] * cos + other[1] * sin, other[1] * cos - other[0] * sin)
             for span, shift in zip(spans, shifted):
                 emit(t, span, RELAX * ((e_ref[ab, k, t, rows, span] + b_of(t, span)) - shift))
@@ -263,12 +262,13 @@
     high, low = table_ref[0], table_ref[1]
     slabs = 2 * SHOTS_DEV
     metas = []
+    data = [in_ref[:, c * slabs : (c + 1) * slabs].reshape(ROLES * slabs * fl, 128) for c in range(q2 // 128)]
+    data = jnp.concatenate(data, axis=1)
+    both = jnp.dot(data, high, preferred_element_type=f32) + jnp.dot(data, low, preferred_element_type=f32)
+    both = both.reshape(ROLES, 2, SHOTS_DEV, fl, q2)
     for src in range(ROLES):
         ab, p = src // 2, src % 2
-        data = [in_ref[src, c * slabs : (c + 1) * slabs].reshape(slabs * fl, 128) for c in range(q2 // 128)]
-        data = jnp.concatenate(data, axis=1)
-        out = jnp.dot(data, high, preferred_element_type=f32) + jnp.dot(data, low, preferred_element_type=f32)
-        out = out.reshape(2, SHOTS_DEV, fl, q2)
+        out = both[src]
         e_ref[ab, p] = out[0]
         bh_ref[ab, p] = out[1]
         raw = in_ref[src, slabs * (q2 // 128), :16, :]
@@ -305,17 +305,22 @@
     lax.fori_loop(0, fl // 16, body, 0)
 
 
-def wide_sums_kernel(n, z_ref, up_ref, down_ref, out_ref, halo_ref):
+def fetch_halo(n, up_ref, down_ref, halo_ref):
     g = lax.axis_index("g")
     for ab in range(2):
         halo_ref[0, ab] = up_ref[jnp.where(g == 0, 1 - ab, ab)].astype(f32)
         halo_ref[1, ab] = down_ref[jnp.where(g == n - 1, 1 - ab, ab)].astype(f32)
+
+
+def wide_sums_kernel(n, z_ref, up_ref, down_ref, out_ref, halo_ref):
+    fetch_halo(n, up_ref, down_ref, halo_ref)
     add_sums(n, z_ref, halo_ref, out_ref, True)
 
 
-def middle_kernel(n, size, z_ref, halo_ref, parts_ref, levels_ref, b_even_ref, b_odd_ref, meta_ref, phase_ref,
-                  b_up_ref, b_down_ref, x_out, parts_out, e_ref, far_meta_ref, far_ref, z2_ref, halo2_ref):
+def middle_kernel(n, size, z_ref, up_ref, down_ref, parts_ref, levels_ref, b_even_ref, b_odd_ref, meta_ref, phase_ref,
+                  b_up_ref, b_down_ref, x_out, parts_out, e_ref, far_meta_ref, far_ref, z2_ref, halo2_ref, halo_ref):
     fl, q = z_ref.shape[3], z_ref.shape[4] // 2
+    fetch_halo(n, up_ref, down_ref, halo_ref)
     g = lax.axis_index("g")
     marks = seams(n)
 
@@ -445,26 +450,23 @@
     up = lax.ppermute(zs, "g", after)
     b_down = lax.ppermute(b_even, "g", before)
     b_up = lax.ppermute(b_odd, "g", after)
-    parts, halo = call(
-        functools.partial(wide_sums_kernel, n),
-        "wide_sums",
-        (parts_shape, shape((2, 2, 2, *block), f32)),
-        [VMEM] * 3,
-    )(z, up, down)
+    far = pltpu.VMEM((2, 2, 2, *block), f32)
+    parts = call(functools.partial(wide_sums_kernel, n), "wide_sums", parts_shape, [VMEM] * 3, [far])(z, up, down)
     parts = lax.all_to_all(parts, SUM_GROUP, 0, 0, tiled=True)
     x, parts = call(
         functools.partial(middle_kernel, n, size),
         "middle",
         (shape((2, 3, 8, fl, 2 * q), f32), parts_shape),
-        [VMEM] * 3 + [SMEM] + [VMEM] * 6,
+        [VMEM] * 4 + [SMEM] + [VMEM] * 6,
         [
             pltpu.VMEM((2, 4, *block), f32),
             pltpu.VMEM((ROLES, 16, 128), f32),
             pltpu.VMEM((2, fl, 128), f32),
             pltpu.VMEM((2, 2, *block), f32),
             pltpu.VMEM((2, 2, 1, *block), f32),
+            far,
         ],
-    )(z, halo, parts, levels, b_even, b_odd, meta, phase, b_up, b_down)
+    )(z, up, down, parts, levels, b_even, b_odd, meta, phase, b_up, b_down)
     parts = lax.all_to_all(parts, SUM_GROUP, 0, 0, tiled=True)
     out = call(
         functools.partial(last_kernel, n, size),

time: 131 us -> 129 us (0.985)
  Pallas kernels: 14.8 us -> 13 us
where the time goes in v4:
time: 129 us
  blocking collectives  69.7 us (54%)
  starting transfers between devices  28.9 us (22%)
  waiting for transfers between devices  16.9 us (13%)
  Pallas kernels  13 us (10%)
    all_to_all x1, blocking collectives, on_device(): gathered = lax.all_to_all(packed, GROUP, 0, 0, tiled=True)  38.2 us
    all_to_all x1, blocking collectives, on_device(): out = lax.all_to_all(out, GROUP, 0, 0, tiled=True)  18.3 us
    all_to_all x1, blocking collectives, on_device(): parts = lax.all_to_all(parts, SUM_GROUP, 0, 0, tiled=True)  13.2 us
    ppermute x1, starting transfers between devices, on_device(): down = lax.ppermute(zs, 'g', before)  12.3 us
    all_to_all x1, waiting for transfers between devices, on_device(): parts = lax.all_to_all(parts, SUM_GROUP, 0, 0, tiled=True)  10.1 us
    all_to_all x1, starting transfers between devices, on_device(): parts = lax.all_to_all(parts, SUM_GROUP, 0, 0, tiled=True)  7.24 us
    ppermute x1, waiting for transfers between devices, on_device(): up = lax.ppermute(zs, 'g', after)  5.95 us
    ppermute x1, starting transfers between devices, on_device(): b_down = lax.ppermute(b_even, 'g', before)  5.47 us
  transfers between devices with their start and end apart: 5, of which 3 were waited for; matrix products, arithmetic and copies ran while one was open for 0% of the time, Pallas kernels for 2%

profile of v4, /device:TPU:17, one launch (start us, length us, event | category | flops | bytes accessed | tf_op | source)
XLA Modules:
  0.0 128.6 jit_solution(15487118684319528248)
XLA Ops:
  0.0 1.5 %pack.1 = bf16[4,33,32,128]{3,2,1,0:T(8,128)(2,1)S(1)} custom-call(bf16[2,4,128,256]{3,2,1,0:T(8,128)(2,1)} %e_ref.1, bf16[2,4,128,256]{3,2,1,0:T(8,128)(2,1)} %b_ref.1, s32[4]{0:T(128)} %partner_ref.1, s32[512]{0:T(512)} %delays_ref.1), custom_call_target="tpu_custom_call" | custom-call | tf_op jit(solution)/shard_map/pack/pallas_call | solution.py:422
  1.5 0.0 copy-start
  1.5 38.2 %all_to_all.20.in_ref = bf16[4,33,32,128]{3,2,1,0:T(8,128)(2,1)S(1)} all-to-all(bf16[4,33,32,128]{3,2,1,0:T(8,128)(2,1)S(1)} %pack.1), channel_id=1, replica_groups=mesh['yh'=2,'g'=32,'h'=2,'f'=4] {'yh','h'}, dimensions={0} | all-to-all | bytes 2162688 | tf_op jit(solution)/shard_map/all_to_all | solution.py:434
  39.7 0.0 copy-done
  39.7 1.7 %first.1 = (f32[2,2,4,32,512]{4,3,2,1,0:T(8,128)S(1)}, f32[4,16,128]{2,1,0:T(8,128)S(1)}, f32[2,32,128]{2,1,0:T(8,128)S(1)}, bf16[2,2,4,32,512]{4,3,2,1,0:T(8,12...) custom-call(bf16[4,33,32,128]{3,2,1,0:T(8,128)(2,1)S(1)} %all_to_all.20.in_ref, ...), custom_call_target="tpu_custom_call" | custom-call | tf_op jit(solution)/shard_map/first/pallas_call | solution.py:435
  41.4 12.3 %collective-permute-start.1 = (bf16[2,2,4,32,512]{4,3,2,1,0:T(8,128)(2,1)S(1)}, bf16[2,2,4,32,512]{4,3,2,1,0:T(8,128)(2,1)S(1)}, u32[]{:S(2)}, u32[]{:S(2)}) collective-permute-start(bf16[2,2,4,32,512]{4,3,2,1,0:T(8,128)(2,1)S(1)} %get-tuple-element.14), channel_id=1, source_target_pairs={{0,248},{8,0},{16,8},{24,16},{32,24},{40,32},{48,40},{56,48},{64,5... | collective-permute-start | bytes 1572872 | tf_op jit(solution)/shard_map/ppermute | solution.py:449
  53.7 1.9 %collective-permute-start = (bf16[2,2,4,32,512]{4,3,2,1,0:T(8,128)(2,1)S(1)}, bf16[2,2,4,32,512]{4,3,2,1,0:T(8,128)(2,1)S(1)}, u32[]{:S(2)}, u32[]{:S(2)}) collective-permute-start(bf16[2,2,4,32,512]{4,3,2,1,0:T(8,128)(2,1)S(1)} %get-tuple-element.14), channel_id=1, source_target_pairs={{0,8},{8,16},{16,24},{24,32},{32,40},{40,48},{48,56},{56,64},{64,7... | collective-permute-start | bytes 1572872 | tf_op jit(solution)/shard_map/ppermute | solution.py:450
  55.7 5.5 %collective-permute-start.3 = (bf16[2,144,512]{2,1,0:T(8,128)(2,1)S(1)}, bf16[2,144,512]{2,1,0:T(8,128)(2,1)S(1)}, u32[]{:S(2)}, u32[]{:S(2)}) collective-permute-start(bf16[2,144,512]{2,1,0:T(8,128)(2,1)S(1)} %get-tuple-element.15.b_even_ref), channel_id=1, source_target_pairs={{0,248},{8,0},{16,8},{24,16},{32,24},{40,32},{48,40},{56,48},{64,5... | collective-permute-start | bytes 884744 | tf_op jit(solution)/shard_map/ppermute | solution.py:451
  61.1 1.9 %collective-permute-start.2 = (bf16[2,144,512]{2,1,0:T(8,128)(2,1)S(1)}, bf16[2,144,512]{2,1,0:T(8,128)(2,1)S(1)}, u32[]{:S(2)}, u32[]{:S(2)}) collective-permute-start(bf16[2,144,512]{2,1,0:T(8,128)(2,1)S(1)} %get-tuple-element.16.b_odd_ref), channel_id=1, source_target_pairs={{0,8},{8,16},{16,24},{24,32},{32,40},{40,48},{48,56},{56,64},{64,7... | collective-permute-start | bytes 884744 | tf_op jit(solution)/shard_map/ppermute | solution.py:452
  63.1 0.9 collective-permute-done.1.down_ref
  64.0 5.9 %collective-permute-done.up_ref = bf16[2,2,4,32,512]{4,3,2,1,0:T(8,128)(2,1)S(1)} collective-permute-done((bf16[2,2,4,32,512]{4,3,2,1,0:T(8,128)(2,1)S(1)}, bf16[2,2,4,32,512]{4,3,2,1,0:T(8,128)(2,1)S(1)}, u32[]{:S(2)}, u32[]{:S(2)}) %collective-permute-start) | collective-permute-done | bytes 524320 | tf_op jit(solution)/shard_map/ppermute | solution.py:450
  69.9 0.0 copy-start.2
  69.9 2.2 %wide_sums.1 = f32[16,16,128]{2,1,0:T(8,128)} custom-call(f32[2,2,4,32,512]{4,3,2,1,0:T(8,128)S(1)} %get-tuple-element.13.z_ref, bf16[2,2,4,32,512]{4,3,2,1,0:T(8,128)(2,1)S(1)} %collective-permute-done.up_ref, bf16[2,2,4,32,512]{4,3,2,1,0:T(8,128)(2,1)S(1)} %collective-permute-done.1.down_ref), custom_call_target="tpu_custom_call" | custom-call | tf_op jit(solution)/shard_map/wide_sums/pallas_call | solution.py:454
  72.1 7.2 %all-to-all-start.1 = ((f32[16,16,128]{2,1,0:T(8,128)}), f32[16,16,128]{2,1,0:T(8,128)S(1)}, u32[]{:S(2)}, u32[]{:S(2)}) async-start(f32[16,16,128]{2,1,0:T(8,128)} %wide_sums.1), calls=%async_computation.1 | async-start | bytes 262144 | tf_op jit(solution)/shard_map/all_to_all | solution.py:455
  79.4 0.0 collective-permute-done.3.b_down_ref
  79.4 0.0 collective-permute-done.2.b_up_ref
  79.4 10.1 %all-to-all-done.1.parts_ref = f32[16,16,128]{2,1,0:T(8,128)S(1)} async-done(((f32[16,16,128]{2,1,0:T(8,128)}), f32[16,16,128]{2,1,0:T(8,128)S(1)}, u32[]{:S(2)}, u32[]{:S(2)}) %all-to-all-start.1) | async-done | bytes 131104 | tf_op jit(solution)/shard_map/all_to_all | solution.py:455
  89.5 0.0 copy-done.2
  89.5 0.0 copy-start.1
  89.5 4.7 %middle.1 = (f32[2,3,8,32,512]{4,3,2,1,0:T(8,128)S(1)}, f32[16,16,128]{2,1,0:T(8,128)S(1)}) custom-call(f32[2,2,4,32,512]{4,3,2,1,0:T(8,128)S(1)} %get-tuple-element.13.z_ref, bf16[2,2,4,32,512]{4,3,2,1,0:T(8,128)(2,1)S(1)} %collective-permute-done.up_ref, bf16[2,2,4,32,512]{4,3,2,1,0:T(8,128)(2,1)S(1)} %collective-permute-done.1.down_ref, ...), custom_call_target="tpu_custom_call" | custom-call | tf_op jit(solution)/shard_map/middle/pallas_call | solution.py:456
  94.2 13.2 %all_to_all.21.parts_ref = f32[16,16,128]{2,1,0:T(8,128)S(1)} all-to-all(f32[16,16,128]{2,1,0:T(8,128)S(1)} %get-tuple-element.20), channel_id=1, replica_groups=mesh['yh'=2,'g'=32,'h'=2,'f'=4] {'yh','h','f'}, dimensions={0} | all-to-all | bytes 262144 | tf_op jit(solution)/shard_map/all_to_all | solution.py:470
  107.4 0.0 copy-done.1
  107.4 2.0 %last.1 = bf16[4,4,32,512]{3,2,1,0:T(8,128)(2,1)S(1)} custom-call(f32[2,3,8,32,512]{4,3,2,1,0:T(8,128)S(1)} %get-tuple-element.19.x_ref, f32[16,16,128]{2,1,0:T(8,128)S(1)} %all_to_all.21.parts_ref, s32[128]{0:T(128)S(1)} %copy-done.2, bf16[1,512,512]{2,1,0:T(8,128)(2,1)S(1)} %copy-done.1), custom_call_target="tpu_custom_call" | custom-call | tf_op jit(solution)/shard_map/last/pallas_call | solution.py:471
  109.5 18.3 %all_to_all.22.in_ref = bf16[4,4,32,512]{3,2,1,0:T(8,128)(2,1)S(1)} all-to-all(bf16[4,4,32,512]{3,2,1,0:T(8,128)(2,1)S(1)} %last.1), channel_id=1, replica_groups=mesh['yh'=2,'g'=32,'h'=2,'f'=4] {'yh','h'}, dimensions={0} | all-to-all | bytes 1048576 | tf_op jit(solution)/shard_map/all_to_all | solution.py:478
  127.7 0.8 unpack.1
Async XLA Ops:
  1.5 38.2 %copy-start = (bf16[2,512,512]{2,1,0:T(8,128)(2,1)S(1)}, bf16[2,512,512]{2,1,0:T(8,128)(2,1)}, u32[]{:S(2)}) copy-start(bf16[2,512,512]{2,1,0:T(8,128)(2,1)} %constant.4.clone.table_ref) | copy-start | bytes 3145732
  41.4 22.5 %collective-permute-start.1 = (bf16[2,2,4,32,512]{4,3,2,1,0:T(8,128)(2,1)S(1)}, bf16[2,2,4,32,512]{4,3,2,1,0:T(8,128)(2,1)S(1)}, u32[]{:S(2)}, u32[]{:S(2)}) collective-permute-start(bf16[2,2,4,32,512]{4,3,2,1,0:T(8,128)(2,1)S(1)} %get-tuple-element.14), channel_id=1, source_target_pairs={{0,248},{8,0},{16,8},{24,16},{32,24},{40,32},{48,40},{56,48},{64,5... | collective-permute-start | bytes 1572872 | tf_op jit(solution)/shard_map/ppermute | solution.py:449
  53.7 16.2 %collective-permute-start = (bf16[2,2,4,32,512]{4,3,2,1,0:T(8,128)(2,1)S(1)}, bf16[2,2,4,32,512]{4,3,2,1,0:T(8,128)(2,1)S(1)}, u32[]{:S(2)}, u32[]{:S(2)}) collective-permute-start(bf16[2,2,4,32,512]{4,3,2,1,0:T(8,128)(2,1)S(1)} %get-tuple-element.14), channel_id=1, source_target_pairs={{0,8},{8,16},{16,24},{24,32},{32,40},{40,48},{48,56},{56,64},{64,7... | collective-permute-start | bytes 1572872 | tf_op jit(solution)/shard_map/ppermute | solution.py:450
  55.7 23.7 %collective-permute-start.3 = (bf16[2,144,512]{2,1,0:T(8,128)(2,1)S(1)}, bf16[2,144,512]{2,1,0:T(8,128)(2,1)S(1)}, u32[]{:S(2)}, u32[]{:S(2)}) collective-permute-start(bf16[2,144,512]{2,1,0:T(8,128)(2,1)S(1)} %get-tuple-element.15.b_even_ref), channel_id=1, source_target_pairs={{0,248},{8,0},{16,8},{24,16},{32,24},{40,32},{48,40},{56,48},{64,5... | collective-permute-start | bytes 884744 | tf_op jit(solution)/shard_map/ppermute | solution.py:451
  61.1 18.2 %collective-permute-start.2 = (bf16[2,144,512]{2,1,0:T(8,128)(2,1)S(1)}, bf16[2,144,512]{2,1,0:T(8,128)(2,1)S(1)}, u32[]{:S(2)}, u32[]{:S(2)}) collective-permute-start(bf16[2,144,512]{2,1,0:T(8,128)(2,1)S(1)} %get-tuple-element.16.b_odd_ref), channel_id=1, source_target_pairs={{0,8},{8,16},{16,24},{24,32},{32,40},{40,48},{48,56},{56,64},{64,7... | collective-permute-start | bytes 884744 | tf_op jit(solution)/shard_map/ppermute | solution.py:452
  69.9 19.6 %copy-start.2 = (s32[128]{0:T(128)S(1)}, s32[128]{0:T(128)}, u32[]{:S(2)}) copy-start(s32[128]{0:T(128)} %levels_ref.3) | copy-start | bytes 1540
  72.1 17.4 %all-to-all-start.1 = ((f32[16,16,128]{2,1,0:T(8,128)}), f32[16,16,128]{2,1,0:T(8,128)S(1)}, u32[]{:S(2)}, u32[]{:S(2)}) async-start(f32[16,16,128]{2,1,0:T(8,128)} %wide_sums.1), calls=%async_computation.1 | async-start | bytes 262144 | tf_op jit(solution)/shard_map/all_to_all | solution.py:455
  89.5 17.9 %copy-start.1 = (bf16[1,512,512]{2,1,0:T(8,128)(2,1)S(1)}, bf16[1,512,512]{2,1,0:T(8,128)(2,1)}, u32[]{:S(2)}) copy-start(bf16[1,512,512]{2,1,0:T(8,128)(2,1)} %constant.5.clone.table_ref) | copy-start | bytes 1572868

commit v5 on v4

--- a/solution.py
+++ b/solution.py
@@ -19,6 +19,7 @@
 ROOT8 = 1.0 / math.sqrt(8.0)
 HALF_ROOT = math.sqrt(0.5)
 TAPER = [math.sin(math.pi * (t + 0.5) / 8) ** 2 * ROOT8 for t in range(8)]
+STEPS = (0, 2, 3, 1)
 GROUP = ("yh", "h")
 SUM_GROUP = ("yh", "h", "f")
 
@@ -177,7 +178,12 @@
     lax.fori_loop(0, fl // 8, body, 0)
 
 
-def pack_kernel(e_ref, b_ref, partner_ref, delays_ref, out_ref, partner_smem, delays_smem, sems, small_sems):
+def place():
+    return lax.axis_index("yh") * 2 + lax.axis_index("h")
+
+
+def pack_kernel(e_ref, b_ref, partner_ref, delays_ref, *refs):
+    outs, (partner_smem, delays_smem, sems, small_sems) = refs[:ROLES], refs[ROLES:]
     fl = e_ref.shape[2] // ROLES
     columns = e_ref.shape[3] // 128
     small = [
@@ -190,10 +196,11 @@
     for k, ref in enumerate((e_ref, b_ref)):
         for part in range(2):
             for half in range(columns):
-                for role in range(ROLES):
-                    source = ref.at[part, :, pl.ds(role * fl, fl), pl.ds(half * 128, 128)]
+                for step in range(ROLES):
+                    rows = pl.ds(pl.multiple_of((place() ^ step) * fl, fl), fl)
+                    source = ref.at[part, :, rows, pl.ds(half * 128, 128)]
                     first = (part * columns + half) * 2 * SHOTS_DEV + k * SHOTS_DEV
-                    target = out_ref.at[role, pl.ds(first, SHOTS_DEV)]
+                    target = outs[step].at[pl.ds(first, SHOTS_DEV)]
                     copies.append(pltpu.make_async_copy(source, target, sems.at[len(copies)]))
                     copies[-1].start()
     for copy in small:
@@ -206,8 +213,8 @@
         offset = (delays_smem[other] - delays_smem[block * SHOTS_DEV + t]) & (NT - 1)
         for i, value in enumerate((other & (SHOTS_DEV - 1), offset >> 5, offset & 31)):
             meta = jnp.where(row == 3 * t + i, value.astype(f32), meta)
-    for role in range(ROLES):
-        out_ref[role, 4 * SHOTS_DEV * columns] = meta.astype(bf16)
+    for out_ref in outs:
+        out_ref[4 * SHOTS_DEV * columns] = meta.astype(bf16)
     for copy in copies:
         copy.wait()
 
@@ -257,7 +264,13 @@
                 emit(t, span, RELAX * ((e_ref[ab, k, t, rows, span] + b_of(t, span)) - shift))
 
 
-def first_kernel(in_ref, table_ref, z_ref, meta_ref, phase_ref, zs_ref, b_even_ref, b_odd_ref, e_ref, bh_ref):
+def first_kernel(own_ref, y_ref, yh_ref, h_ref, table_hbm, z_ref, meta_ref, phase_ref, zs_ref, b_even_ref, b_odd_ref,
+                 e_ref, bh_ref, in_ref, table_ref, table_sem):
+    tables = pltpu.make_async_copy(table_hbm, table_ref, table_sem)
+    tables.start()
+    for step, ref in zip(STEPS, (own_ref, y_ref, yh_ref, h_ref)):
+        in_ref[place() ^ step] = ref[...]
+    tables.wait()
     fl, q2 = in_ref.shape[2], table_ref.shape[1]
     high, low = table_ref[0], table_ref[1]
     slabs = 2 * SHOTS_DEV
@@ -422,7 +435,7 @@
     packed = call(
         pack_kernel,
         "pack",
-        shape((ROLES, slabs + 1, fl, 128), bf16),
+        (shape((slabs + 1, fl, 128), bf16),) * ROLES,
         [HBM] * 4,
         [
             pltpu.SMEM(partner.shape, jnp.int32),
@@ -431,7 +444,9 @@
             pltpu.SemaphoreType.DMA((2,)),
         ],
     )(*[pltpu.with_memory_space_constraint(x, pltpu.HBM) for x in (estimate, blended, partner, delays)])
-    gathered = lax.all_to_all(packed, GROUP, 0, 0, tiled=True)
+    gathered = {0: packed[0]}
+    for step in STEPS[1:]:
+        gathered[step] = lax.ppermute(packed[step], GROUP, [(i, i ^ step) for i in range(ROLES)])
     z, meta, phase, zs, b_even, b_odd = call(
         first_kernel,
         "first",
@@ -443,9 +458,15 @@
             side,
             side,
         ),
-        [VMEM, VMEM],
-        [pltpu.VMEM((2, 2, *block), f32)] * 2,
-    )(gathered, jnp.asarray(forward))
+        [VMEM] * 4 + [HBM],
+        [
+            pltpu.VMEM((2, 2, *block), f32),
+            pltpu.VMEM((2, 2, *block), f32),
+            pltpu.VMEM((ROLES, slabs + 1, fl, 128), bf16),
+            pltpu.VMEM(forward.shape, bf16),
+            pltpu.SemaphoreType.DMA,
+        ],
+    )(*gathered.values(), pltpu.with_memory_space_constraint(jnp.asarray(forward), pltpu.HBM))
     down = lax.ppermute(zs, "g", before)
     up = lax.ppermute(zs, "g", after)
     b_down = lax.ppermute(b_even, "g", before)

time: 129 us -> 133 us (1.031)
  the two profiles are of different devices: /device:TPU:17 before, /device:TPU:9 now
where the time goes in v5:
time: 133 us; the launch traced here: 132 us
  starting transfers between devices  48.3 us (36%)
  waiting for transfers between devices  34.7 us (26%)
  blocking collectives  34.2 us (26%)
  Pallas kernels  14.8 us (11%)
    all_to_all x1, blocking collectives, on_device(): out = lax.all_to_all(out, GROUP, 0, 0, tiled=True)  21.1 us
    ppermute x3, waiting for transfers between devices, on_device(): lax.ppermute(packed[step], GROUP, [(i, i ^ step) for i in range(ROLES)])  18 us
    all_to_all x1, starting transfers between devices, on_device(): parts = lax.all_to_all(parts, SUM_GROUP, 0, 0, tiled=True)  17.6 us
    ppermute x3, starting transfers between devices, on_device(): lax.ppermute(packed[step], GROUP, [(i, i ^ step) for i in range(ROLES)])  13.8 us
    all_to_all x1, blocking collectives, on_device(): parts = lax.all_to_all(parts, SUM_GROUP, 0, 0, tiled=True)  13.1 us
    all_to_all x1, waiting for transfers between devices, on_device(): parts = lax.all_to_all(parts, SUM_GROUP, 0, 0, tiled=True)  11 us
    ppermute x1, starting transfers between devices, on_device(): down = lax.ppermute(zs, 'g', before)  7.55 us
    ppermute x1, waiting for transfers between devices, on_device(): up = lax.ppermute(zs, 'g', after)  5.78 us
  transfers between devices with their start and end apart: 8, of which 4 were waited for; matrix products, arithmetic and copies ran while one was open for 0% of the time, Pallas kernels for 2%

profile of v5, /device:TPU:9, one launch (start us, length us, event | category | flops | bytes accessed | tf_op | source)
XLA Modules:
  0.0 132.1 jit_solution(4139948440828688217)
XLA Ops:
  0.0 0.0 copy-start.1
  0.0 1.5 %pack.1 = (bf16[33,32,128]{2,1,0:T(8,128)(2,1)S(1)}, bf16[33,32,128]{2,1,0:T(8,128)(2,1)S(1)}, bf16[33,32,128]{2,1,0:T(8,128)(2,1)S(1)}, bf16[33,32,128]{2,1,0:T(8,128)(2,1)S(1)}) custom-call(bf16[2,4,128,256]{3,2,1,0:T(8,128)(2,1)} %e_ref.1, bf16[2,4,128,256]{3,2,1,0:T(8,128)(2,1)} %b_ref.1, s32[4]{0:T(128)} %partner_ref.1, s32[512]{0:T(512)} %delays_ref.1), custom_call_target="tpu_custom_call" | custom-call | tf_op jit(solution)/shard_map/pack/pallas_call | solution.py:435
  1.5 6.6 %collective-permute-start = (bf16[33,32,128]{2,1,0:T(8,128)(2,1)S(1)}, bf16[33,32,128]{2,1,0:T(8,128)(2,1)S(1)}, u32[]{:S(2)}, u32[]{:S(2)}) collective-permute-start(bf16[33,32,128]{2,1,0:T(8,128)(2,1)S(1)} %get-tuple-element.18), channel_id=1, source_target_pairs={{0,256},{4,260},{256,0},{260,4},{1,257},{5,261},{257,1},{261,5},{2... | collective-permute-start | bytes 811016 | tf_op jit(solution)/shard_map/ppermute | solution.py:449
  8.1 5.1 %collective-permute-start.1 = (bf16[33,32,128]{2,1,0:T(8,128)(2,1)S(1)}, bf16[33,32,128]{2,1,0:T(8,128)(2,1)S(1)}, u32[]{:S(2)}, u32[]{:S(2)}) collective-permute-start(bf16[33,32,128]{2,1,0:T(8,128)(2,1)S(1)} %get-tuple-element.19), channel_id=1, source_target_pairs={{0,260},{4,256},{256,4},{260,0},{1,261},{5,257},{257,5},{261,1},{2... | collective-permute-start | bytes 811016 | tf_op jit(solution)/shard_map/ppermute | solution.py:449
  13.2 2.1 %collective-permute-start.2 = (bf16[33,32,128]{2,1,0:T(8,128)(2,1)S(1)}, bf16[33,32,128]{2,1,0:T(8,128)(2,1)S(1)}, u32[]{:S(2)}, u32[]{:S(2)}) collective-permute-start(bf16[33,32,128]{2,1,0:T(8,128)(2,1)S(1)} %get-tuple-element.20), channel_id=1, source_target_pairs={{0,4},{4,0},{256,260},{260,256},{1,5},{5,1},{257,261},{261,257},{2... | collective-permute-start | bytes 811016 | tf_op jit(solution)/shard_map/ppermute | solution.py:449
  15.3 4.6 %collective-permute-done.y_ref = bf16[33,32,128]{2,1,0:T(8,128)(2,1)S(1)} collective-permute-done((bf16[33,32,128]{2,1,0:T(8,128)(2,1)S(1)}, bf16[33,32,128]{2,1,0:T(8,128)(2,1)S(1)}, u32[]{:S(2)}, u32[]{:S(2)}) %collective-permute-start) | collective-permute-done | bytes 270368 | tf_op jit(solution)/shard_map/ppermute | solution.py:449
  19.9 13.4 %collective-permute-done.1.yh_ref = bf16[33,32,128]{2,1,0:T(8,128)(2,1)S(1)} collective-permute-done((bf16[33,32,128]{2,1,0:T(8,128)(2,1)S(1)}, bf16[33,32,128]{2,1,0:T(8,128)(2,1)S(1)}, u32[]{:S(2)}, u32[]{:S(2)}) %collective-permute-start.1) | collective-permute-done | bytes 270368 | tf_op jit(solution)/shard_map/ppermute | solution.py:449
  33.3 0.0 collective-permute-done.2.h_ref
  33.3 2.9 %first.1 = (f32[2,2,4,32,512]{4,3,2,1,0:T(8,128)S(1)}, f32[4,16,128]{2,1,0:T(8,128)S(1)}, f32[2,32,128]{2,1,0:T(8,128)S(1)}, bf16[2,2,4,32,512]{4,3,2,1,0:T(8,12...) custom-call(bf16[33,32,128]{2,1,0:T(8,128)(2,1)S(1)} %get-tuple-element.17.own_ref, ...), custom_call_target="tpu_custom_call" | custom-call | tf_op jit(solution)/shard_map/first/pallas_call | solution.py:450
  36.2 0.0 copy-start
  36.2 7.5 %collective-permute-start.4 = (bf16[2,2,4,32,512]{4,3,2,1,0:T(8,128)(2,1)S(1)}, bf16[2,2,4,32,512]{4,3,2,1,0:T(8,128)(2,1)S(1)}, u32[]{:S(2)}, u32[]{:S(2)}) collective-permute-start(bf16[2,2,4,32,512]{4,3,2,1,0:T(8,128)(2,1)S(1)} %get-tuple-element.22), channel_id=1, source_target_pairs={{0,248},{8,0},{16,8},{24,16},{32,24},{40,32},{48,40},{56,48},{64,5... | collective-permute-start | bytes 1572872 | tf_op jit(solution)/shard_map/ppermute | solution.py:470
  43.8 1.9 %collective-permute-start.3 = (bf16[2,2,4,32,512]{4,3,2,1,0:T(8,128)(2,1)S(1)}, bf16[2,2,4,32,512]{4,3,2,1,0:T(8,128)(2,1)S(1)}, u32[]{:S(2)}, u32[]{:S(2)}) collective-permute-start(bf16[2,2,4,32,512]{4,3,2,1,0:T(8,128)(2,1)S(1)} %get-tuple-element.22), channel_id=1, source_target_pairs={{0,8},{8,16},{16,24},{24,32},{32,40},{40,48},{48,56},{56,64},{64,7... | collective-permute-start | bytes 1572872 | tf_op jit(solution)/shard_map/ppermute | solution.py:471
  45.7 5.5 %collective-permute-start.6 = (bf16[2,144,512]{2,1,0:T(8,128)(2,1)S(1)}, bf16[2,144,512]{2,1,0:T(8,128)(2,1)}, u32[]{:S(2)}, u32[]{:S(2)}) collective-permute-start(bf16[2,144,512]{2,1,0:T(8,128)(2,1)S(1)} %get-tuple-element.23.b_even_ref), channel_id=1, source_target_pairs={{0,248},{8,0},{16,8},{24,16},{32,24},{40,32},{48,40},{56,48},{64,5... | collective-permute-start | bytes 884744 | tf_op jit(solution)/shard_map/ppermute | solution.py:472
  51.2 1.9 %collective-permute-start.5 = (bf16[2,144,512]{2,1,0:T(8,128)(2,1)S(1)}, bf16[2,144,512]{2,1,0:T(8,128)(2,1)}, u32[]{:S(2)}, u32[]{:S(2)}) collective-permute-start(bf16[2,144,512]{2,1,0:T(8,128)(2,1)S(1)} %get-tuple-element.24.b_odd_ref), channel_id=1, source_target_pairs={{0,8},{8,16},{16,24},{24,32},{32,40},{40,48},{48,56},{56,64},{64,7... | collective-permute-start | bytes 884744 | tf_op jit(solution)/shard_map/ppermute | solution.py:473
  53.1 0.0 collective-permute-done.4.down_ref
  53.1 5.8 %collective-permute-done.3.up_ref = bf16[2,2,4,32,512]{4,3,2,1,0:T(8,128)(2,1)S(1)} collective-permute-done((bf16[2,2,4,32,512]{4,3,2,1,0:T(8,128)(2,1)S(1)}, bf16[2,2,4,32,512]{4,3,2,1,0:T(8,128)(2,1)S(1)}, u32[]{:S(2)}, u32[]{:S(2)}) %collective-permute-start.3) | collective-permute-done | bytes 524320 | tf_op jit(solution)/shard_map/ppermute | solution.py:471
  58.9 2.2 %wide_sums.1 = f32[16,16,128]{2,1,0:T(8,128)} custom-call(f32[2,2,4,32,512]{4,3,2,1,0:T(8,128)S(1)} %get-tuple-element.21.z_ref, bf16[2,2,4,32,512]{4,3,2,1,0:T(8,128)(2,1)S(1)} %collective-permute-done.3.up_ref, bf16[2,2,4,32,512]{4,3,2,1,0:T(8,128)(2,1)S(1)} %collective-permute-done.4.down_ref), custom_call_target="tpu_custom_call" | custom-call | tf_op jit(solution)/shard_map/wide_sums/pallas_call | solution.py:475
  61.1 17.6 %all-to-all-start = ((f32[16,16,128]{2,1,0:T(8,128)}), f32[16,16,128]{2,1,0:T(8,128)S(1)}, u32[]{:S(2)}, u32[]{:S(2)}) async-start(f32[16,16,128]{2,1,0:T(8,128)} %wide_sums.1), calls=%async_computation | async-start | bytes 262144 | tf_op jit(solution)/shard_map/all_to_all | solution.py:476
  78.8 0.0 collective-permute-done.6.b_down_ref
  78.8 0.0 collective-permute-done.5.b_up_ref
  78.8 11.0 %all-to-all-done.parts_ref = f32[16,16,128]{2,1,0:T(8,128)S(1)} async-done(((f32[16,16,128]{2,1,0:T(8,128)}), f32[16,16,128]{2,1,0:T(8,128)S(1)}, u32[]{:S(2)}, u32[]{:S(2)}) %all-to-all-start) | async-done | bytes 131104 | tf_op jit(solution)/shard_map/all_to_all | solution.py:476
  89.7 0.0 copy-done.1
  89.7 5.3 %middle.1 = (f32[2,3,8,32,512]{4,3,2,1,0:T(8,128)S(1)}, f32[16,16,128]{2,1,0:T(8,128)S(1)}) custom-call(f32[2,2,4,32,512]{4,3,2,1,0:T(8,128)S(1)} %get-tuple-element.21.z_ref, bf16[2,2,4,32,512]{4,3,2,1,0:T(8,128)(2,1)S(1)} %collective-permute-done.3.up_ref, bf16[2,2,4,32,512]{4,3,2,1,0:T(8,128)(2,1)S(1)} %collective-permute-done.4.down_ref, ...), custom_call_target="tpu_custom_call" | custom-call | tf_op jit(solution)/shard_map/middle/pallas_call | solution.py:477
  95.0 13.1 %all_to_all.15.parts_ref = f32[16,16,128]{2,1,0:T(8,128)S(1)} all-to-all(f32[16,16,128]{2,1,0:T(8,128)S(1)} %get-tuple-element.28), channel_id=1, replica_groups=mesh['yh'=2,'g'=32,'h'=2,'f'=4] {'yh','h','f'}, dimensions={0} | all-to-all | bytes 262144 | tf_op jit(solution)/shard_map/all_to_all | solution.py:491
  108.1 0.0 copy-done
  108.1 2.0 %last.1 = bf16[4,4,32,512]{3,2,1,0:T(8,128)(2,1)S(1)} custom-call(f32[2,3,8,32,512]{4,3,2,1,0:T(8,128)S(1)} %get-tuple-element.27.x_ref, f32[16,16,128]{2,1,0:T(8,128)S(1)} %all_to_all.15.parts_ref, s32[128]{0:T(128)S(1)} %copy-done.1, bf16[1,512,512]{2,1,0:T(8,128)(2,1)S(1)} %copy-done), custom_call_target="tpu_custom_call" | custom-call | tf_op jit(solution)/shard_map/last/pallas_call | solution.py:492
  110.1 21.1 %all_to_all.16.in_ref = bf16[4,4,32,512]{3,2,1,0:T(8,128)(2,1)S(1)} all-to-all(bf16[4,4,32,512]{3,2,1,0:T(8,128)(2,1)S(1)} %last.1), channel_id=1, replica_groups=mesh['yh'=2,'g'=32,'h'=2,'f'=4] {'yh','h'}, dimensions={0} | all-to-all | bytes 1048576 | tf_op jit(solution)/shard_map/all_to_all | solution.py:499
  131.3 0.8 unpack.1
Async XLA Ops:
  0.0 89.7 %copy-start.1 = (s32[128]{0:T(128)S(1)}, s32[128]{0:T(128)}, u32[]{:S(2)}) copy-start(s32[128]{0:T(128)} %levels_ref.3) | copy-start | bytes 1540
  1.5 18.4 %collective-permute-start = (bf16[33,32,128]{2,1,0:T(8,128)(2,1)S(1)}, bf16[33,32,128]{2,1,0:T(8,128)(2,1)S(1)}, u32[]{:S(2)}, u32[]{:S(2)}) collective-permute-start(bf16[33,32,128]{2,1,0:T(8,128)(2,1)S(1)} %get-tuple-element.18), channel_id=1, source_target_pairs={{0,256},{4,260},{256,0},{260,4},{1,257},{5,261},{257,1},{261,5},{2... | collective-permute-start | bytes 811016 | tf_op jit(solution)/shard_map/ppermute | solution.py:449
  8.1 25.2 %collective-permute-start.1 = (bf16[33,32,128]{2,1,0:T(8,128)(2,1)S(1)}, bf16[33,32,128]{2,1,0:T(8,128)(2,1)S(1)}, u32[]{:S(2)}, u32[]{:S(2)}) collective-permute-start(bf16[33,32,128]{2,1,0:T(8,128)(2,1)S(1)} %get-tuple-element.19), channel_id=1, source_target_pairs={{0,260},{4,256},{256,4},{260,0},{1,261},{5,257},{257,5},{261,1},{2... | collective-permute-start | bytes 811016 | tf_op jit(solution)/shard_map/ppermute | solution.py:449
  13.2 20.1 %collective-permute-start.2 = (bf16[33,32,128]{2,1,0:T(8,128)(2,1)S(1)}, bf16[33,32,128]{2,1,0:T(8,128)(2,1)S(1)}, u32[]{:S(2)}, u32[]{:S(2)}) collective-permute-start(bf16[33,32,128]{2,1,0:T(8,128)(2,1)S(1)} %get-tuple-element.20), channel_id=1, source_target_pairs={{0,4},{4,0},{256,260},{260,256},{1,5},{5,1},{257,261},{261,257},{2... | collective-permute-start | bytes 811016 | tf_op jit(solution)/shard_map/ppermute | solution.py:449
  36.2 71.9 %copy-start = (bf16[1,512,512]{2,1,0:T(8,128)(2,1)S(1)}, bf16[1,512,512]{2,1,0:T(8,128)(2,1)}, u32[]{:S(2)}) copy-start(bf16[1,512,512]{2,1,0:T(8,128)(2,1)} %constant.5.clone.table_ref) | copy-start | bytes 1572868
  36.2 16.9 %collective-permute-start.4 = (bf16[2,2,4,32,512]{4,3,2,1,0:T(8,128)(2,1)S(1)}, bf16[2,2,4,32,512]{4,3,2,1,0:T(8,128)(2,1)S(1)}, u32[]{:S(2)}, u32[]{:S(2)}) collective-permute-start(bf16[2,2,4,32,512]{4,3,2,1,0:T(8,128)(2,1)S(1)} %get-tuple-element.22), channel_id=1, source_target_pairs={{0,248},{8,0},{16,8},{24,16},{32,24},{40,32},{48,40},{56,48},{64,5... | collective-permute-start | bytes 1572872 | tf_op jit(solution)/shard_map/ppermute | solution.py:470
  43.8 15.1 %collective-permute-start.3 = (bf16[2,2,4,32,512]{4,3,2,1,0:T(8,128)(2,1)S(1)}, bf16[2,2,4,32,512]{4,3,2,1,0:T(8,128)(2,1)S(1)}, u32[]{:S(2)}, u32[]{:S(2)}) collective-permute-start(bf16[2,2,4,32,512]{4,3,2,1,0:T(8,128)(2,1)S(1)} %get-tuple-element.22), channel_id=1, source_target_pairs={{0,8},{8,16},{16,24},{24,32},{32,40},{40,48},{48,56},{56,64},{64,7... | collective-permute-start | bytes 1572872 | tf_op jit(solution)/shard_map/ppermute | solution.py:471
  45.7 33.0 %collective-permute-start.6 = (bf16[2,144,512]{2,1,0:T(8,128)(2,1)S(1)}, bf16[2,144,512]{2,1,0:T(8,128)(2,1)}, u32[]{:S(2)}, u32[]{:S(2)}) collective-permute-start(bf16[2,144,512]{2,1,0:T(8,128)(2,1)S(1)} %get-tuple-element.23.b_even_ref), channel_id=1, source_target_pairs={{0,248},{8,0},{16,8},{24,16},{32,24},{40,32},{48,40},{56,48},{64,5... | collective-permute-start | bytes 884744 | tf_op jit(solution)/shard_map/ppermute | solution.py:472
  51.2 27.6 %collective-permute-start.5 = (bf16[2,144,512]{2,1,0:T(8,128)(2,1)S(1)}, bf16[2,144,512]{2,1,0:T(8,128)(2,1)}, u32[]{:S(2)}, u32[]{:S(2)}) collective-permute-start(bf16[2,144,512]{2,1,0:T(8,128)(2,1)S(1)} %get-tuple-element.24.b_odd_ref), channel_id=1, source_target_pairs={{0,8},{8,16},{16,24},{24,32},{32,40},{40,48},{48,56},{56,64},{64,7... | collective-permute-start | bytes 884744 | tf_op jit(solution)/shard_map/ppermute | solution.py:473
  61.1 28.6 %all-to-all-start = ((f32[16,16,128]{2,1,0:T(8,128)}), f32[16,16,128]{2,1,0:T(8,128)S(1)}, u32[]{:S(2)}, u32[]{:S(2)}) async-start(f32[16,16,128]{2,1,0:T(8,128)} %wide_sums.1), calls=%async_computation | async-start | bytes 262144 | tf_op jit(solution)/shard_map/all_to_all | solution.py:476

commit v6 on v4

--- a/solution.py
+++ b/solution.py
@@ -305,22 +305,34 @@
     lax.fori_loop(0, fl // 16, body, 0)
 
 
-def fetch_halo(n, up_ref, down_ref, halo_ref):
+def fetch_halo(n, up_ref, down_ref, cross_ref, halo_ref):
     g = lax.axis_index("g")
-    for ab in range(2):
-        halo_ref[0, ab] = up_ref[jnp.where(g == 0, 1 - ab, ab)].astype(f32)
-        halo_ref[1, ab] = down_ref[jnp.where(g == n - 1, 1 - ab, ab)].astype(f32)
-
-
-def wide_sums_kernel(n, z_ref, up_ref, down_ref, out_ref, halo_ref):
-    fetch_halo(n, up_ref, down_ref, halo_ref)
+    row = n // 4
+    for side, ref, at_edge, swapped in (
+        (0, up_ref, g % row == 0, g == 0),
+        (1, down_ref, g % row == row - 1, g == n - 1),
+    ):
+
+        @pl.when(jnp.logical_not(at_edge))
+        def _(side=side, ref=ref):
+            for ab in range(2):
+                halo_ref[side, ab] = ref[ab].astype(f32)
+
+        @pl.when(at_edge)
+        def _(side=side, swapped=swapped):
+            for ab in range(2):
+                halo_ref[side, ab] = cross_ref[jnp.where(swapped, 1 - ab, ab)].astype(f32)
+
+
+def wide_sums_kernel(n, z_ref, cross_ref, up_ref, down_ref, out_ref, halo_ref):
+    fetch_halo(n, up_ref, down_ref, cross_ref, halo_ref)
     add_sums(n, z_ref, halo_ref, out_ref, True)
 
 
-def middle_kernel(n, size, z_ref, up_ref, down_ref, parts_ref, levels_ref, b_even_ref, b_odd_ref, meta_ref, phase_ref,
+def middle_kernel(n, size, z_ref, up_ref, down_ref, cross_ref, parts_ref, levels_ref, b_even_ref, b_odd_ref, meta_ref, phase_ref,
                   b_up_ref, b_down_ref, x_out, parts_out, e_ref, far_meta_ref, far_ref, z2_ref, halo2_ref, halo_ref):
     fl, q = z_ref.shape[3], z_ref.shape[4] // 2
-    fetch_halo(n, up_ref, down_ref, halo_ref)
+    fetch_halo(n, up_ref, down_ref, cross_ref, halo_ref)
     g = lax.axis_index("g")
     marks = seams(n)
 
@@ -446,18 +458,20 @@
         [VMEM, VMEM],
         [pltpu.VMEM((2, 2, *block), f32)] * 2,
     )(gathered, jnp.asarray(forward))
-    down = lax.ppermute(zs, "g", before)
-    up = lax.ppermute(zs, "g", after)
+    row = n // 4
+    down = lax.ppermute(zs, "g", [(i, j) for i, j in before if i % row > 0])
+    up = lax.ppermute(zs, "g", [(i, j) for i, j in after if j % row > 0])
+    cross = lax.ppermute(zs, "g", [(i, j) for i, j in before if i % row == 0] + [(i, j) for i, j in after if j % row == 0])
     b_down = lax.ppermute(b_even, "g", before)
     b_up = lax.ppermute(b_odd, "g", after)
     far = pltpu.VMEM((2, 2, 2, *block), f32)
-    parts = call(functools.partial(wide_sums_kernel, n), "wide_sums", parts_shape, [VMEM] * 3, [far])(z, up, down)
+    parts = call(functools.partial(wide_sums_kernel, n), "wide_sums", parts_shape, [VMEM] * 4, [far])(z, cross, up, down)
     parts = lax.all_to_all(parts, SUM_GROUP, 0, 0, tiled=True)
     x, parts = call(
         functools.partial(middle_kernel, n, size),
         "middle",
         (shape((2, 3, 8, fl, 2 * q), f32), parts_shape),
-        [VMEM] * 4 + [SMEM] + [VMEM] * 6,
+        [VMEM] * 5 + [SMEM] + [VMEM] * 6,
         [
             pltpu.VMEM((2, 4, *block), f32),
             pltpu.VMEM((ROLES, 16, 128), f32),
@@ -466,7 +480,7 @@
             pltpu.VMEM((2, 2, 1, *block), f32),
             far,
         ],
-    )(z, up, down, parts, levels, b_even, b_odd, meta, phase, b_up, b_down)
+    )(z, up, down, cross, parts, levels, b_even, b_odd, meta, phase, b_up, b_down)
     parts = lax.all_to_all(parts, SUM_GROUP, 0, 0, tiled=True)
     out = call(
         functools.partial(last_kernel, n, size),

time: 129 us -> 128 us (level)
  the two profiles are of different devices: /device:TPU:17 before, /device:TPU:121 now
where the time goes in v6:
time: 128 us
  blocking collectives  57.7 us (45%)
  starting transfers between devices  45.5 us (36%)
  Pallas kernels  13.7 us (11%)
  waiting for transfers between devices  11 us (9%)
    all_to_all x1, blocking collectives, on_device(): gathered = lax.all_to_all(packed, GROUP, 0, 0, tiled=True)  23.8 us
    ppermute x1, starting transfers between devices, on_device(): down = lax.ppermute(zs, 'g', [(i, j) for i, j in before if i % row > 0])  23 us
    all_to_all x1, blocking collectives, on_device(): out = lax.all_to_all(out, GROUP, 0, 0, tiled=True)  20.7 us
    all_to_all x1, starting transfers between devices, on_device(): parts = lax.all_to_all(parts, SUM_GROUP, 0, 0, tiled=True)  14.5 us
    all_to_all x1, blocking collectives, on_device(): parts = lax.all_to_all(parts, SUM_GROUP, 0, 0, tiled=True)  13.2 us
    pallas_call x1, Pallas kernels, on_device(): call(functools.partial(middle_kernel, n, size), 'middle', (shape((2, 3, 8...  5.43 us
    all_to_all x1, waiting for transfers between devices, on_device(): parts = lax.all_to_all(parts, SUM_GROUP, 0, 0, tiled=True)  5.29 us
    ppermute x1, waiting for transfers between devices, on_device(): up = lax.ppermute(zs, 'g', [(i, j) for i, j in after if j % row > 0])  3.94 us
  transfers between devices with their start and end apart: 6, of which 3 were waited for; matrix products, arithmetic and copies ran while one was open for 0% of the time, Pallas kernels for 2%

profile of v6, /device:TPU:121, one launch (start us, length us, event | category | flops | bytes accessed | tf_op | source)
XLA Modules:
  0.0 128.0 jit_solution(17948878877818447943)
XLA Ops:
  0.0 1.5 %pack.1 = bf16[4,33,32,128]{3,2,1,0:T(8,128)(2,1)S(1)} custom-call(bf16[2,4,128,256]{3,2,1,0:T(8,128)(2,1)} %e_ref.1, bf16[2,4,128,256]{3,2,1,0:T(8,128)(2,1)} %b_ref.1, s32[4]{0:T(128)} %partner_ref.1, s32[512]{0:T(512)} %delays_ref.1), custom_call_target="tpu_custom_call" | custom-call | tf_op jit(solution)/shard_map/pack/pallas_call | solution.py:434
  1.5 0.0 copy-start
  1.5 23.8 %all_to_all.20.in_ref = bf16[4,33,32,128]{3,2,1,0:T(8,128)(2,1)S(1)} all-to-all(bf16[4,33,32,128]{3,2,1,0:T(8,128)(2,1)S(1)} %pack.1), channel_id=1, replica_groups=mesh['yh'=2,'g'=32,'h'=2,'f'=4] {'yh','h'}, dimensions={0} | all-to-all | bytes 2162688 | tf_op jit(solution)/shard_map/all_to_all | solution.py:446
  25.3 0.0 copy-done
  25.3 1.7 %first.1 = (f32[2,2,4,32,512]{4,3,2,1,0:T(8,128)S(1)}, f32[4,16,128]{2,1,0:T(8,128)S(1)}, f32[2,32,128]{2,1,0:T(8,128)S(1)}, bf16[2,2,4,32,512]{4,3,2,1,0:T(8,12...) custom-call(bf16[4,33,32,128]{3,2,1,0:T(8,128)(2,1)S(1)} %all_to_all.20.in_ref, ...), custom_call_target="tpu_custom_call" | custom-call | tf_op jit(solution)/shard_map/first/pallas_call | solution.py:447
  27.0 0.7 collective-permute-start.2
  27.7 23.0 %collective-permute-start.1 = (bf16[2,2,4,32,512]{4,3,2,1,0:T(8,128)(2,1)S(1)}, bf16[2,2,4,32,512]{4,3,2,1,0:T(8,128)(2,1)S(1)}, u32[]{:S(2)}, u32[]{:S(2)}) collective-permute-start(bf16[2,2,4,32,512]{4,3,2,1,0:T(8,128)(2,1)S(1)} %get-tuple-element.14), channel_id=1, source_target_pairs={{8,0},{16,8},{24,16},{32,24},{40,32},{48,40},{56,48},{72,64},{80,7... | collective-permute-start | bytes 1572872 | tf_op jit(solution)/shard_map/ppermute | solution.py:462
  50.7 1.9 %collective-permute-start = (bf16[2,2,4,32,512]{4,3,2,1,0:T(8,128)(2,1)S(1)}, bf16[2,2,4,32,512]{4,3,2,1,0:T(8,128)(2,1)S(1)}, u32[]{:S(2)}, u32[]{:S(2)}) collective-permute-start(bf16[2,2,4,32,512]{4,3,2,1,0:T(8,128)(2,1)S(1)} %get-tuple-element.14), channel_id=1, source_target_pairs={{0,8},{8,16},{16,24},{24,32},{32,40},{40,48},{48,56},{64,72},{72,8... | collective-permute-start | bytes 1572872 | tf_op jit(solution)/shard_map/ppermute | solution.py:463
  52.6 3.4 %collective-permute-start.4 = (bf16[2,144,512]{2,1,0:T(8,128)(2,1)S(1)}, bf16[2,144,512]{2,1,0:T(8,128)(2,1)}, u32[]{:S(2)}, u32[]{:S(2)}) collective-permute-start(bf16[2,144,512]{2,1,0:T(8,128)(2,1)S(1)} %get-tuple-element.15.b_even_ref), channel_id=1, source_target_pairs={{0,248},{8,0},{16,8},{24,16},{32,24},{40,32},{48,40},{56,48},{64,5... | collective-permute-start | bytes 884744 | tf_op jit(solution)/shard_map/ppermute | solution.py:465
  56.0 1.9 %collective-permute-start.3 = (bf16[2,144,512]{2,1,0:T(8,128)(2,1)S(1)}, bf16[2,144,512]{2,1,0:T(8,128)(2,1)}, u32[]{:S(2)}, u32[]{:S(2)}) collective-permute-start(bf16[2,144,512]{2,1,0:T(8,128)(2,1)S(1)} %get-tuple-element.16.b_odd_ref), channel_id=1, source_target_pairs={{0,8},{8,16},{16,24},{24,32},{32,40},{40,48},{48,56},{56,64},{64,7... | collective-permute-start | bytes 884744 | tf_op jit(solution)/shard_map/ppermute | solution.py:466
  58.0 0.0 collective-permute-done.2.cross_ref
  58.0 1.7 %collective-permute-done.1.down_ref = bf16[2,2,4,32,512]{4,3,2,1,0:T(8,128)(2,1)S(1)} collective-permute-done((bf16[2,2,4,32,512]{4,3,2,1,0:T(8,128)(2,1)S(1)}, bf16[2,2,4,32,512]{4,3,2,1,0:T(8,128)(2,1)S(1)}, u32[]{:S(2)}, u32[]{:S(2)}) %collective-permute-start.1) | collective-permute-done | bytes 524320 | tf_op jit(solution)/shard_map/ppermute | solution.py:462
  59.7 3.9 %collective-permute-done.up_ref = bf16[2,2,4,32,512]{4,3,2,1,0:T(8,128)(2,1)S(1)} collective-permute-done((bf16[2,2,4,32,512]{4,3,2,1,0:T(8,128)(2,1)S(1)}, bf16[2,2,4,32,512]{4,3,2,1,0:T(8,128)(2,1)S(1)}, u32[]{:S(2)}, u32[]{:S(2)}) %collective-permute-start) | collective-permute-done | bytes 524320 | tf_op jit(solution)/shard_map/ppermute | solution.py:463
  63.6 0.0 copy-start.2
  63.6 2.2 %wide_sums.1 = f32[16,16,128]{2,1,0:T(8,128)} custom-call(f32[2,2,4,32,512]{4,3,2,1,0:T(8,128)S(1)} %get-tuple-element.13.z_ref, bf16[2,2,4,32,512]{4,3,2,1,0:T(8,128)(2,1)S(1)} %collective-permute-done.2.cross_ref, bf16[2,2,4,32,512]{4,3,2,1,0:T(8,128)(2,1)S(1)} %collective-permute-done.up_ref, bf16[2,2,4,32,512]{4,3,2,1,0:T(8,128)(2,1)S(1)} %collective-permute-done.1.down_ref), custom_call_target="tpu_custom_call" | custom-call | tf_op jit(solution)/shard_map/wide_sums/pallas_call | solution.py:468
  65.9 14.5 %all-to-all-start.1 = ((f32[16,16,128]{2,1,0:T(8,128)}), f32[16,16,128]{2,1,0:T(8,128)S(1)}, u32[]{:S(2)}, u32[]{:S(2)}) async-start(f32[16,16,128]{2,1,0:T(8,128)} %wide_sums.1), calls=%async_computation.1 | async-start | bytes 262144 | tf_op jit(solution)/shard_map/all_to_all | solution.py:469
  80.4 0.0 collective-permute-done.4.b_down_ref
  80.4 0.0 collective-permute-done.3.b_up_ref
  80.4 5.3 %all-to-all-done.1.parts_ref = f32[16,16,128]{2,1,0:T(8,128)S(1)} async-done(((f32[16,16,128]{2,1,0:T(8,128)}), f32[16,16,128]{2,1,0:T(8,128)S(1)}, u32[]{:S(2)}, u32[]{:S(2)}) %all-to-all-start.1) | async-done | bytes 131104 | tf_op jit(solution)/shard_map/all_to_all | solution.py:469
  85.7 0.0 copy-done.2
  85.7 0.0 copy-start.1
  85.7 5.4 %middle.1 = (f32[2,3,8,32,512]{4,3,2,1,0:T(8,128)S(1)}, f32[16,16,128]{2,1,0:T(8,128)S(1)}) custom-call(f32[2,2,4,32,512]{4,3,2,1,0:T(8,128)S(1)} %get-tuple-element.13.z_ref, bf16[2,2,4,32,512]{4,3,2,1,0:T(8,128)(2,1)S(1)} %collective-permute-done.up_ref, bf16[2,2,4,32,512]{4,3,2,1,0:T(8,128)(2,1)S(1)} %collective-permute-done.1.down_ref, ...), custom_call_target="tpu_custom_call" | custom-call | tf_op jit(solution)/shard_map/middle/pallas_call | solution.py:470
  91.2 13.2 %all_to_all.21.parts_ref = f32[16,16,128]{2,1,0:T(8,128)S(1)} all-to-all(f32[16,16,128]{2,1,0:T(8,128)S(1)} %get-tuple-element.20), channel_id=1, replica_groups=mesh['yh'=2,'g'=32,'h'=2,'f'=4] {'yh','h','f'}, dimensions={0} | all-to-all | bytes 262144 | tf_op jit(solution)/shard_map/all_to_all | solution.py:484
  104.4 0.0 copy-done.1
  104.4 2.0 %last.1 = bf16[4,4,32,512]{3,2,1,0:T(8,128)(2,1)S(1)} custom-call(f32[2,3,8,32,512]{4,3,2,1,0:T(8,128)S(1)} %get-tuple-element.19.x_ref, f32[16,16,128]{2,1,0:T(8,128)S(1)} %all_to_all.21.parts_ref, s32[128]{0:T(128)S(1)} %copy-done.2, bf16[1,512,512]{2,1,0:T(8,128)(2,1)S(1)} %copy-done.1), custom_call_target="tpu_custom_call" | custom-call | tf_op jit(solution)/shard_map/last/pallas_call | solution.py:485
  106.4 20.7 %all_to_all.22.in_ref = bf16[4,4,32,512]{3,2,1,0:T(8,128)(2,1)S(1)} all-to-all(bf16[4,4,32,512]{3,2,1,0:T(8,128)(2,1)S(1)} %last.1), channel_id=1, replica_groups=mesh['yh'=2,'g'=32,'h'=2,'f'=4] {'yh','h'}, dimensions={0} | all-to-all | bytes 1048576 | tf_op jit(solution)/shard_map/all_to_all | solution.py:492
  127.1 0.8 unpack.1
Async XLA Ops:
  1.5 23.8 %copy-start = (bf16[2,512,512]{2,1,0:T(8,128)(2,1)S(1)}, bf16[2,512,512]{2,1,0:T(8,128)(2,1)}, u32[]{:S(2)}) copy-start(bf16[2,512,512]{2,1,0:T(8,128)(2,1)} %constant.4.clone.table_ref) | copy-start | bytes 3145732
  27.0 31.0 %collective-permute-start.2 = (bf16[2,2,4,32,512]{4,3,2,1,0:T(8,128)(2,1)S(1)}, bf16[2,2,4,32,512]{4,3,2,1,0:T(8,128)(2,1)S(1)}, u32[]{:S(2)}, u32[]{:S(2)}) collective-permute-start(bf16[2,2,4,32,512]{4,3,2,1,0:T(8,128)(2,1)S(1)} %get-tuple-element.14), channel_id=1, source_target_pairs={{0,248},{64,56},{128,120},{192,184},{56,64},{120,128},{184,192},{2... | collective-permute-start | bytes 1572872 | tf_op jit(solution)/shard_map/ppermute | solution.py:464
  27.7 32.0 %collective-permute-start.1 = (bf16[2,2,4,32,512]{4,3,2,1,0:T(8,128)(2,1)S(1)}, bf16[2,2,4,32,512]{4,3,2,1,0:T(8,128)(2,1)S(1)}, u32[]{:S(2)}, u32[]{:S(2)}) collective-permute-start(bf16[2,2,4,32,512]{4,3,2,1,0:T(8,128)(2,1)S(1)} %get-tuple-element.14), channel_id=1, source_target_pairs={{8,0},{16,8},{24,16},{32,24},{40,32},{48,40},{56,48},{72,64},{80,7... | collective-permute-start | bytes 1572872 | tf_op jit(solution)/shard_map/ppermute | solution.py:462
  50.7 12.9 %collective-permute-start = (bf16[2,2,4,32,512]{4,3,2,1,0:T(8,128)(2,1)S(1)}, bf16[2,2,4,32,512]{4,3,2,1,0:T(8,128)(2,1)S(1)}, u32[]{:S(2)}, u32[]{:S(2)}) collective-permute-start(bf16[2,2,4,32,512]{4,3,2,1,0:T(8,128)(2,1)S(1)} %get-tuple-element.14), channel_id=1, source_target_pairs={{0,8},{8,16},{16,24},{24,32},{32,40},{40,48},{48,56},{64,72},{72,8... | collective-permute-start | bytes 1572872 | tf_op jit(solution)/shard_map/ppermute | solution.py:463
  52.6 27.8 %collective-permute-start.4 = (bf16[2,144,512]{2,1,0:T(8,128)(2,1)S(1)}, bf16[2,144,512]{2,1,0:T(8,128)(2,1)}, u32[]{:S(2)}, u32[]{:S(2)}) collective-permute-start(bf16[2,144,512]{2,1,0:T(8,128)(2,1)S(1)} %get-tuple-element.15.b_even_ref), channel_id=1, source_target_pairs={{0,248},{8,0},{16,8},{24,16},{32,24},{40,32},{48,40},{56,48},{64,5... | collective-permute-start | bytes 884744 | tf_op jit(solution)/shard_map/ppermute | solution.py:465
  56.0 24.4 %collective-permute-start.3 = (bf16[2,144,512]{2,1,0:T(8,128)(2,1)S(1)}, bf16[2,144,512]{2,1,0:T(8,128)(2,1)}, u32[]{:S(2)}, u32[]{:S(2)}) collective-permute-start(bf16[2,144,512]{2,1,0:T(8,128)(2,1)S(1)} %get-tuple-element.16.b_odd_ref), channel_id=1, source_target_pairs={{0,8},{8,16},{16,24},{24,32},{32,40},{40,48},{48,56},{56,64},{64,7... | collective-permute-start | bytes 884744 | tf_op jit(solution)/shard_map/ppermute | solution.py:466
  63.6 22.1 %copy-start.2 = (s32[128]{0:T(128)S(1)}, s32[128]{0:T(128)}, u32[]{:S(2)}) copy-start(s32[128]{0:T(128)} %levels_ref.3) | copy-start | bytes 1540
  65.9 19.8 %all-to-all-start.1 = ((f32[16,16,128]{2,1,0:T(8,128)}), f32[16,16,128]{2,1,0:T(8,128)S(1)}, u32[]{:S(2)}, u32[]{:S(2)}) async-start(f32[16,16,128]{2,1,0:T(8,128)} %wide_sums.1), calls=%async_computation.1 | async-start | bytes 262144 | tf_op jit(solution)/shard_map/all_to_all | solution.py:469
  85.7 18.6 %copy-start.1 = (bf16[1,512,512]{2,1,0:T(8,128)(2,1)S(1)}, bf16[1,512,512]{2,1,0:T(8,128)(2,1)}, u32[]{:S(2)}) copy-start(bf16[1,512,512]{2,1,0:T(8,128)(2,1)} %constant.5.clone.table_ref) | copy-start | bytes 1572868

commit v7 on v6

--- a/solution.py
+++ b/solution.py
@@ -407,14 +407,13 @@
         copy.wait()
 
 
-def call(kernel, name, outs, in_specs, scratch=(), out_specs=None):
+def call(kernel, outs, in_specs, scratch=(), out_specs=None):
     return pl.pallas_call(
         kernel,
         out_shape=outs,
         in_specs=in_specs,
         out_specs=jax.tree.map(lambda _: VMEM, outs) if out_specs is None else out_specs,
         scratch_shapes=list(scratch),
-        name=name,
         compiler_params=pltpu.CompilerParams(vmem_limit_bytes=24 * 1024 * 1024),
     )
 
@@ -433,7 +432,6 @@
     slabs = 2 * SHOTS_DEV * (2 * q // 128)
     packed = call(
         pack_kernel,
-        "pack",
         shape((ROLES, slabs + 1, fl, 128), bf16),
         [HBM] * 4,
         [
@@ -446,7 +444,6 @@
     gathered = lax.all_to_all(packed, GROUP, 0, 0, tiled=True)
     z, meta, phase, zs, b_even, b_odd = call(
         first_kernel,
-        "first",
         (
             shape((2, 2, *block), f32),
             shape((ROLES, 16, 128), f32),
@@ -461,15 +458,15 @@
     row = n // 4
     down = lax.ppermute(zs, "g", [(i, j) for i, j in before if i % row > 0])
     up = lax.ppermute(zs, "g", [(i, j) for i, j in after if j % row > 0])
-    cross = lax.ppermute(zs, "g", [(i, j) for i, j in before if i % row == 0] + [(i, j) for i, j in after if j % row == 0])
+    ends = [(i, j) for i, j in before if i % row == 0] + [(i, j) for i, j in after if j % row == 0]
+    cross = lax.ppermute(zs, "g", ends)
     b_down = lax.ppermute(b_even, "g", before)
     b_up = lax.ppermute(b_odd, "g", after)
     far = pltpu.VMEM((2, 2, 2, *block), f32)
-    parts = call(functools.partial(wide_sums_kernel, n), "wide_sums", parts_shape, [VMEM] * 4, [far])(z, cross, up, down)
+    parts = call(functools.partial(wide_sums_kernel, n), parts_shape, [VMEM] * 4, [far])(z, cross, up, down)
     parts = lax.all_to_all(parts, SUM_GROUP, 0, 0, tiled=True)
     x, parts = call(
         functools.partial(middle_kernel, n, size),
-        "middle",
         (shape((2, 3, 8, fl, 2 * q), f32), parts_shape),
         [VMEM] * 5 + [SMEM] + [VMEM] * 6,
         [
@@ -484,20 +481,12 @@
     parts = lax.all_to_all(parts, SUM_GROUP, 0, 0, tiled=True)
     out = call(
         functools.partial(last_kernel, n, size),
-        "last",
         shape((ROLES, *block), bf16),
         [VMEM] * 2 + [SMEM] + [VMEM],
         [pltpu.VMEM((2, 2, *block), f32)],
     )(x, parts, levels, jnp.asarray(backward[:1]))
     out = lax.all_to_all(out, GROUP, 0, 0, tiled=True)
-    return call(
-        unpack_kernel,
-        "unpack",
-        shape(estimate.shape, bf16),
-        [VMEM],
-        [pltpu.SemaphoreType.DMA((2 * ROLES,))],
-        HBM,
-    )(out)
+    return call(unpack_kernel, shape(estimate.shape, bf16), [VMEM], [pltpu.SemaphoreType.DMA((2 * ROLES,))], HBM)(out)
 
 
 def solution(mesh):

time: 128 us -> 128 us (level)
  no operation moved by 1% of the time
where the time goes in v7:
time: 128 us
  blocking collectives  57.7 us (45%)
  starting transfers between devices  45.5 us (36%)
  Pallas kernels  13.7 us (11%)
  waiting for transfers between devices  11 us (9%)
    all_to_all x1, blocking collectives, on_device(): gathered = lax.all_to_all(packed, GROUP, 0, 0, tiled=True)  23.8 us
    ppermute x1, starting transfers between devices, on_device(): down = lax.ppermute(zs, 'g', [(i, j) for i, j in before if i % row > 0])  23 us
    all_to_all x1, blocking collectives, on_device(): out = lax.all_to_all(out, GROUP, 0, 0, tiled=True)  20.7 us
    all_to_all x1, starting transfers between devices, on_device(): parts = lax.all_to_all(parts, SUM_GROUP, 0, 0, tiled=True)  14.5 us
    all_to_all x1, blocking collectives, on_device(): parts = lax.all_to_all(parts, SUM_GROUP, 0, 0, tiled=True)  13.2 us
    pallas_call x1, Pallas kernels, on_device(): call(functools.partial(middle_kernel, n, size), (shape((2, 3, 8, fl, 2 *...  5.43 us
    all_to_all x1, waiting for transfers between devices, on_device(): parts = lax.all_to_all(parts, SUM_GROUP, 0, 0, tiled=True)  5.29 us
    ppermute x1, waiting for transfers between devices, on_device(): up = lax.ppermute(zs, 'g', [(i, j) for i, j in after if j % row > 0])  3.94 us
  transfers between devices with their start and end apart: 6, of which 3 were waited for; matrix products, arithmetic and copies ran while one was open for 0% of the time, Pallas kernels for 2%

profile of v7, /device:TPU:121, one launch (start us, length us, event | category | flops | bytes accessed | tf_op | source)
XLA Modules:
  0.0 128.0 jit_solution(17948878877818447943)
XLA Ops:
  0.0 1.5 %shard_map.73 = bf16[4,33,32,128]{3,2,1,0:T(8,128)(2,1)S(1)} custom-call(bf16[2,4,128,256]{3,2,1,0:T(8,128)(2,1)} %e_ref.1, bf16[2,4,128,256]{3,2,1,0:T(8,128)(2,1)} %b_ref.1, s32[4]{0:T(128)} %partner_ref.1, s32[512]{0:T(512)} %delays_ref.1), custom_call_target="tpu_custom_call" | custom-call | tf_op jit(solution)/shard_map/pallas_call | solution.py:433
  1.5 0.0 copy-start
  1.5 23.8 %all_to_all.20.in_ref = bf16[4,33,32,128]{3,2,1,0:T(8,128)(2,1)S(1)} all-to-all(bf16[4,33,32,128]{3,2,1,0:T(8,128)(2,1)S(1)} %shard_map.73), channel_id=1, replica_groups=mesh['yh'=2,'g'=32,'h'=2,'f'=4] {'yh','h'}, dimensions={0} | all-to-all | bytes 2162688 | tf_op jit(solution)/shard_map/all_to_all | solution.py:444
  25.3 0.0 copy-done
  25.3 1.7 %shard_map.74 = (f32[2,2,4,32,512]{4,3,2,1,0:T(8,128)S(1)}, f32[4,16,128]{2,1,0:T(8,128)S(1)}, f32[2,32,128]{2,1,0:T(8,128)S(1)}, bf16[2,2,4,32,512]{4,3,2,1,0:T...) custom-call(bf16[4,33,32,128]{3,2,1,0:T(8,128)(2,1)S(1)} %all_to_all.20.in_ref, ...), custom_call_target="tpu_custom_call" | custom-call | tf_op jit(solution)/shard_map/pallas_call | solution.py:445
  27.0 0.7 collective-permute-start.2
  27.7 23.0 %collective-permute-start.1 = (bf16[2,2,4,32,512]{4,3,2,1,0:T(8,128)(2,1)S(1)}, bf16[2,2,4,32,512]{4,3,2,1,0:T(8,128)(2,1)S(1)}, u32[]{:S(2)}, u32[]{:S(2)}) collective-permute-start(bf16[2,2,4,32,512]{4,3,2,1,0:T(8,128)(2,1)S(1)} %get-tuple-element.14), channel_id=1, source_target_pairs={{8,0},{16,8},{24,16},{32,24},{40,32},{48,40},{56,48},{72,64},{80,7... | collective-permute-start | bytes 1572872 | tf_op jit(solution)/shard_map/ppermute | solution.py:459
  50.7 1.9 %collective-permute-start = (bf16[2,2,4,32,512]{4,3,2,1,0:T(8,128)(2,1)S(1)}, bf16[2,2,4,32,512]{4,3,2,1,0:T(8,128)(2,1)S(1)}, u32[]{:S(2)}, u32[]{:S(2)}) collective-permute-start(bf16[2,2,4,32,512]{4,3,2,1,0:T(8,128)(2,1)S(1)} %get-tuple-element.14), channel_id=1, source_target_pairs={{0,8},{8,16},{16,24},{24,32},{32,40},{40,48},{48,56},{64,72},{72,8... | collective-permute-start | bytes 1572872 | tf_op jit(solution)/shard_map/ppermute | solution.py:460
  52.6 3.4 %collective-permute-start.4 = (bf16[2,144,512]{2,1,0:T(8,128)(2,1)S(1)}, bf16[2,144,512]{2,1,0:T(8,128)(2,1)}, u32[]{:S(2)}, u32[]{:S(2)}) collective-permute-start(bf16[2,144,512]{2,1,0:T(8,128)(2,1)S(1)} %get-tuple-element.15.b_even_ref), channel_id=1, source_target_pairs={{0,248},{8,0},{16,8},{24,16},{32,24},{40,32},{48,40},{56,48},{64,5... | collective-permute-start | bytes 884744 | tf_op jit(solution)/shard_map/ppermute | solution.py:463
  56.0 1.9 %collective-permute-start.3 = (bf16[2,144,512]{2,1,0:T(8,128)(2,1)S(1)}, bf16[2,144,512]{2,1,0:T(8,128)(2,1)}, u32[]{:S(2)}, u32[]{:S(2)}) collective-permute-start(bf16[2,144,512]{2,1,0:T(8,128)(2,1)S(1)} %get-tuple-element.16.b_odd_ref), channel_id=1, source_target_pairs={{0,8},{8,16},{16,24},{24,32},{32,40},{40,48},{48,56},{56,64},{64,7... | collective-permute-start | bytes 884744 | tf_op jit(solution)/shard_map/ppermute | solution.py:464
  58.0 0.0 collective-permute-done.2.cross_ref
  58.0 1.7 %collective-permute-done.1.down_ref = bf16[2,2,4,32,512]{4,3,2,1,0:T(8,128)(2,1)S(1)} collective-permute-done((bf16[2,2,4,32,512]{4,3,2,1,0:T(8,128)(2,1)S(1)}, bf16[2,2,4,32,512]{4,3,2,1,0:T(8,128)(2,1)S(1)}, u32[]{:S(2)}, u32[]{:S(2)}) %collective-permute-start.1) | collective-permute-done | bytes 524320 | tf_op jit(solution)/shard_map/ppermute | solution.py:459
  59.7 3.9 %collective-permute-done.up_ref = bf16[2,2,4,32,512]{4,3,2,1,0:T(8,128)(2,1)S(1)} collective-permute-done((bf16[2,2,4,32,512]{4,3,2,1,0:T(8,128)(2,1)S(1)}, bf16[2,2,4,32,512]{4,3,2,1,0:T(8,128)(2,1)S(1)}, u32[]{:S(2)}, u32[]{:S(2)}) %collective-permute-start) | collective-permute-done | bytes 524320 | tf_op jit(solution)/shard_map/ppermute | solution.py:460
  63.6 0.0 copy-start.2
  63.6 2.2 %shard_map.75 = f32[16,16,128]{2,1,0:T(8,128)} custom-call(f32[2,2,4,32,512]{4,3,2,1,0:T(8,128)S(1)} %get-tuple-element.13.z_ref, bf16[2,2,4,32,512]{4,3,2,1,0:T(8,128)(2,1)S(1)} %collective-permute-done.2.cross_ref, bf16[2,2,4,32,512]{4,3,2,1,0:T(8,128)(2,1)S(1)} %collective-permute-done.up_ref, bf16[2,2,4,32,512]{4,3,2,1,0:T(8,128)(2,1)S(1)} %collective-permute-done.1.down_ref), custom_call_target="tpu_custom_call" | custom-call | tf_op jit(solution)/shard_map/pallas_call | solution.py:466
  65.9 14.5 %all-to-all-start.1 = ((f32[16,16,128]{2,1,0:T(8,128)}), f32[16,16,128]{2,1,0:T(8,128)S(1)}, u32[]{:S(2)}, u32[]{:S(2)}) async-start(f32[16,16,128]{2,1,0:T(8,128)} %shard_map.75), calls=%async_computation.1 | async-start | bytes 262144 | tf_op jit(solution)/shard_map/all_to_all | solution.py:467
  80.4 0.0 collective-permute-done.4.b_down_ref
  80.4 0.0 collective-permute-done.3.b_up_ref
  80.4 5.3 %all-to-all-done.1.parts_ref = f32[16,16,128]{2,1,0:T(8,128)S(1)} async-done(((f32[16,16,128]{2,1,0:T(8,128)}), f32[16,16,128]{2,1,0:T(8,128)S(1)}, u32[]{:S(2)}, u32[]{:S(2)}) %all-to-all-start.1) | async-done | bytes 131104 | tf_op jit(solution)/shard_map/all_to_all | solution.py:467
  85.7 0.0 copy-done.2
  85.7 0.0 copy-start.1
  85.7 5.4 %shard_map.76 = (f32[2,3,8,32,512]{4,3,2,1,0:T(8,128)S(1)}, f32[16,16,128]{2,1,0:T(8,128)S(1)}) custom-call(f32[2,2,4,32,512]{4,3,2,1,0:T(8,128)S(1)} %get-tuple-element.13.z_ref, bf16[2,2,4,32,512]{4,3,2,1,0:T(8,128)(2,1)S(1)} %collective-permute-done.up_ref, bf16[2,2,4,32,512]{4,3,2,1,0:T(8,128)(2,1)S(1)} %collective-permute-done.1.down_ref, ...), custom_call_target="tpu_custom_call" | custom-call | tf_op jit(solution)/shard_map/pallas_call | solution.py:468
  91.2 13.2 %all_to_all.21.parts_ref = f32[16,16,128]{2,1,0:T(8,128)S(1)} all-to-all(f32[16,16,128]{2,1,0:T(8,128)S(1)} %get-tuple-element.20), channel_id=1, replica_groups=mesh['yh'=2,'g'=32,'h'=2,'f'=4] {'yh','h','f'}, dimensions={0} | all-to-all | bytes 262144 | tf_op jit(solution)/shard_map/all_to_all | solution.py:481
  104.4 0.0 copy-done.1
  104.4 2.0 %shard_map.77 = bf16[4,4,32,512]{3,2,1,0:T(8,128)(2,1)S(1)} custom-call(f32[2,3,8,32,512]{4,3,2,1,0:T(8,128)S(1)} %get-tuple-element.19.x_ref, f32[16,16,128]{2,1,0:T(8,128)S(1)} %all_to_all.21.parts_ref, s32[128]{0:T(128)S(1)} %copy-done.2, bf16[1,512,512]{2,1,0:T(8,128)(2,1)S(1)} %copy-done.1), custom_call_target="tpu_custom_call" | custom-call | tf_op jit(solution)/shard_map/pallas_call | solution.py:482
  106.4 20.7 %all_to_all.22.in_ref = bf16[4,4,32,512]{3,2,1,0:T(8,128)(2,1)S(1)} all-to-all(bf16[4,4,32,512]{3,2,1,0:T(8,128)(2,1)S(1)} %shard_map.77), channel_id=1, replica_groups=mesh['yh'=2,'g'=32,'h'=2,'f'=4] {'yh','h'}, dimensions={0} | all-to-all | bytes 1048576 | tf_op jit(solution)/shard_map/all_to_all | solution.py:488
  127.1 0.8 shard_map.78
Async XLA Ops:
  1.5 23.8 %copy-start = (bf16[2,512,512]{2,1,0:T(8,128)(2,1)S(1)}, bf16[2,512,512]{2,1,0:T(8,128)(2,1)}, u32[]{:S(2)}) copy-start(bf16[2,512,512]{2,1,0:T(8,128)(2,1)} %constant.4.clone.table_ref) | copy-start | bytes 3145732
  27.0 31.0 %collective-permute-start.2 = (bf16[2,2,4,32,512]{4,3,2,1,0:T(8,128)(2,1)S(1)}, bf16[2,2,4,32,512]{4,3,2,1,0:T(8,128)(2,1)S(1)}, u32[]{:S(2)}, u32[]{:S(2)}) collective-permute-start(bf16[2,2,4,32,512]{4,3,2,1,0:T(8,128)(2,1)S(1)} %get-tuple-element.14), channel_id=1, source_target_pairs={{0,248},{64,56},{128,120},{192,184},{56,64},{120,128},{184,192},{2... | collective-permute-start | bytes 1572872 | tf_op jit(solution)/shard_map/ppermute | solution.py:462
  27.7 32.0 %collective-permute-start.1 = (bf16[2,2,4,32,512]{4,3,2,1,0:T(8,128)(2,1)S(1)}, bf16[2,2,4,32,512]{4,3,2,1,0:T(8,128)(2,1)S(1)}, u32[]{:S(2)}, u32[]{:S(2)}) collective-permute-start(bf16[2,2,4,32,512]{4,3,2,1,0:T(8,128)(2,1)S(1)} %get-tuple-element.14), channel_id=1, source_target_pairs={{8,0},{16,8},{24,16},{32,24},{40,32},{48,40},{56,48},{72,64},{80,7... | collective-permute-start | bytes 1572872 | tf_op jit(solution)/shard_map/ppermute | solution.py:459
  50.7 12.9 %collective-permute-start = (bf16[2,2,4,32,512]{4,3,2,1,0:T(8,128)(2,1)S(1)}, bf16[2,2,4,32,512]{4,3,2,1,0:T(8,128)(2,1)S(1)}, u32[]{:S(2)}, u32[]{:S(2)}) collective-permute-start(bf16[2,2,4,32,512]{4,3,2,1,0:T(8,128)(2,1)S(1)} %get-tuple-element.14), channel_id=1, source_target_pairs={{0,8},{8,16},{16,24},{24,32},{32,40},{40,48},{48,56},{64,72},{72,8... | collective-permute-start | bytes 1572872 | tf_op jit(solution)/shard_map/ppermute | solution.py:460
  52.6 27.8 %collective-permute-start.4 = (bf16[2,144,512]{2,1,0:T(8,128)(2,1)S(1)}, bf16[2,144,512]{2,1,0:T(8,128)(2,1)}, u32[]{:S(2)}, u32[]{:S(2)}) collective-permute-start(bf16[2,144,512]{2,1,0:T(8,128)(2,1)S(1)} %get-tuple-element.15.b_even_ref), channel_id=1, source_target_pairs={{0,248},{8,0},{16,8},{24,16},{32,24},{40,32},{48,40},{56,48},{64,5... | collective-permute-start | bytes 884744 | tf_op jit(solution)/shard_map/ppermute | solution.py:463
  56.0 24.4 %collective-permute-start.3 = (bf16[2,144,512]{2,1,0:T(8,128)(2,1)S(1)}, bf16[2,144,512]{2,1,0:T(8,128)(2,1)}, u32[]{:S(2)}, u32[]{:S(2)}) collective-permute-start(bf16[2,144,512]{2,1,0:T(8,128)(2,1)S(1)} %get-tuple-element.16.b_odd_ref), channel_id=1, source_target_pairs={{0,8},{8,16},{16,24},{24,32},{32,40},{40,48},{48,56},{56,64},{64,7... | collective-permute-start | bytes 884744 | tf_op jit(solution)/shard_map/ppermute | solution.py:464
  63.6 22.1 %copy-start.2 = (s32[128]{0:T(128)S(1)}, s32[128]{0:T(128)}, u32[]{:S(2)}) copy-start(s32[128]{0:T(128)} %levels_ref.3) | copy-start | bytes 1540
  65.9 19.8 %all-to-all-start.1 = ((f32[16,16,128]{2,1,0:T(8,128)}), f32[16,16,128]{2,1,0:T(8,128)S(1)}, u32[]{:S(2)}, u32[]{:S(2)}) async-start(f32[16,16,128]{2,1,0:T(8,128)} %shard_map.75), calls=%async_computation.1 | async-start | bytes 262144 | tf_op jit(solution)/shard_map/all_to_all | solution.py:467
  85.7 18.6 %copy-start.1 = (bf16[1,512,512]{2,1,0:T(8,128)(2,1)S(1)}, bf16[1,512,512]{2,1,0:T(8,128)(2,1)}, u32[]{:S(2)}) copy-start(bf16[1,512,512]{2,1,0:T(8,128)(2,1)} %constant.5.clone.table_ref) | copy-start | bytes 1572868

commit v8 on v7

--- a/solution.py
+++ b/solution.py
@@ -29,11 +29,11 @@
 HBM = pl.BlockSpec(memory_space=pltpu.HBM)
 
 
-def receiver_tables(length, sign):
+def receiver_tables(length, sign, gain):
     k = np.arange(length)
     angle = 2.0 * np.pi / length * ((k[:, None] * k[None, :]) % length)
     c, s = np.cos(angle) / math.sqrt(length), sign * np.sin(angle) / math.sqrt(length)
-    full = np.block([[c, -s], [s, c]]).astype(np.float32)
+    full = (gain * np.block([[c, -s], [s, c]])).astype(np.float32)
     high = full.astype(jnp.bfloat16)
     low = (full - high.astype(np.float32)).astype(jnp.bfloat16)
     return np.stack([high, low])
@@ -143,6 +143,7 @@
 def shrink_windows(n, size, spectra_of, parts_ref, levels_ref, e_ref, wide):
     fl, q = e_ref.shape[3], e_ref.shape[4] // 2
     count = 5 if wide else 3
+    root = ROOT8 * RELAX if wide else ROOT8
     marks = seams(n)
     tile = parts_ref[0]
     for k in range(1, parts_ref.shape[0]):
@@ -152,7 +153,7 @@
     for ab in range(2):
         for w in range(count):
             window = (2 * (ab * n + lax.axis_index("g")) + w - count // 2 + 4 * n) & (4 * n - 1)
-            scale = LEVEL_SCALE / size * ROOT8 * levels_ref[window].astype(f32)
+            scale = LEVEL_SCALE / size * root * levels_ref[window].astype(f32)
             lams.append(jnp.broadcast_to(total[count * ab + w : count * ab + w + 1, :] * scale, (8, 128)))
 
     def body(i, carry):
@@ -165,7 +166,7 @@
                     kept = []
                     for re, im in x:
                         inverse = lax.rsqrt(jnp.maximum(re * re + im * im, TINY))
-                        factor = jnp.maximum(ROOT8 - lams[count * ab + w] * inverse, 0.0)
+                        factor = jnp.maximum(root - lams[count * ab + w] * inverse, 0.0)
                         kept.append((re * factor, im * factor))
                     y = dft8(kept, -1, "second" if w == 0 else "first" if w == count - 1 else "both")
                     if w > 0:
@@ -254,7 +255,7 @@
                 other = [jnp.where(slots[t] == j, new, old) for old, new in zip(other, others[j])]
             shifted = (other[0] * cos + other[1] * sin, other[1] * cos - other[0] * sin)
             for span, shift in zip(spans, shifted):
-                emit(t, span, RELAX * ((e_ref[ab, k, t, rows, span] + b_of(t, span)) - shift))
+                emit(t, span, (e_ref[ab, k, t, rows, span] + b_of(t, span)) - shift)
 
 
 def first_kernel(in_ref, table_ref, z_ref, meta_ref, phase_ref, zs_ref, b_even_ref, b_odd_ref, e_ref, bh_ref):
@@ -305,7 +306,7 @@
     lax.fori_loop(0, fl // 16, body, 0)
 
 
-def fetch_halo(n, up_ref, down_ref, cross_ref, halo_ref):
+def wide_sums_kernel(n, z_ref, cross_ref, up_ref, down_ref, out_ref, near_ref, halo_ref):
     g = lax.axis_index("g")
     row = n // 4
     for side, ref, at_edge, swapped in (
@@ -316,23 +317,23 @@
         @pl.when(jnp.logical_not(at_edge))
         def _(side=side, ref=ref):
             for ab in range(2):
+                near_ref[side, ab] = ref[ab]
                 halo_ref[side, ab] = ref[ab].astype(f32)
 
         @pl.when(at_edge)
         def _(side=side, swapped=swapped):
             for ab in range(2):
-                halo_ref[side, ab] = cross_ref[jnp.where(swapped, 1 - ab, ab)].astype(f32)
-
-
-def wide_sums_kernel(n, z_ref, cross_ref, up_ref, down_ref, out_ref, halo_ref):
-    fetch_halo(n, up_ref, down_ref, cross_ref, halo_ref)
+                block = cross_ref[jnp.where(swapped, 1 - ab, ab)]
+                near_ref[side, ab] = block
+                halo_ref[side, ab] = block.astype(f32)
+
     add_sums(n, z_ref, halo_ref, out_ref, True)
 
 
-def middle_kernel(n, size, z_ref, up_ref, down_ref, cross_ref, parts_ref, levels_ref, b_even_ref, b_odd_ref, meta_ref, phase_ref,
+def middle_kernel(n, size, z_ref, near_ref, parts_ref, levels_ref, b_even_ref, b_odd_ref, meta_ref, phase_ref,
                   b_up_ref, b_down_ref, x_out, parts_out, e_ref, far_meta_ref, far_ref, z2_ref, halo2_ref, halo_ref):
     fl, q = z_ref.shape[3], z_ref.shape[4] // 2
-    fetch_halo(n, up_ref, down_ref, cross_ref, halo_ref)
+    halo_ref[...] = near_ref[...].astype(f32)
     g = lax.axis_index("g")
     marks = seams(n)
 
@@ -425,7 +426,7 @@
     side = shape((2, SHOTS_DEV * fl + 16, 2 * q), bf16)
     size = 8 * nf * ROLES * fl * q
     parts_shape = shape((ROLES * nf, 16, 128), f32)
-    forward, backward = receiver_tables(q, 1.0), receiver_tables(q, -1.0)
+    forward, backward = receiver_tables(q, 1.0, RELAX), receiver_tables(q, -1.0, 1.0)
     before = [(i, (i - 1) % n) for i in range(n)]
     after = [(i, (i + 1) % n) for i in range(n)]
 
@@ -463,12 +464,14 @@
     b_down = lax.ppermute(b_even, "g", before)
     b_up = lax.ppermute(b_odd, "g", after)
     far = pltpu.VMEM((2, 2, 2, *block), f32)
-    parts = call(functools.partial(wide_sums_kernel, n), parts_shape, [VMEM] * 4, [far])(z, cross, up, down)
+    parts, near = call(
+        functools.partial(wide_sums_kernel, n), (parts_shape, shape((2, 2, 2, *block), bf16)), [VMEM] * 4, [far]
+    )(z, cross, up, down)
     parts = lax.all_to_all(parts, SUM_GROUP, 0, 0, tiled=True)
     x, parts = call(
         functools.partial(middle_kernel, n, size),
         (shape((2, 3, 8, fl, 2 * q), f32), parts_shape),
-        [VMEM] * 5 + [SMEM] + [VMEM] * 6,
+        [VMEM] * 3 + [SMEM] + [VMEM] * 6,
         [
             pltpu.VMEM((2, 4, *block), f32),
             pltpu.VMEM((ROLES, 16, 128), f32),
@@ -477,7 +480,7 @@
             pltpu.VMEM((2, 2, 1, *block), f32),
             far,
         ],
-    )(z, up, down, cross, parts, levels, b_even, b_odd, meta, phase, b_up, b_down)
+    )(z, near, parts, levels, b_even, b_odd, meta, phase, b_up, b_down)
     parts = lax.all_to_all(parts, SUM_GROUP, 0, 0, tiled=True)
     out = call(
         functools.partial(last_kernel, n, size),

time: 128 us -> 127 us (level)
  the two profiles are of different devices: /device:TPU:121 before, /device:TPU:56 now
where the time goes in v8:
time: 127 us
  blocking collectives  60.5 us (48%)
  starting transfers between devices  41 us (32%)
  Pallas kernels  13 us (10%)
  waiting for transfers between devices  12.2 us (10%)
    all_to_all x1, blocking collectives, on_device(): gathered = lax.all_to_all(packed, GROUP, 0, 0, tiled=True)  25 us
    all_to_all x1, blocking collectives, on_device(): out = lax.all_to_all(out, GROUP, 0, 0, tiled=True)  22.3 us
    ppermute x1, starting transfers between devices, on_device(): cross = lax.ppermute(zs, 'g', ends)  20.3 us
    all_to_all x1, blocking collectives, on_device(): parts = lax.all_to_all(parts, SUM_GROUP, 0, 0, tiled=True)  13.2 us
    all_to_all x1, starting transfers between devices, on_device(): parts = lax.all_to_all(parts, SUM_GROUP, 0, 0, tiled=True)  8.63 us
    ppermute x1, waiting for transfers between devices, on_device(): cross = lax.ppermute(zs, 'g', ends)  6.88 us
    all_to_all x1, waiting for transfers between devices, on_device(): parts = lax.all_to_all(parts, SUM_GROUP, 0, 0, tiled=True)  5.29 us
    ppermute x1, starting transfers between devices, on_device(): up = lax.ppermute(zs, 'g', [(i, j) for i, j in after if j % row > 0])  4.93 us
  transfers between devices with their start and end apart: 6, of which 2 were waited for; matrix products, arithmetic and copies ran while one was open for 0% of the time, Pallas kernels for 2%

profile of v8, /device:TPU:56, one launch (start us, length us, event | category | flops | bytes accessed | tf_op | source)
XLA Modules:
  0.0 126.8 jit_solution(8444499259084150828)
XLA Ops:
  0.0 1.5 %shard_map.73 = bf16[4,33,32,128]{3,2,1,0:T(8,128)(2,1)S(1)} custom-call(bf16[2,4,128,256]{3,2,1,0:T(8,128)(2,1)} %e_ref.1, bf16[2,4,128,256]{3,2,1,0:T(8,128)(2,1)} %b_ref.1, s32[4]{0:T(128)} %partner_ref.1, s32[512]{0:T(512)} %delays_ref.1), custom_call_target="tpu_custom_call" | custom-call | tf_op jit(solution)/shard_map/pallas_call | solution.py:434
  1.5 0.0 copy-start
  1.5 25.0 %all_to_all.20.in_ref = bf16[4,33,32,128]{3,2,1,0:T(8,128)(2,1)S(1)} all-to-all(bf16[4,33,32,128]{3,2,1,0:T(8,128)(2,1)S(1)} %shard_map.73), channel_id=1, replica_groups=mesh['yh'=2,'g'=32,'h'=2,'f'=4] {'yh','h'}, dimensions={0} | all-to-all | bytes 2162688 | tf_op jit(solution)/shard_map/all_to_all | solution.py:445
  26.6 0.0 copy-done
  26.6 1.6 %shard_map.74 = (f32[2,2,4,32,512]{4,3,2,1,0:T(8,128)S(1)}, f32[4,16,128]{2,1,0:T(8,128)S(1)}, f32[2,32,128]{2,1,0:T(8,128)S(1)}, bf16[2,2,4,32,512]{4,3,2,1,0:T...) custom-call(bf16[4,33,32,128]{3,2,1,0:T(8,128)(2,1)S(1)} %all_to_all.20.in_ref, ...), custom_call_target="tpu_custom_call" | custom-call | tf_op jit(solution)/shard_map/pallas_call | solution.py:446
  28.2 1.3 %collective-permute-start.2 = (bf16[2,2,4,32,512]{4,3,2,1,0:T(8,128)(2,1)S(1)}, bf16[2,2,4,32,512]{4,3,2,1,0:T(8,128)(2,1)S(1)}, u32[]{:S(2)}, u32[]{:S(2)}) collective-permute-start(bf16[2,2,4,32,512]{4,3,2,1,0:T(8,128)(2,1)S(1)} %get-tuple-element.16), channel_id=1, source_target_pairs={{8,0},{16,8},{24,16},{32,24},{40,32},{48,40},{56,48},{72,64},{80,7... | collective-permute-start | bytes 1572872 | tf_op jit(solution)/shard_map/ppermute | solution.py:460
  29.5 4.9 %collective-permute-start.1 = (bf16[2,2,4,32,512]{4,3,2,1,0:T(8,128)(2,1)S(1)}, bf16[2,2,4,32,512]{4,3,2,1,0:T(8,128)(2,1)S(1)}, u32[]{:S(2)}, u32[]{:S(2)}) collective-permute-start(bf16[2,2,4,32,512]{4,3,2,1,0:T(8,128)(2,1)S(1)} %get-tuple-element.16), channel_id=1, source_target_pairs={{0,8},{8,16},{16,24},{24,32},{32,40},{40,48},{48,56},{64,72},{72,8... | collective-permute-start | bytes 1572872 | tf_op jit(solution)/shard_map/ppermute | solution.py:461
  34.5 20.3 %collective-permute-start = (bf16[2,2,4,32,512]{4,3,2,1,0:T(8,128)(2,1)S(1)}, bf16[2,2,4,32,512]{4,3,2,1,0:T(8,128)(2,1)S(1)}, u32[]{:S(2)}, u32[]{:S(2)}) collective-permute-start(bf16[2,2,4,32,512]{4,3,2,1,0:T(8,128)(2,1)S(1)} %get-tuple-element.16), channel_id=1, source_target_pairs={{0,248},{64,56},{128,120},{192,184},{56,64},{120,128},{184,192},{2... | collective-permute-start | bytes 1572872 | tf_op jit(solution)/shard_map/ppermute | solution.py:463
  54.8 1.9 %collective-permute-start.4 = (bf16[2,144,512]{2,1,0:T(8,128)(2,1)S(1)}, bf16[2,144,512]{2,1,0:T(8,128)(2,1)S(1)}, u32[]{:S(2)}, u32[]{:S(2)}) collective-permute-start(bf16[2,144,512]{2,1,0:T(8,128)(2,1)S(1)} %get-tuple-element.19.b_even_ref), channel_id=1, source_target_pairs={{0,248},{8,0},{16,8},{24,16},{32,24},{40,32},{48,40},{56,48},{64,5... | collective-permute-start | bytes 884744 | tf_op jit(solution)/shard_map/ppermute | solution.py:464
  56.7 3.9 %collective-permute-start.3 = (bf16[2,144,512]{2,1,0:T(8,128)(2,1)S(1)}, bf16[2,144,512]{2,1,0:T(8,128)(2,1)S(1)}, u32[]{:S(2)}, u32[]{:S(2)}) collective-permute-start(bf16[2,144,512]{2,1,0:T(8,128)(2,1)S(1)} %get-tuple-element.20.b_odd_ref), channel_id=1, source_target_pairs={{0,8},{8,16},{16,24},{24,32},{32,40},{40,48},{48,56},{56,64},{64,7... | collective-permute-start | bytes 884744 | tf_op jit(solution)/shard_map/ppermute | solution.py:465
  60.6 0.0 collective-permute-done.2.down_ref
  60.6 0.0 collective-permute-done.1.up_ref
  60.6 6.9 %collective-permute-done.cross_ref = bf16[2,2,4,32,512]{4,3,2,1,0:T(8,128)(2,1)S(1)} collective-permute-done((bf16[2,2,4,32,512]{4,3,2,1,0:T(8,128)(2,1)S(1)}, bf16[2,2,4,32,512]{4,3,2,1,0:T(8,128)(2,1)S(1)}, u32[]{:S(2)}, u32[]{:S(2)}) %collective-permute-start) | collective-permute-done | bytes 524320 | tf_op jit(solution)/shard_map/ppermute | solution.py:463
  67.5 0.0 copy-start.2
  67.5 2.3 %shard_map.75 = (f32[16,16,128]{2,1,0:T(8,128)}, bf16[2,2,2,4,32,512]{5,4,3,2,1,0:T(8,128)(2,1)S(1)}) custom-call(f32[2,2,4,32,512]{4,3,2,1,0:T(8,128)S(1)} %get-tuple-element.15.z_ref, bf16[2,2,4,32,512]{4,3,2,1,0:T(8,128)(2,1)S(1)} %collective-permute-done.cross_ref, bf16[2,2,4,32,512]{4,3,2,1,0:T(8,128)(2,1)S(1)} %collective-permute-done.1.up_ref, ...), custom_call_target="tpu_custom_call" | custom-call | tf_op jit(solution)/shard_map/pallas_call | solution.py:467
  69.8 8.6 %all-to-all-start.1 = ((f32[16,16,128]{2,1,0:T(8,128)}), f32[16,16,128]{2,1,0:T(8,128)S(1)}, u32[]{:S(2)}, u32[]{:S(2)}) async-start(f32[16,16,128]{2,1,0:T(8,128)} %get-tuple-element.18), calls=%async_computation.1 | async-start | bytes 262144 | tf_op jit(solution)/shard_map/all_to_all | solution.py:470
  78.5 0.0 collective-permute-done.4.b_down_ref
  78.5 0.0 collective-permute-done.3.b_up_ref
  78.5 5.3 %all-to-all-done.1.parts_ref = f32[16,16,128]{2,1,0:T(8,128)S(1)} async-done(((f32[16,16,128]{2,1,0:T(8,128)}), f32[16,16,128]{2,1,0:T(8,128)S(1)}, u32[]{:S(2)}, u32[]{:S(2)}) %all-to-all-start.1) | async-done | bytes 131104 | tf_op jit(solution)/shard_map/all_to_all | solution.py:470
  83.8 0.0 copy-done.2
  83.8 0.0 copy-start.1
  83.8 4.7 %shard_map.76 = (f32[2,3,8,32,512]{4,3,2,1,0:T(8,128)S(1)}, f32[16,16,128]{2,1,0:T(8,128)S(1)}) custom-call(f32[2,2,4,32,512]{4,3,2,1,0:T(8,128)S(1)} %get-tuple-element.15.z_ref, bf16[2,2,2,4,32,512]{5,4,3,2,1,0:T(8,128)(2,1)S(1)} %get-tuple-element.17.near_ref, f32[16,16,128]{2,1,0:T(8,128)S(1)} %all-to-all-done.1.parts_ref, s32[128]{0:T(128)S(1)} %copy-done.2, ...), custom_call_target="tpu_custom_call" | custom-call | tf_op jit(solution)/shard_map/pallas_call | solution.py:471
  88.5 13.2 %all_to_all.21.parts_ref = f32[16,16,128]{2,1,0:T(8,128)S(1)} all-to-all(f32[16,16,128]{2,1,0:T(8,128)S(1)} %get-tuple-element.24), channel_id=1, replica_groups=mesh['yh'=2,'g'=32,'h'=2,'f'=4] {'yh','h','f'}, dimensions={0} | all-to-all | bytes 262144 | tf_op jit(solution)/shard_map/all_to_all | solution.py:484
  101.6 0.0 copy-done.1
  101.7 2.0 %shard_map.77 = bf16[4,4,32,512]{3,2,1,0:T(8,128)(2,1)S(1)} custom-call(f32[2,3,8,32,512]{4,3,2,1,0:T(8,128)S(1)} %get-tuple-element.23.x_ref, f32[16,16,128]{2,1,0:T(8,128)S(1)} %all_to_all.21.parts_ref, s32[128]{0:T(128)S(1)} %copy-done.2, bf16[1,512,512]{2,1,0:T(8,128)(2,1)S(1)} %copy-done.1), custom_call_target="tpu_custom_call" | custom-call | tf_op jit(solution)/shard_map/pallas_call | solution.py:485
  103.7 22.3 %all_to_all.22.in_ref = bf16[4,4,32,512]{3,2,1,0:T(8,128)(2,1)S(1)} all-to-all(bf16[4,4,32,512]{3,2,1,0:T(8,128)(2,1)S(1)} %shard_map.77), channel_id=1, replica_groups=mesh['yh'=2,'g'=32,'h'=2,'f'=4] {'yh','h'}, dimensions={0} | all-to-all | bytes 1048576 | tf_op jit(solution)/shard_map/all_to_all | solution.py:491
  126.0 0.8 shard_map.78
Async XLA Ops:
  1.5 25.1 %copy-start = (bf16[2,512,512]{2,1,0:T(8,128)(2,1)S(1)}, bf16[2,512,512]{2,1,0:T(8,128)(2,1)}, u32[]{:S(2)}) copy-start(bf16[2,512,512]{2,1,0:T(8,128)(2,1)} %constant.4.clone.table_ref) | copy-start | bytes 3145732
  28.2 32.4 %collective-permute-start.2 = (bf16[2,2,4,32,512]{4,3,2,1,0:T(8,128)(2,1)S(1)}, bf16[2,2,4,32,512]{4,3,2,1,0:T(8,128)(2,1)S(1)}, u32[]{:S(2)}, u32[]{:S(2)}) collective-permute-start(bf16[2,2,4,32,512]{4,3,2,1,0:T(8,128)(2,1)S(1)} %get-tuple-element.16), channel_id=1, source_target_pairs={{8,0},{16,8},{24,16},{32,24},{40,32},{48,40},{56,48},{72,64},{80,7... | collective-permute-start | bytes 1572872 | tf_op jit(solution)/shard_map/ppermute | solution.py:460
  29.5 31.1 %collective-permute-start.1 = (bf16[2,2,4,32,512]{4,3,2,1,0:T(8,128)(2,1)S(1)}, bf16[2,2,4,32,512]{4,3,2,1,0:T(8,128)(2,1)S(1)}, u32[]{:S(2)}, u32[]{:S(2)}) collective-permute-start(bf16[2,2,4,32,512]{4,3,2,1,0:T(8,128)(2,1)S(1)} %get-tuple-element.16), channel_id=1, source_target_pairs={{0,8},{8,16},{16,24},{24,32},{32,40},{40,48},{48,56},{64,72},{72,8... | collective-permute-start | bytes 1572872 | tf_op jit(solution)/shard_map/ppermute | solution.py:461
  34.5 33.1 %collective-permute-start = (bf16[2,2,4,32,512]{4,3,2,1,0:T(8,128)(2,1)S(1)}, bf16[2,2,4,32,512]{4,3,2,1,0:T(8,128)(2,1)S(1)}, u32[]{:S(2)}, u32[]{:S(2)}) collective-permute-start(bf16[2,2,4,32,512]{4,3,2,1,0:T(8,128)(2,1)S(1)} %get-tuple-element.16), channel_id=1, source_target_pairs={{0,248},{64,56},{128,120},{192,184},{56,64},{120,128},{184,192},{2... | collective-permute-start | bytes 1572872 | tf_op jit(solution)/shard_map/ppermute | solution.py:463
  54.8 23.7 %collective-permute-start.4 = (bf16[2,144,512]{2,1,0:T(8,128)(2,1)S(1)}, bf16[2,144,512]{2,1,0:T(8,128)(2,1)S(1)}, u32[]{:S(2)}, u32[]{:S(2)}) collective-permute-start(bf16[2,144,512]{2,1,0:T(8,128)(2,1)S(1)} %get-tuple-element.19.b_even_ref), channel_id=1, source_target_pairs={{0,248},{8,0},{16,8},{24,16},{32,24},{40,32},{48,40},{56,48},{64,5... | collective-permute-start | bytes 884744 | tf_op jit(solution)/shard_map/ppermute | solution.py:464
  56.7 21.8 %collective-permute-start.3 = (bf16[2,144,512]{2,1,0:T(8,128)(2,1)S(1)}, bf16[2,144,512]{2,1,0:T(8,128)(2,1)S(1)}, u32[]{:S(2)}, u32[]{:S(2)}) collective-permute-start(bf16[2,144,512]{2,1,0:T(8,128)(2,1)S(1)} %get-tuple-element.20.b_odd_ref), channel_id=1, source_target_pairs={{0,8},{8,16},{16,24},{24,32},{32,40},{40,48},{48,56},{56,64},{64,7... | collective-permute-start | bytes 884744 | tf_op jit(solution)/shard_map/ppermute | solution.py:465
  67.5 16.2 %copy-start.2 = (s32[128]{0:T(128)S(1)}, s32[128]{0:T(128)}, u32[]{:S(2)}) copy-start(s32[128]{0:T(128)} %levels_ref.3) | copy-start | bytes 1540
  69.8 13.9 %all-to-all-start.1 = ((f32[16,16,128]{2,1,0:T(8,128)}), f32[16,16,128]{2,1,0:T(8,128)S(1)}, u32[]{:S(2)}, u32[]{:S(2)}) async-start(f32[16,16,128]{2,1,0:T(8,128)} %get-tuple-element.18), calls=%async_computation.1 | async-start | bytes 262144 | tf_op jit(solution)/shard_map/all_to_all | solution.py:470
  83.8 17.9 %copy-start.1 = (bf16[1,512,512]{2,1,0:T(8,128)(2,1)S(1)}, bf16[1,512,512]{2,1,0:T(8,128)(2,1)}, u32[]{:S(2)}) copy-start(bf16[1,512,512]{2,1,0:T(8,128)(2,1)} %constant.5.clone.table_ref) | copy-start | bytes 1572868

commit v9 on v8

--- a/solution.py
+++ b/solution.py
@@ -132,8 +132,8 @@
         return tuple(totals)
 
     totals = lax.fori_loop(0, fl // 8, body, (jnp.zeros((8, 128), f32),) * (2 * count))
-    row = lax.broadcasted_iota(jnp.int32, (16, 128), 0)
-    tile = jnp.zeros((16, 128), f32)
+    row = lax.broadcasted_iota(jnp.int32, out_ref.shape[1:], 0)
+    tile = jnp.zeros(out_ref.shape[1:], f32)
     for k, total in enumerate(totals):
         tile = jnp.where(row == k, jnp.sum(total, axis=0, keepdims=True), tile)
     for k in range(out_ref.shape[0]):
@@ -470,7 +470,7 @@
     parts = lax.all_to_all(parts, SUM_GROUP, 0, 0, tiled=True)
     x, parts = call(
         functools.partial(middle_kernel, n, size),
-        (shape((2, 3, 8, fl, 2 * q), f32), parts_shape),
+        (shape((2, 3, 8, fl, 2 * q), f32), shape((ROLES * nf, 8, 128), f32)),
         [VMEM] * 3 + [SMEM] + [VMEM] * 6,
         [
             pltpu.VMEM((2, 4, *block), f32),

time: 127 us -> 127 us (level)
  no operation moved by 1% of the time
where the time goes in v9:
time: 127 us
  blocking collectives  60.2 us (47%)
  starting transfers between devices  41 us (32%)
  Pallas kernels  13 us (10%)
  waiting for transfers between devices  12.2 us (10%)
    all_to_all x1, blocking collectives, on_device(): gathered = lax.all_to_all(packed, GROUP, 0, 0, tiled=True)  25 us
    all_to_all x1, blocking collectives, on_device(): out = lax.all_to_all(out, GROUP, 0, 0, tiled=True)  22.5 us
    ppermute x1, starting transfers between devices, on_device(): cross = lax.ppermute(zs, 'g', ends)  20.3 us
    all_to_all x1, blocking collectives, on_device(): parts = lax.all_to_all(parts, SUM_GROUP, 0, 0, tiled=True)  12.7 us
    all_to_all x1, starting transfers between devices, on_device(): parts = lax.all_to_all(parts, SUM_GROUP, 0, 0, tiled=True)  8.63 us
    ppermute x1, waiting for transfers between devices, on_device(): cross = lax.ppermute(zs, 'g', ends)  6.88 us
    all_to_all x1, waiting for transfers between devices, on_device(): parts = lax.all_to_all(parts, SUM_GROUP, 0, 0, tiled=True)  5.29 us
    ppermute x1, starting transfers between devices, on_device(): up = lax.ppermute(zs, 'g', [(i, j) for i, j in after if j % row > 0])  4.93 us
  transfers between devices with their start and end apart: 6, of which 2 were waited for; matrix products, arithmetic and copies ran while one was open for 0% of the time, Pallas kernels for 2%

profile of v9, /device:TPU:56, one launch (start us, length us, event | category | flops | bytes accessed | tf_op | source)
XLA Modules:
  0.0 126.5 jit_solution(138538593394061603)
XLA Ops:
  0.0 1.5 %shard_map.73 = bf16[4,33,32,128]{3,2,1,0:T(8,128)(2,1)S(1)} custom-call(bf16[2,4,128,256]{3,2,1,0:T(8,128)(2,1)} %e_ref.1, bf16[2,4,128,256]{3,2,1,0:T(8,128)(2,1)} %b_ref.1, s32[4]{0:T(128)} %partner_ref.1, s32[512]{0:T(512)} %delays_ref.1), custom_call_target="tpu_custom_call" | custom-call | tf_op jit(solution)/shard_map/pallas_call | solution.py:434
  1.5 0.0 copy-start
  1.5 25.0 %all_to_all.20.in_ref = bf16[4,33,32,128]{3,2,1,0:T(8,128)(2,1)S(1)} all-to-all(bf16[4,33,32,128]{3,2,1,0:T(8,128)(2,1)S(1)} %shard_map.73), channel_id=1, replica_groups=mesh['yh'=2,'g'=32,'h'=2,'f'=4] {'yh','h'}, dimensions={0} | all-to-all | bytes 2162688 | tf_op jit(solution)/shard_map/all_to_all | solution.py:445
  26.6 0.0 copy-done
  26.6 1.6 %shard_map.74 = (f32[2,2,4,32,512]{4,3,2,1,0:T(8,128)S(1)}, f32[4,16,128]{2,1,0:T(8,128)S(1)}, f32[2,32,128]{2,1,0:T(8,128)S(1)}, bf16[2,2,4,32,512]{4,3,2,1,0:T...) custom-call(bf16[4,33,32,128]{3,2,1,0:T(8,128)(2,1)S(1)} %all_to_all.20.in_ref, ...), custom_call_target="tpu_custom_call" | custom-call | tf_op jit(solution)/shard_map/pallas_call | solution.py:446
  28.2 1.3 %collective-permute-start.2 = (bf16[2,2,4,32,512]{4,3,2,1,0:T(8,128)(2,1)S(1)}, bf16[2,2,4,32,512]{4,3,2,1,0:T(8,128)(2,1)S(1)}, u32[]{:S(2)}, u32[]{:S(2)}) collective-permute-start(bf16[2,2,4,32,512]{4,3,2,1,0:T(8,128)(2,1)S(1)} %get-tuple-element.16), channel_id=1, source_target_pairs={{8,0},{16,8},{24,16},{32,24},{40,32},{48,40},{56,48},{72,64},{80,7... | collective-permute-start | bytes 1572872 | tf_op jit(solution)/shard_map/ppermute | solution.py:460
  29.5 4.9 %collective-permute-start.1 = (bf16[2,2,4,32,512]{4,3,2,1,0:T(8,128)(2,1)S(1)}, bf16[2,2,4,32,512]{4,3,2,1,0:T(8,128)(2,1)S(1)}, u32[]{:S(2)}, u32[]{:S(2)}) collective-permute-start(bf16[2,2,4,32,512]{4,3,2,1,0:T(8,128)(2,1)S(1)} %get-tuple-element.16), channel_id=1, source_target_pairs={{0,8},{8,16},{16,24},{24,32},{32,40},{40,48},{48,56},{64,72},{72,8... | collective-permute-start | bytes 1572872 | tf_op jit(solution)/shard_map/ppermute | solution.py:461
  34.5 20.3 %collective-permute-start = (bf16[2,2,4,32,512]{4,3,2,1,0:T(8,128)(2,1)S(1)}, bf16[2,2,4,32,512]{4,3,2,1,0:T(8,128)(2,1)S(1)}, u32[]{:S(2)}, u32[]{:S(2)}) collective-permute-start(bf16[2,2,4,32,512]{4,3,2,1,0:T(8,128)(2,1)S(1)} %get-tuple-element.16), channel_id=1, source_target_pairs={{0,248},{64,56},{128,120},{192,184},{56,64},{120,128},{184,192},{2... | collective-permute-start | bytes 1572872 | tf_op jit(solution)/shard_map/ppermute | solution.py:463
  54.8 1.9 %collective-permute-start.4 = (bf16[2,144,512]{2,1,0:T(8,128)(2,1)S(1)}, bf16[2,144,512]{2,1,0:T(8,128)(2,1)S(1)}, u32[]{:S(2)}, u32[]{:S(2)}) collective-permute-start(bf16[2,144,512]{2,1,0:T(8,128)(2,1)S(1)} %get-tuple-element.19.b_even_ref), channel_id=1, source_target_pairs={{0,248},{8,0},{16,8},{24,16},{32,24},{40,32},{48,40},{56,48},{64,5... | collective-permute-start | bytes 884744 | tf_op jit(solution)/shard_map/ppermute | solution.py:464
  56.7 3.9 %collective-permute-start.3 = (bf16[2,144,512]{2,1,0:T(8,128)(2,1)S(1)}, bf16[2,144,512]{2,1,0:T(8,128)(2,1)S(1)}, u32[]{:S(2)}, u32[]{:S(2)}) collective-permute-start(bf16[2,144,512]{2,1,0:T(8,128)(2,1)S(1)} %get-tuple-element.20.b_odd_ref), channel_id=1, source_target_pairs={{0,8},{8,16},{16,24},{24,32},{32,40},{40,48},{48,56},{56,64},{64,7... | collective-permute-start | bytes 884744 | tf_op jit(solution)/shard_map/ppermute | solution.py:465
  60.6 0.0 collective-permute-done.2.down_ref
  60.6 0.0 collective-permute-done.1.up_ref
  60.6 6.9 %collective-permute-done.cross_ref = bf16[2,2,4,32,512]{4,3,2,1,0:T(8,128)(2,1)S(1)} collective-permute-done((bf16[2,2,4,32,512]{4,3,2,1,0:T(8,128)(2,1)S(1)}, bf16[2,2,4,32,512]{4,3,2,1,0:T(8,128)(2,1)S(1)}, u32[]{:S(2)}, u32[]{:S(2)}) %collective-permute-start) | collective-permute-done | bytes 524320 | tf_op jit(solution)/shard_map/ppermute | solution.py:463
  67.5 0.0 copy-start.2
  67.5 2.3 %shard_map.75 = (f32[16,16,128]{2,1,0:T(8,128)}, bf16[2,2,2,4,32,512]{5,4,3,2,1,0:T(8,128)(2,1)S(1)}) custom-call(f32[2,2,4,32,512]{4,3,2,1,0:T(8,128)S(1)} %get-tuple-element.15.z_ref, bf16[2,2,4,32,512]{4,3,2,1,0:T(8,128)(2,1)S(1)} %collective-permute-done.cross_ref, bf16[2,2,4,32,512]{4,3,2,1,0:T(8,128)(2,1)S(1)} %collective-permute-done.1.up_ref, ...), custom_call_target="tpu_custom_call" | custom-call | tf_op jit(solution)/shard_map/pallas_call | solution.py:467
  69.8 8.6 %all-to-all-start.1 = ((f32[16,16,128]{2,1,0:T(8,128)}), f32[16,16,128]{2,1,0:T(8,128)S(1)}, u32[]{:S(2)}, u32[]{:S(2)}) async-start(f32[16,16,128]{2,1,0:T(8,128)} %get-tuple-element.18), calls=%async_computation.1 | async-start | bytes 262144 | tf_op jit(solution)/shard_map/all_to_all | solution.py:470
  78.5 0.0 collective-permute-done.4.b_down_ref
  78.5 0.0 collective-permute-done.3.b_up_ref
  78.5 5.3 %all-to-all-done.1.parts_ref = f32[16,16,128]{2,1,0:T(8,128)S(1)} async-done(((f32[16,16,128]{2,1,0:T(8,128)}), f32[16,16,128]{2,1,0:T(8,128)S(1)}, u32[]{:S(2)}, u32[]{:S(2)}) %all-to-all-start.1) | async-done | bytes 131104 | tf_op jit(solution)/shard_map/all_to_all | solution.py:470
  83.8 0.0 copy-done.2
  83.8 0.0 copy-start.1
  83.8 4.7 %shard_map.76 = (f32[2,3,8,32,512]{4,3,2,1,0:T(8,128)S(1)}, f32[16,8,128]{2,1,0:T(8,128)S(1)}) custom-call(f32[2,2,4,32,512]{4,3,2,1,0:T(8,128)S(1)} %get-tuple-element.15.z_ref, bf16[2,2,2,4,32,512]{5,4,3,2,1,0:T(8,128)(2,1)S(1)} %get-tuple-element.17.near_ref, f32[16,16,128]{2,1,0:T(8,128)S(1)} %all-to-all-done.1.parts_ref, s32[128]{0:T(128)S(1)} %copy-done.2, ...), custom_call_target="tpu_custom_call" | custom-call | tf_op jit(solution)/shard_map/pallas_call | solution.py:471
  88.5 12.7 %all_to_all.21.parts_ref = f32[16,8,128]{2,1,0:T(8,128)S(1)} all-to-all(f32[16,8,128]{2,1,0:T(8,128)S(1)} %get-tuple-element.24), channel_id=1, replica_groups=mesh['yh'=2,'g'=32,'h'=2,'f'=4] {'yh','h','f'}, dimensions={0} | all-to-all | bytes 131072 | tf_op jit(solution)/shard_map/all_to_all | solution.py:484
  101.1 0.0 copy-done.1
  101.1 2.0 %shard_map.77 = bf16[4,4,32,512]{3,2,1,0:T(8,128)(2,1)S(1)} custom-call(f32[2,3,8,32,512]{4,3,2,1,0:T(8,128)S(1)} %get-tuple-element.23.x_ref, f32[16,8,128]{2,1,0:T(8,128)S(1)} %all_to_all.21.parts_ref, s32[128]{0:T(128)S(1)} %copy-done.2, bf16[1,512,512]{2,1,0:T(8,128)(2,1)S(1)} %copy-done.1), custom_call_target="tpu_custom_call" | custom-call | tf_op jit(solution)/shard_map/pallas_call | solution.py:485
  103.2 22.5 %all_to_all.22.in_ref = bf16[4,4,32,512]{3,2,1,0:T(8,128)(2,1)S(1)} all-to-all(bf16[4,4,32,512]{3,2,1,0:T(8,128)(2,1)S(1)} %shard_map.77), channel_id=1, replica_groups=mesh['yh'=2,'g'=32,'h'=2,'f'=4] {'yh','h'}, dimensions={0} | all-to-all | bytes 1048576 | tf_op jit(solution)/shard_map/all_to_all | solution.py:491
  125.7 0.8 shard_map.78
Async XLA Ops:
  1.5 25.1 %copy-start = (bf16[2,512,512]{2,1,0:T(8,128)(2,1)S(1)}, bf16[2,512,512]{2,1,0:T(8,128)(2,1)}, u32[]{:S(2)}) copy-start(bf16[2,512,512]{2,1,0:T(8,128)(2,1)} %constant.4.clone.table_ref) | copy-start | bytes 3145732
  28.2 32.4 %collective-permute-start.2 = (bf16[2,2,4,32,512]{4,3,2,1,0:T(8,128)(2,1)S(1)}, bf16[2,2,4,32,512]{4,3,2,1,0:T(8,128)(2,1)S(1)}, u32[]{:S(2)}, u32[]{:S(2)}) collective-permute-start(bf16[2,2,4,32,512]{4,3,2,1,0:T(8,128)(2,1)S(1)} %get-tuple-element.16), channel_id=1, source_target_pairs={{8,0},{16,8},{24,16},{32,24},{40,32},{48,40},{56,48},{72,64},{80,7... | collective-permute-start | bytes 1572872 | tf_op jit(solution)/shard_map/ppermute | solution.py:460
  29.5 31.1 %collective-permute-start.1 = (bf16[2,2,4,32,512]{4,3,2,1,0:T(8,128)(2,1)S(1)}, bf16[2,2,4,32,512]{4,3,2,1,0:T(8,128)(2,1)S(1)}, u32[]{:S(2)}, u32[]{:S(2)}) collective-permute-start(bf16[2,2,4,32,512]{4,3,2,1,0:T(8,128)(2,1)S(1)} %get-tuple-element.16), channel_id=1, source_target_pairs={{0,8},{8,16},{16,24},{24,32},{32,40},{40,48},{48,56},{64,72},{72,8... | collective-permute-start | bytes 1572872 | tf_op jit(solution)/shard_map/ppermute | solution.py:461
  34.5 33.1 %collective-permute-start = (bf16[2,2,4,32,512]{4,3,2,1,0:T(8,128)(2,1)S(1)}, bf16[2,2,4,32,512]{4,3,2,1,0:T(8,128)(2,1)S(1)}, u32[]{:S(2)}, u32[]{:S(2)}) collective-permute-start(bf16[2,2,4,32,512]{4,3,2,1,0:T(8,128)(2,1)S(1)} %get-tuple-element.16), channel_id=1, source_target_pairs={{0,248},{64,56},{128,120},{192,184},{56,64},{120,128},{184,192},{2... | collective-permute-start | bytes 1572872 | tf_op jit(solution)/shard_map/ppermute | solution.py:463
  54.8 23.7 %collective-permute-start.4 = (bf16[2,144,512]{2,1,0:T(8,128)(2,1)S(1)}, bf16[2,144,512]{2,1,0:T(8,128)(2,1)S(1)}, u32[]{:S(2)}, u32[]{:S(2)}) collective-permute-start(bf16[2,144,512]{2,1,0:T(8,128)(2,1)S(1)} %get-tuple-element.19.b_even_ref), channel_id=1, source_target_pairs={{0,248},{8,0},{16,8},{24,16},{32,24},{40,32},{48,40},{56,48},{64,5... | collective-permute-start | bytes 884744 | tf_op jit(solution)/shard_map/ppermute | solution.py:464
  56.7 21.8 %collective-permute-start.3 = (bf16[2,144,512]{2,1,0:T(8,128)(2,1)S(1)}, bf16[2,144,512]{2,1,0:T(8,128)(2,1)S(1)}, u32[]{:S(2)}, u32[]{:S(2)}) collective-permute-start(bf16[2,144,512]{2,1,0:T(8,128)(2,1)S(1)} %get-tuple-element.20.b_odd_ref), channel_id=1, source_target_pairs={{0,8},{8,16},{16,24},{24,32},{32,40},{40,48},{48,56},{56,64},{64,7... | collective-permute-start | bytes 884744 | tf_op jit(solution)/shard_map/ppermute | solution.py:465
  67.5 16.2 %copy-start.2 = (s32[128]{0:T(128)S(1)}, s32[128]{0:T(128)}, u32[]{:S(2)}) copy-start(s32[128]{0:T(128)} %levels_ref.3) | copy-start | bytes 1540
  69.8 13.9 %all-to-all-start.1 = ((f32[16,16,128]{2,1,0:T(8,128)}), f32[16,16,128]{2,1,0:T(8,128)S(1)}, u32[]{:S(2)}, u32[]{:S(2)}) async-start(f32[16,16,128]{2,1,0:T(8,128)} %get-tuple-element.18), calls=%async_computation.1 | async-start | bytes 262144 | tf_op jit(solution)/shard_map/all_to_all | solution.py:470
  83.8 17.4 %copy-start.1 = (bf16[1,512,512]{2,1,0:T(8,128)(2,1)S(1)}, bf16[1,512,512]{2,1,0:T(8,128)(2,1)}, u32[]{:S(2)}) copy-start(bf16[1,512,512]{2,1,0:T(8,128)(2,1)} %constant.5.clone.table_ref) | copy-start | bytes 1572868
